TPU v7x, 128 devices: a whole 4x4x4 slice. The times are simulated.
128 devices in a mesh: ctx: 8 (over y, core), exp: 16 (over x, z).
Axes of the slice: x: 4, y: 4, z: 4, core: 2. Of those that a mesh axis runs over, the one named last changes fastest.
Arguments:
- mixer_input: bfloat16 [1024, 2, 8192], P('ctx', None, 'exp'), may hold values from -6 to 6
- gate_in: bfloat16 [1024, 2, 8192], P('ctx', None, 'exp'), may hold values from -6 to 6
- step_size: float32 [1024, 2, 8192], P('ctx', None, 'exp'), may hold values from 0.004 to 10
- decay_rate: float32 [16, 8192], P(None, 'exp'), may hold values from 0.03 to 2.5
- state_in: float32 [1024, 2, 16], P('ctx'), may hold values from -6 to 6
- state_out: float32 [1024, 2, 16], P('ctx'), may hold values from -6 to 6
- skip: float32 [8192], P('exp'), may hold values from 0.5 to 1.5
- out_proj: bfloat16 [8192, 4096], P('exp', 'ctx'), may hold values from -0.0625 to 0.0625
- hidden_in: bfloat16 [1024, 2, 4096], P('ctx', None, 'exp'), may hold values from -14 to 14
- norm_gain: float32 [4096], replicated, may hold values from 0.4 to 2.5
- w_gate: bfloat16 [16, 4096, 7168], P('exp', None, 'ctx'), may hold values from -0.09375 to 0.09375
- w_up: bfloat16 [16, 4096, 7168], P('exp', None, 'ctx'), may hold values from -0.09375 to 0.09375
- w_down: bfloat16 [16, 7168, 4096], P('exp', 'ctx'), may hold values from -0.0625 to 0.0625
- route_ids: int32 [1024, 2, 2], P('ctx'), may hold values from 0 to 15, all different within a row; in each aligned block of 256 rows (0 to 255, 256 to 511, ..., all dimensions but the last counted through in order) at most 64 rows name the same one
- route_weight: float32 [1024, 2, 2], P('ctx'), may hold values from 0.1 to 0.9
Outputs:
- layer_out: bfloat16 [1024, 2, 4096], P('ctx', None, 'exp')
Inputs may be any that keep to these rules, and one draw needn't show every extreme that they name: `route_ids`: the 2 experts of a token differ; within the rows of one index of ctx no expert is named by more than 64 rows.
All inputs are finite; a program needn't handle non-finite values.
Results may differ from a plain program's by a relative error of at most 0.009.
Values may be sent and summed in bfloat16 or wider, within the bound.
No kernel may reach another device: no remote copies, remote signals or barrier semaphores. Data moves between devices by JAX's collectives and lax.ppermute only.
A program may use at most 192 MiB of HBM per device.

v0:
```python
import functools

import jax
import jax.numpy as jnp
from jax import lax
from jax.experimental import pallas as pl
from jax.experimental.pallas import tpu as pltpu
from jax.sharding import PartitionSpec as P

epsilon = 1e-06
LOG2E = 1.4426950408889634
SUBS = 8
LANES = 128
MIB = 1 << 20
f32, bf16 = jnp.float32, jnp.bfloat16


def params(mib):
    return pltpu.CompilerParams(vmem_limit_bytes=mib * MIB)


def vmem():
    return pl.BlockSpec(memory_space=pltpu.VMEM)


def smem():
    return pl.BlockSpec(memory_space=pltpu.SMEM)


def anywhere():
    return pl.BlockSpec(memory_space=pl.ANY)


def spread(table_ref, out_ref):
    turns, _, columns = table_ref.shape

    def turn(t, _):
        row = table_ref[t]
        for i in range(columns):
            out_ref[t, i] = jnp.broadcast_to(row[:, i : i + 1], (SUBS, LANES))
        return 0

    lax.fori_loop(0, turns, turn, 0)


def split_lanes(step_ref, sig_ref, st4, v4):
    for q in range(st4.shape[0]):
        lanes = slice(q * LANES, (q + 1) * LANES)
        st = step_ref[:, lanes]
        st4[q] = st
        v4[q] = st * sig_ref[:, lanes].astype(f32)


def first_pass(step_ref, sig_ref, into_ref, rate_ref, fin_ref, before_ref, pre_ref, st4, v4, into_b):
    states, channels = rate_ref.shape
    prompts = fin_ref.shape[0]
    turns = into_ref.shape[0]
    hop = turns * prompts
    spread(into_ref, into_b)
    split_lanes(step_ref, sig_ref, st4, v4)
    sub = lax.broadcasted_iota(jnp.int32, (SUBS, LANES), 0)
    for q in range(channels // LANES):
        lanes = slice(q * LANES, (q + 1) * LANES)
        rates = [
            jnp.broadcast_to(rate_ref[n : n + 1, lanes] * -LOG2E, (SUBS, LANES)) for n in range(states)
        ]
        for b in range(prompts):

            def turn(t, held, q=q, b=b, rates=rates):
                total, hs = held
                st = st4[q, pl.ds(t * prompts + b, SUBS, stride=hop), :]
                v = v4[q, pl.ds(t * prompts + b, SUBS, stride=hop), :]
                new = []
                for n in range(states):
                    new.append(jnp.exp2(st * rates[n]) * hs[n] + v * into_b[t, b * states + n])
                return total + st, tuple(new)

            zero = jnp.zeros((SUBS, LANES), f32)
            width, hs = lax.fori_loop(0, turns, turn, (zero, (zero,) * states))
            hs = list(hs)
            for d in (1, 2, 4):
                live = sub >= d
                for n in range(states):
                    moved = jnp.where(live, pltpu.roll(hs[n], d, 0), 0.0)
                    hs[n] = hs[n] + jnp.exp2(rates[n] * width) * moved
                width = width + jnp.where(live, pltpu.roll(width, d, 0), 0.0)
            for n in range(states):
                fin_ref[b, n : n + 1, lanes] = hs[n][SUBS - 1 :]
                before_ref[b, n, :, lanes] = jnp.where(sub >= 1, pltpu.roll(hs[n], 1, 0), 0.0)
            fin_ref[b, states : states + 1, lanes] = width[SUBS - 1 :]
            pre_ref[b, :, lanes] = jnp.where(sub >= 1, pltpu.roll(width, 1, 0), 0.0)


def second_pass(
    mine_ref, step_ref, sig_ref, gate_ref, into_ref, outof_ref, rate_ref, skip_ref, before_ref, pre_ref,
    ends_ref, proj_hbm, out_ref, st4, v4, y4, into_b, outof_b, enter, mixed, proj, sem,
):
    states, channels = rate_ref.shape
    prompts = pre_ref.shape[0]
    turns = into_ref.shape[0]
    hop = turns * prompts
    fetch = pltpu.make_async_copy(proj_hbm, proj, sem)
    fetch.start()
    spread(into_ref, into_b)
    spread(outof_ref, outof_b)
    split_lanes(step_ref, sig_ref, st4, v4)
    mine = mine_ref[0]
    for q in range(channels // LANES):
        lanes = slice(q * LANES, (q + 1) * LANES)
        rate_q = rate_ref[:, lanes] * -LOG2E
        rates = [jnp.broadcast_to(rate_q[n : n + 1], (SUBS, LANES)) for n in range(states)]
        for b in range(prompts):
            h0 = jnp.zeros((states, LANES), f32)
            for c in range(ends_ref.shape[0] - 1):
                live = jnp.where(c < mine, 1.0, 0.0).astype(f32)
                decay = jnp.exp2(rate_q * (ends_ref[c, b, states : states + 1, lanes] * live))
                h0 = decay * h0 + ends_ref[c, b, :states, lanes] * live
            enter[...] = h0
            pre = pre_ref[b, :, lanes]
            hs = tuple(
                before_ref[b, n, :, lanes]
                + jnp.exp2(rates[n] * pre) * jnp.broadcast_to(enter[n : n + 1], (SUBS, LANES))
                for n in range(states)
            )

            def turn(t, hs, q=q, b=b, rates=rates):
                rows = pl.ds(t * prompts + b, SUBS, stride=hop)
                st = st4[q, rows, :]
                v = v4[q, rows, :]
                new, sums = [], [None] * 4
                for n in range(states):
                    h = jnp.exp2(st * rates[n]) * hs[n] + v * into_b[t, b * states + n]
                    new.append(h)
                    term = h * outof_b[t, b * states + n]
                    sums[n % 4] = term if sums[n % 4] is None else sums[n % 4] + term
                y4[q, rows, :] = (sums[0] + sums[1]) + (sums[2] + sums[3])
                return tuple(new)

            lax.fori_loop(0, turns, turn, hs)
        sig = sig_ref[:, lanes].astype(f32)
        gate = gate_ref[:, lanes].astype(f32)
        y = y4[q] + skip_ref[:, lanes] * sig
        mixed[:, lanes] = (y * (gate / (1.0 + jnp.exp(-gate)))).astype(bf16)
    fetch.wait()
    width = out_ref.shape[2]
    blocks, _, columns = proj.shape
    for c in range(blocks):
        part = jnp.dot(mixed[...], proj[c], preferred_element_type=f32).astype(bf16)
        for i in range(columns // width):
            out_ref[c * (columns // width) + i] = part[:, i * width : (i + 1) * width]


def dispatch(recv_ref, hidden_ref, ids_ref, res_ref, slots_ref, pick):
    experts, slots, width = slots_ref.shape
    tokens = hidden_ref.shape[0]
    total = hidden_ref[...].astype(f32)
    for i in range(recv_ref.shape[0]):
        total = total + recv_ref[i].astype(f32)
    res_ref[...] = total
    expert = lax.broadcasted_iota(jnp.int32, (experts, tokens), 0)
    chosen = jnp.zeros((experts, tokens), f32)
    for k in range(ids_ref.shape[0]):
        chosen = jnp.where(ids_ref[k : k + 1, :] == expert, 1.0, chosen)
    row = lax.broadcasted_iota(jnp.int32, (tokens, tokens), 0)
    col = lax.broadcasted_iota(jnp.int32, (tokens, tokens), 1)
    earlier = jnp.where(row < col, 1.0, 0.0).astype(bf16)
    place = jnp.dot(chosen.astype(bf16), earlier, preferred_element_type=f32)
    place = jnp.where(chosen > 0.5, place, -1.0)
    slot = lax.broadcasted_iota(jnp.int32, (slots, tokens), 0).astype(f32)
    for e in range(experts):
        pick[e * slots : (e + 1) * slots] = jnp.where(place[e : e + 1] == slot, 1.0, 0.0).astype(bf16)
    rows = jnp.dot(pick[...], total.astype(bf16), preferred_element_type=f32).astype(bf16)
    slots_ref[...] = rows.reshape(experts, slots, width)


def normalize(recv_ref, gain_ref, out_ref):
    blocks, slots, width = recv_ref.shape
    square = jnp.zeros((slots, width), f32)
    for i in range(blocks):
        part = recv_ref[i].astype(f32)
        square = square + part * part
    mean = jnp.sum(square, axis=1, keepdims=True) / (blocks * width)
    scale = lax.rsqrt(mean + epsilon)
    for i in range(blocks):
        lanes = slice(i * width, (i + 1) * width)
        out_ref[:, lanes] = (recv_ref[i].astype(f32) * scale * gain_ref[:, lanes]).astype(bf16)


def feed_forward(x_ref, gate_hbm, up_hbm, down_hbm, out_ref, gates, ups, downs, act, gate_sem, up_sem, down_sem):
    pieces, _, wide = gates.shape
    blocks, _, width = downs.shape
    slabs, _, slots, _ = out_ref.shape

    def gate_copy(i):
        return pltpu.make_async_copy(gate_hbm.at[:, pl.ds(i * wide, wide)], gates.at[i], gate_sem.at[i])

    def up_copy(i):
        return pltpu.make_async_copy(up_hbm.at[:, pl.ds(i * wide, wide)], ups.at[i], up_sem.at[i])

    def down_copy(i):
        return pltpu.make_async_copy(down_hbm.at[:, pl.ds(i * width, width)], downs.at[i], down_sem.at[i])

    for i in range(pieces):
        gate_copy(i).start()
        up_copy(i).start()
    for i in range(blocks):
        down_copy(i).start()
    for i in range(pieces):
        gate_copy(i).wait()
        up_copy(i).wait()
        both = jnp.concatenate([gates[i], ups[i]], axis=1)
        part = jnp.dot(x_ref[...], both, preferred_element_type=f32)
        g, u = part[:, :wide], part[:, wide:]
        act[:, i * wide : (i + 1) * wide] = (g / (1.0 + jnp.exp(-g)) * u).astype(bf16)
    for i in range(blocks):
        down_copy(i).wait()

    @pl.loop(0, blocks)
    def _(i):
        part = jnp.dot(act[...], downs[i], preferred_element_type=f32).astype(bf16)
        for s in range(slabs):
            out_ref[s, i] = part[s * slots : (s + 1) * slots]


def combine(recv_ref, ids_ref, weight_ref, res_ref, out_ref):
    experts, slots, width = recv_ref.shape
    tokens, top = ids_ref.shape
    rows = recv_ref[...].reshape(experts * slots, width)
    expert = lax.broadcasted_iota(jnp.int32, (tokens, experts), 1)
    named = [ids_ref[:, k : k + 1] == expert for k in range(top)]
    chosen = jnp.zeros((tokens, experts), f32)
    for k in range(top):
        chosen = jnp.where(named[k], 1.0, chosen)
    row = lax.broadcasted_iota(jnp.int32, (tokens, tokens), 0)
    col = lax.broadcasted_iota(jnp.int32, (tokens, tokens), 1)
    earlier = jnp.where(col < row, 1.0, 0.0).astype(bf16)
    place = jnp.dot(earlier, chosen.astype(bf16), preferred_element_type=f32)
    place = place + (expert * slots).astype(f32)
    slot = lax.broadcasted_iota(jnp.int32, (tokens, experts * slots), 1)
    total = res_ref[...]
    for k in range(top):
        at = jnp.sum(jnp.where(named[k], place, 0.0), axis=1, keepdims=True).astype(jnp.int32)
        pick = jnp.where(slot == at, 1.0, 0.0).astype(bf16)
        total = total + weight_ref[:, k : k + 1] * jnp.dot(pick, rows, preferred_element_type=f32)
    out_ref[...] = total.astype(out_ref.dtype)


def scan_tables(table, turns):
    return table.reshape(SUBS, turns, -1).transpose(1, 0, 2)


def run_first(step, sig, into, rate, prompts):
    tokens, channels = step.shape
    states = rate.shape[0]
    turns = into.shape[0]
    tiles = channels // LANES
    return pl.pallas_call(
        first_pass,
        out_shape=(
            jax.ShapeDtypeStruct((prompts, states + 1, channels), f32),
            jax.ShapeDtypeStruct((prompts, states, SUBS, channels), f32),
            jax.ShapeDtypeStruct((prompts, SUBS, channels), f32),
        ),
        in_specs=[vmem()] * 4,
        out_specs=(vmem(),) * 3,
        scratch_shapes=[
            pltpu.VMEM((tiles, tokens, LANES), f32),
            pltpu.VMEM((tiles, tokens, LANES), f32),
            pltpu.VMEM((turns, prompts * states, SUBS, LANES), f32),
        ],
        compiler_params=params(24),
        name="scan_first",
    )(step, sig, into, rate)


def run_second(mine, step, sig, gate, into, outof, rate, skip, before, pre, ends, proj, share):
    tokens, channels = step.shape
    prompts, states = before.shape[:2]
    turns = into.shape[0]
    tiles = channels // LANES
    return pl.pallas_call(
        second_pass,
        out_shape=jax.ShapeDtypeStruct((proj.shape[0] * proj.shape[2] // share, tokens, share), bf16),
        in_specs=[smem()] + [vmem()] * 10 + [anywhere()],
        out_specs=vmem(),
        scratch_shapes=[
            pltpu.VMEM((tiles, tokens, LANES), f32),
            pltpu.VMEM((tiles, tokens, LANES), f32),
            pltpu.VMEM((tiles, tokens, LANES), f32),
            pltpu.VMEM((turns, prompts * states, SUBS, LANES), f32),
            pltpu.VMEM((turns, prompts * states, SUBS, LANES), f32),
            pltpu.VMEM((states, LANES), f32),
            pltpu.VMEM((tokens, channels), bf16),
            pltpu.VMEM(proj.shape, bf16),
            pltpu.SemaphoreType.DMA,
        ],
        compiler_params=params(32),
        name="scan_second",
    )(mine, step, sig, gate, into, outof, rate, skip, before, pre, ends, proj)


def run_dispatch(recv, hidden, ids, experts, slots):
    tokens, share = hidden.shape
    return pl.pallas_call(
        dispatch,
        out_shape=(
            jax.ShapeDtypeStruct((tokens, share), f32),
            jax.ShapeDtypeStruct((experts, slots, share), bf16),
        ),
        in_specs=[vmem()] * 3,
        out_specs=(vmem(),) * 2,
        scratch_shapes=[pltpu.VMEM((experts * slots, tokens), bf16)],
        compiler_params=params(16),
        name="dispatch",
    )(recv, hidden, ids)


def run_normalize(recv, gain):
    blocks, slots, width = recv.shape
    return pl.pallas_call(
        normalize,
        out_shape=jax.ShapeDtypeStruct((slots, blocks * width), bf16),
        in_specs=[vmem()] * 2,
        out_specs=vmem(),
        compiler_params=params(8),
        name="normalize",
    )(recv, gain)


def run_ffn(x, w_gate, w_up, w_down, slabs, share):
    rows, depth = x.shape
    hidden = w_gate.shape[1]
    wide = LANES
    pieces, blocks = hidden // wide, w_down.shape[1] // share
    return pl.pallas_call(
        feed_forward,
        out_shape=jax.ShapeDtypeStruct((slabs, blocks, rows // slabs, share), bf16),
        in_specs=[vmem()] + [anywhere()] * 3,
        out_specs=vmem(),
        scratch_shapes=[
            pltpu.VMEM((pieces, depth, wide), bf16),
            pltpu.VMEM((pieces, depth, wide), bf16),
            pltpu.VMEM((blocks, hidden, share), bf16),
            pltpu.VMEM((rows, hidden), bf16),
            pltpu.SemaphoreType.DMA((pieces,)),
            pltpu.SemaphoreType.DMA((pieces,)),
            pltpu.SemaphoreType.DMA((blocks,)),
        ],
        compiler_params=params(48),
        name="feed_forward",
    )(x, w_gate, w_up, w_down)


def run_combine(recv, ids, weights, res):
    return pl.pallas_call(
        combine,
        out_shape=jax.ShapeDtypeStruct(res.shape, bf16),
        in_specs=[vmem()] * 4,
        out_specs=vmem(),
        compiler_params=params(16),
        name="combine",
    )(recv, ids, weights, res)


def on_device(
    mixer_input, gate_in, step_size, decay_rate, state_in, state_out, skip, out_proj, hidden_in, norm_gain,
    w_gate, w_up, w_down, route_ids, route_weight,
):
    slab_len, prompts, channels = mixer_input.shape
    tokens = slab_len * prompts
    share = hidden_in.shape[2]
    slabs = lax.axis_size("ctx")
    experts = lax.axis_size("exp") * w_gate.shape[0]
    slots = 4 * tokens // experts
    turns = slab_len // SUBS
    proj = lax.all_gather(out_proj, "ctx")
    sig = mixer_input.reshape(tokens, channels)
    step = step_size.reshape(tokens, channels)
    into = scan_tables(state_in, turns)
    outof = scan_tables(state_out, turns)
    end, before, pre = run_first(step, sig, into, decay_rate, prompts)
    ends = lax.all_gather(end, "ctx")
    mine = lax.axis_index("ctx").astype(jnp.int32).reshape(1)
    gate = gate_in.reshape(tokens, channels)
    partial_value = run_second(
        mine, step, sig, gate, into, outof, decay_rate, skip.reshape(1, channels), before, pre, ends, proj, share
    )
    recv = lax.all_to_all(partial_value, "exp", 0, 0, tiled=True)
    ids = route_ids.reshape(tokens, -1)
    residual, slot_rows = run_dispatch(recv, hidden_in.reshape(tokens, share), ids.T, experts, slots)
    whole = lax.all_to_all(slot_rows, "exp", 0, 0, tiled=True)
    normed = run_normalize(whole, norm_gain.reshape(1, -1))
    segment = lax.all_gather(normed, "ctx", axis=0, tiled=True)
    part = run_ffn(segment, w_gate[0], w_up[0], w_down[0], slabs, share)
    returned = lax.psum_scatter(part, "ctx", scatter_dimension=0, tiled=True)[0]
    back = lax.all_to_all(returned, "exp", 0, 0, tiled=True)
    out = run_combine(back, ids, route_weight.reshape(tokens, -1), residual)
    return out.reshape(slab_len, prompts, share)


def solution(mesh):
    placed = (
        P("ctx", None, "exp"),
        P("ctx", None, "exp"),
        P("ctx", None, "exp"),
        P(None, "exp"),
        P("ctx", None, None),
        P("ctx", None, None),
        P("exp"),
        P("exp", "ctx"),
        P("ctx", None, "exp"),
        P(),
        P("exp", None, "ctx"),
        P("exp", None, "ctx"),
        P("exp", "ctx", None),
        P("ctx", None, None),
        P("ctx", None, None),
    )
    return jax.shard_map(
        on_device, mesh=mesh, in_specs=placed, out_specs=P("ctx", None, "exp"), check_vma=False
    )
```

profile of v0, /device:TPU:0, one launch (start us, length us, event | category | flops | bytes accessed | tf_op | source)
XLA Modules:
  0.0 236.6 jit_solution(11309709470883802758)
XLA Ops:
  6.5 0.7 all-gather.7.cloned.1.call-update
  7.3 1.4 reshape.37.step_ref
  8.7 1.1 reshape.38.sig_ref
  9.7 0.8 reshape.40
  10.7 1.1 reshape.39.gate_ref
  11.7 0.8 reshape.41
  12.7 0.7 copy-done.2
  13.4 6.1 %scan_first.1 = (f32[2,17,512]{2,1,0:T(8,128)S(1)}, f32[2,16,8,512]{3,2,1,0:T(8,128)S(1)}, f32[2,8,512]{2,1,0:T(8,128)S(1)}) custom-call(f32[256,512]{1,0:T(8,128)S(1)} %reshape.37.step_ref, bf16[256,512]{1,0:T(8,128)(2,1)S(1)} %reshape.38.sig_ref, f32[16,8,32]{2,1,0:T(8,128)S(1)} %bitcast.23, f32[16,512]{1,0:T(8,128)S(1)} %copy-done.2), custom_call_target="tpu_custom_call" | custom-call | tf_op jit(solution)/shard_map/scan_first/pallas_call | solution.py:257
  19.6 15.4 %all-gather = f32[16,17,512]{2,1,0:T(8,128)S(1)} all-gather(f32[2,17,512]{2,1,0:T(8,128)S(1)} %get-tuple-element.12), channel_id=2, replica_groups=mesh['ctx'=8,'exp'=16] {'ctx'}, dimensions={0}, use_global_device_ids=true | all-gather | bytes 626688 | tf_op jit(solution)/shard_map/all_gather | solution.py:382
  34.9 11.4 %all-gather.7.cloned.1.call-done = bf16[4096,512]{1,0:T(8,128)(2,1)} async-done(((bf16[512,512]{1,0:T(8,128)(2,1)}), bf16[4096,512]{1,0:T(8,128)(2,1)}) %all-gather.7.cloned.1.call-update) | async-done | bytes 4194320 | tf_op jit(solution)/shard_map/all_gather | solution.py:376
  46.4 2.2 copy-done.1
  48.5 11.6 %scan_second.1 = bf16[16,256,256]{2,1,0:T(8,128)(2,1)} custom-call(s32[1]{0:T(128)} %bitcast.mine_ref, f32[256,512]{1,0:T(8,128)S(1)} %reshape.37.step_ref, bf16[256,512]{1,0:T(8,128)(2,1)S(1)} %reshape.38.sig_ref, bf16[256,512]{1,0:T(8,128)(2,1)S(1)} %reshape.39.gate_ref, f32[16,8,32]{2,1,0:T(8,128)S(1)} %bitcast.24, f32[16,8,32]{2,1,0:T(8,128)S(1)} %bitcast.26, ...), custom_call_target="tpu_custom_call" | custom-call | tf_op jit(solution)/shard_map/scan_second/pallas_call | solution.py:281
  60.2 7.6 %all-to-all-start = ((bf16[16,256,256]{2,1,0:T(8,128)(2,1)}), bf16[16,256,256]{2,1,0:T(8,128)(2,1)S(1)}, u32[]{:S(2)}, u32[]{:S(2)}) async-start(bf16[16,256,256]{2,1,0:T(8,128)(2,1)} %scan_second.1), calls=%async_computation | async-start | bytes 4194304 | tf_op jit(solution)/shard_map/all_to_all | solution.py:388
  68.2 30.6 %all-to-all-done.recv_ref = bf16[16,256,256]{2,1,0:T(8,128)(2,1)S(1)} async-done(((bf16[16,256,256]{2,1,0:T(8,128)(2,1)}), bf16[16,256,256]{2,1,0:T(8,128)(2,1)S(1)}, u32[]{:S(2)}, u32[]{:S(2)}) %all-to-all-start) | async-done | bytes 2097184 | tf_op jit(solution)/shard_map/all_to_all | solution.py:388
  99.3 15.0 %all_to_all.15.recv_ref = bf16[16,64,256]{2,1,0:T(8,128)(2,1)S(1)} all-to-all(bf16[16,64,256]{2,1,0:T(8,128)(2,1)S(1)} %get-tuple-element.13), channel_id=1, replica_groups=mesh['ctx'=8,'exp'=16] {'exp'}, dimensions={0} | all-to-all | bytes 1048576 | tf_op jit(solution)/shard_map/all_to_all | solution.py:391
  114.3 1.0 normalize.1
  115.6 28.4 %all-gather.5.cloned.1.call-done.x_ref = bf16[512,4096]{1,0:T(8,128)(2,1)} async-done(((bf16[64,4096]{1,0:T(8,128)(2,1)}), bf16[512,4096]{1,0:T(8,128)(2,1)}) %all-gather.5.cloned.1.call-update) | async-done | bytes 4194320 | tf_op jit(solution)/shard_map/all_gather | solution.py:393
  144.0 27.6 %feed_forward.1 = bf16[8,16,64,256]{3,2,1,0:T(8,128)(2,1)S(1)} custom-call(bf16[512,4096]{1,0:T(8,128)(2,1)} %all-gather.5.cloned.1.call-done.x_ref, bf16[4096,896]{1,0:T(8,128)(2,1)} %bitcast.29, bf16[4096,896]{1,0:T(8,128)(2,1)} %bitcast.30, bf16[896,4096]{1,0:T(8,128)(2,1)} %bitcast.31), custom_call_target="tpu_custom_call" | custom-call | tf_op jit(solution)/shard_map/feed_forward/pallas_call | solution.py:335
  171.7 1.9 copy-done
  173.7 38.1 %reduce-scatter.2.cloned.1.call-done = bf16[1,16,64,256]{3,2,1,0:T(8,128)(2,1)} async-done(((bf16[8,16,64,256]{3,2,1,0:T(8,128)(2,1)}), bf16[1,16,64,256]{3,2,1,0:T(8,128)(2,1)}) %reduce-scatter.2.cloned.1.call-update) | async-done | bytes 524304 | tf_op jit(solution)/shard_map/reduce_scatter | solution.py:395
  211.8 6.7 %all-to-all-start.2 = ((bf16[16,64,256]{2,1,0:T(8,128)(2,1)}), bf16[16,64,256]{2,1,0:T(8,128)(2,1)S(1)}, u32[]{:S(2)}, u32[]{:S(2)}) async-start(bf16[16,64,256]{2,1,0:T(8,128)(2,1)} %bitcast.32), calls=%async_computation.3 | async-start | bytes 1048576 | tf_op jit(solution)/shard_map/all_to_all | solution.py:396
  218.7 9.9 %all-to-all-done.2.recv_ref = bf16[16,64,256]{2,1,0:T(8,128)(2,1)S(1)} async-done(((bf16[16,64,256]{2,1,0:T(8,128)(2,1)}), bf16[16,64,256]{2,1,0:T(8,128)(2,1)S(1)}, u32[]{:S(2)}, u32[]{:S(2)}) %all-to-all-start.2) | async-done | bytes 524320 | tf_op jit(solution)/shard_map/all_to_all | solution.py:396
  228.6 0.8 combine.1
  229.4 0.7 reshape.47
  (27 shorter events, 1.6 us)
Async XLA Ops:
  6.5 39.8 %copy-start.3 = (f32[16,512]{1,0:T(8,128)S(1)}, f32[16,512]{1,0:T(8,128)}, u32[]{:S(2)}) copy-start(f32[16,512]{1,0:T(8,128)} %rate_ref.3) | copy-start | bytes 98308
  6.5 39.8 %copy-start.5 = (f32[512]{0:T(512)S(1)}, f32[512]{0:T(512)}, u32[]{:S(2)}) copy-start(f32[512]{0:T(512)} %param.21) | copy-start | bytes 6148
  6.5 39.8 %all-gather.7.cloned.1.call-start = ((), (), s32[]{:S(2)}) async-start(), calls=%async_computation.6 | async-start | bytes 4718592 | tf_op jit(solution)/shard_map/all_gather | solution.py:376
  12.7 0.8 copy-start.2
  46.4 2.2 copy-start.1
  60.2 7.7 %copy-start.7 = (s32[128,2,2]{0,2,1:T(2,128)S(1)}, s32[128,2,2]{0,2,1:T(2,128)}, u32[]{:S(2)}) copy-start(s32[128,2,2]{0,2,1:T(2,128)} %param.28) | copy-start | bytes 6148
  60.2 7.9 %copy-start.6 = (bf16[128,2,256]{2,1,0:T(2,128)(2,1)S(1)}, bf16[128,2,256]{2,1,0:T(2,128)(2,1)}, u32[]{:S(2)}) copy-start(bf16[128,2,256]{2,1,0:T(2,128)(2,1)} %param.23) | copy-start | bytes 393220
  60.2 54.2 %copy-start.4 = (f32[4096]{0:T(1024)S(1)}, f32[4096]{0:T(1024)}, u32[]{:S(2)}) copy-start(f32[4096]{0:T(1024)} %param.24) | copy-start | bytes 49156
  60.2 38.5 %all-to-all-start = ((bf16[16,256,256]{2,1,0:T(8,128)(2,1)}), bf16[16,256,256]{2,1,0:T(8,128)(2,1)S(1)}, u32[]{:S(2)}, u32[]{:S(2)}) async-start(bf16[16,256,256]{2,1,0:T(8,128)(2,1)} %scan_second.1), calls=%async_computation | async-start | bytes 4194304 | tf_op jit(solution)/shard_map/all_to_all | solution.py:388
  67.8 76.2 %all-gather.5.cloned.1.call-start = ((), (), s32[]{:S(2)}) async-start(), calls=%async_computation.4 | async-start | bytes 4718592 | tf_op jit(solution)/shard_map/all_gather | solution.py:393
  115.4 96.4 %reduce-scatter.2.cloned.1.call-start = ((), (), s32[]{:S(2)}) async-start(), calls=%async_computation.5 | async-start | bytes 4718592 | tf_op jit(solution)/shard_map/reduce_scatter | solution.py:395
  171.7 1.9 copy-start
  173.6 44.9 %copy-start.8 = (f32[128,2,2]{0,2,1:T(2,128)S(1)}, f32[128,2,2]{0,2,1:T(2,128)}, u32[]{:S(2)}) copy-start(f32[128,2,2]{0,2,1:T(2,128)} %param.29) | copy-start | bytes 6148
  211.8 16.9 %all-to-all-start.2 = ((bf16[16,64,256]{2,1,0:T(8,128)(2,1)}), bf16[16,64,256]{2,1,0:T(8,128)(2,1)S(1)}, u32[]{:S(2)}, u32[]{:S(2)}) async-start(bf16[16,64,256]{2,1,0:T(8,128)(2,1)} %bitcast.32), calls=%async_computation.3 | async-start | bytes 1048576 | tf_op jit(solution)/shard_map/all_to_all | solution.py:396
Sparse Core Ops, SparseCore 0:
  9.1 37.2 all-gather.6
  115.5 28.4 all-gather.4
  173.8 37.9 reduce-scatter.1
where the time goes:
time: 237 us
  waiting for transfers between devices  119 us (50%)
  Pallas kernels  47.8 us (20%)
  blocking collectives  30.4 us (13%)
  starting transfers between devices  14.6 us (6%)
  between operations  13.3 us (6%)
  local copies, waits for them, and re-layouts  11.4 us (5%)
    reduce_scatter x1, waiting for transfers between devices, on_device(): returned = lax.psum_scatter(part, 'ctx', scatter_dimension=0, tiled=True)[0]  38.1 us
    all_to_all x1, waiting for transfers between devices, on_device(): recv = lax.all_to_all(partial_value, 'exp', 0, 0, tiled=True)  30.6 us
    all_gather x1, waiting for transfers between devices, on_device(): segment = lax.all_gather(normed, 'ctx', axis=0, tiled=True)  28.4 us
    pallas_call x1, Pallas kernels, run_ffn(): pl.pallas_call(feed_forward, out_shape=jax.ShapeDtypeStruct((slabs, block...  27.6 us
    all_gather x1, blocking collectives, on_device(): ends = lax.all_gather(end, 'ctx')  15.4 us
    all_to_all x1, blocking collectives, on_device(): whole = lax.all_to_all(slot_rows, 'exp', 0, 0, tiled=True)  15 us
    pallas_call x1, Pallas kernels, run_second(): pl.pallas_call(second_pass, out_shape=jax.ShapeDtypeStruct((proj.shape[0]...  11.6 us
    all_gather x1, waiting for transfers between devices, on_device(): proj = lax.all_gather(out_proj, 'ctx')  11.4 us
  transfers between devices with their start and end apart: 5, of which 5 were waited for; matrix products, arithmetic and copies ran while one was open for 2% of the time, Pallas kernels for 3%

commit v1 on v0

--- a/solution.py
+++ b/solution.py
@@ -5,6 +5,7 @@
 from jax import lax
 from jax.experimental import pallas as pl
 from jax.experimental.pallas import tpu as pltpu
+from jax.sharding import Mesh
 from jax.sharding import PartitionSpec as P
 
 epsilon = 1e-06
@@ -91,31 +92,42 @@
             pre_ref[b, :, lanes] = jnp.where(sub >= 1, pltpu.roll(width, 1, 0), 0.0)
 
 
+def pair_up(core_ref, own_ref, sib_ref, rate_ref, out_ref):
+    states = rate_ref.shape[0]
+    low = core_ref[0] == 0
+    rate = rate_ref[...] * -LOG2E
+    for b in range(own_ref.shape[0]):
+        first = jnp.where(low, own_ref[b], sib_ref[b])
+        second = jnp.where(low, sib_ref[b], own_ref[b])
+        decay = jnp.exp2(rate * second[states:])
+        out_ref[b, :states] = decay * first[:states] + second[:states]
+        out_ref[b, states:] = first[states:] + second[states:]
+
+
 def second_pass(
-    mine_ref, step_ref, sig_ref, gate_ref, into_ref, outof_ref, rate_ref, skip_ref, before_ref, pre_ref,
-    ends_ref, proj_hbm, out_ref, st4, v4, y4, into_b, outof_b, enter, mixed, proj, sem,
+    core_ref, step_ref, sig_ref, gate_ref, into_ref, outof_ref, rate_ref, skip_ref, before_ref, pre_ref,
+    *rest, earlier,
 ):
+    sib_ref, *pair_refs = rest[: earlier + 1]
+    mixed_ref, st4, v4, y4, into_b, outof_b, enter = rest[earlier + 1 :]
     states, channels = rate_ref.shape
     prompts = pre_ref.shape[0]
     turns = into_ref.shape[0]
     hop = turns * prompts
-    fetch = pltpu.make_async_copy(proj_hbm, proj, sem)
-    fetch.start()
     spread(into_ref, into_b)
     spread(outof_ref, outof_b)
     split_lanes(step_ref, sig_ref, st4, v4)
-    mine = mine_ref[0]
+    live = jnp.where(core_ref[0] > 0, 1.0, 0.0).astype(f32)
     for q in range(channels // LANES):
         lanes = slice(q * LANES, (q + 1) * LANES)
         rate_q = rate_ref[:, lanes] * -LOG2E
         rates = [jnp.broadcast_to(rate_q[n : n + 1], (SUBS, LANES)) for n in range(states)]
         for b in range(prompts):
             h0 = jnp.zeros((states, LANES), f32)
-            for c in range(ends_ref.shape[0] - 1):
-                live = jnp.where(c < mine, 1.0, 0.0).astype(f32)
-                decay = jnp.exp2(rate_q * (ends_ref[c, b, states : states + 1, lanes] * live))
-                h0 = decay * h0 + ends_ref[c, b, :states, lanes] * live
-            enter[...] = h0
+            for pair in pair_refs:
+                h0 = jnp.exp2(rate_q * pair[b, states : states + 1, lanes]) * h0 + pair[b, :states, lanes]
+            decay = jnp.exp2(rate_q * (sib_ref[b, states : states + 1, lanes] * live))
+            enter[...] = decay * h0 + sib_ref[b, :states, lanes] * live
             pre = pre_ref[b, :, lanes]
             hs = tuple(
                 before_ref[b, n, :, lanes]
@@ -140,12 +152,17 @@
         sig = sig_ref[:, lanes].astype(f32)
         gate = gate_ref[:, lanes].astype(f32)
         y = y4[q] + skip_ref[:, lanes] * sig
-        mixed[:, lanes] = (y * (gate / (1.0 + jnp.exp(-gate)))).astype(bf16)
-    fetch.wait()
+        mixed_ref[:, lanes] = (y * (gate / (1.0 + jnp.exp(-gate)))).astype(bf16)
+
+
+def project(mixed_ref, proj_hbm, out_ref, proj, sem):
     width = out_ref.shape[2]
     blocks, _, columns = proj.shape
     for c in range(blocks):
-        part = jnp.dot(mixed[...], proj[c], preferred_element_type=f32).astype(bf16)
+        pltpu.make_async_copy(proj_hbm.at[c], proj.at[c], sem.at[c]).start()
+    for c in range(blocks):
+        pltpu.make_async_copy(proj_hbm.at[c], proj.at[c], sem.at[c]).wait()
+        part = jnp.dot(mixed_ref[...], proj[c], preferred_element_type=f32).astype(bf16)
         for i in range(columns // width):
             out_ref[c * (columns // width) + i] = part[:, i * width : (i + 1) * width]
 
@@ -186,40 +203,50 @@
         out_ref[:, lanes] = (recv_ref[i].astype(f32) * scale * gain_ref[:, lanes]).astype(bf16)
 
 
-def feed_forward(x_ref, gate_hbm, up_hbm, down_hbm, out_ref, gates, ups, downs, act, gate_sem, up_sem, down_sem):
-    pieces, _, wide = gates.shape
-    blocks, _, width = downs.shape
-    slabs, _, slots, _ = out_ref.shape
-
-    def gate_copy(i):
-        return pltpu.make_async_copy(gate_hbm.at[:, pl.ds(i * wide, wide)], gates.at[i], gate_sem.at[i])
-
-    def up_copy(i):
-        return pltpu.make_async_copy(up_hbm.at[:, pl.ds(i * wide, wide)], ups.at[i], up_sem.at[i])
-
-    def down_copy(i):
-        return pltpu.make_async_copy(down_hbm.at[:, pl.ds(i * width, width)], downs.at[i], down_sem.at[i])
-
-    for i in range(pieces):
-        gate_copy(i).start()
-        up_copy(i).start()
+def load_weights(after_ref, *refs):
+    count = (len(refs) - 2) // 2
+    sources, targets, turn_out, sem = refs[:count], refs[count : 2 * count], refs[-2], refs[-1]
+    copies = [pltpu.make_async_copy(s, t, sem.at[i]) for i, (s, t) in enumerate(zip(sources, targets))]
+    for c in copies:
+        c.start()
+    turn_out[...] = after_ref[: turn_out.shape[0], : turn_out.shape[1]].astype(f32) * 0.0
+    for c in copies:
+        c.wait()
+
+
+def feed_forward(*refs, groups):
+    count = sum(sum(g) for g in groups)
+    pieces, (w_gate, w_up, w_down, turn_ref) = refs[:count], refs[count : count + 4]
+    *outs, turn_out, x, act = refs[count + 4 :]
+    at = 0
+    for p in pieces:
+        x[at : at + p.shape[0]] = p[...]
+        at += p.shape[0]
+    blocks, rows, width = outs[0].shape
+    wide = 2 * LANES
+    hidden = w_gate.shape[1]
+    for i in range(0, hidden, wide):
+        size = min(wide, hidden - i)
+        lanes = slice(i, i + size)
+        both = jnp.concatenate([w_gate[:, lanes], w_up[:, lanes]], axis=1)
+        part = jnp.dot(x[...], both, preferred_element_type=f32)
+        g, u = part[:, :size], part[:, size:]
+        act[:, lanes] = (g / (1.0 + jnp.exp(-g)) * u).astype(bf16)
     for i in range(blocks):
-        down_copy(i).start()
-    for i in range(pieces):
-        gate_copy(i).wait()
-        up_copy(i).wait()
-        both = jnp.concatenate([gates[i], ups[i]], axis=1)
-        part = jnp.dot(x_ref[...], both, preferred_element_type=f32)
-        g, u = part[:, :wide], part[:, wide:]
-        act[:, i * wide : (i + 1) * wide] = (g / (1.0 + jnp.exp(-g)) * u).astype(bf16)
-    for i in range(blocks):
-        down_copy(i).wait()
-
-    @pl.loop(0, blocks)
-    def _(i):
-        part = jnp.dot(act[...], downs[i], preferred_element_type=f32).astype(bf16)
-        for s in range(slabs):
-            out_ref[s, i] = part[s * slots : (s + 1) * slots]
+        part = jnp.dot(act[...], w_down[:, i * width : (i + 1) * width], preferred_element_type=f32)
+        part = part.astype(bf16)
+        for j, out in enumerate(outs):
+            out[i] = part[j * rows : (j + 1) * rows]
+    turn_out[...] = turn_ref[...]
+
+
+def add_up(*refs):
+    *parts, out_ref = refs
+    for i in range(out_ref.shape[0]):
+        total = parts[0][i].astype(f32)
+        for p in parts[1:]:
+            total = total + p[i].astype(f32)
+        out_ref[i] = total.astype(bf16)
 
 
 def combine(recv_ref, ids_ref, weight_ref, res_ref, out_ref):
@@ -273,15 +300,26 @@
     )(step, sig, into, rate)
 
 
-def run_second(mine, step, sig, gate, into, outof, rate, skip, before, pre, ends, proj, share):
+def run_pair(core, own, sib, rate):
+    return pl.pallas_call(
+        pair_up,
+        out_shape=jax.ShapeDtypeStruct(own.shape, f32),
+        in_specs=[smem()] + [vmem()] * 3,
+        out_specs=vmem(),
+        compiler_params=params(8),
+        name="pair_up",
+    )(core, own, sib, rate)
+
+
+def run_second(core, step, sig, gate, into, outof, rate, skip, before, pre, sib, pairs):
     tokens, channels = step.shape
     prompts, states = before.shape[:2]
     turns = into.shape[0]
     tiles = channels // LANES
     return pl.pallas_call(
-        second_pass,
-        out_shape=jax.ShapeDtypeStruct((proj.shape[0] * proj.shape[2] // share, tokens, share), bf16),
-        in_specs=[smem()] + [vmem()] * 10 + [anywhere()],
+        functools.partial(second_pass, earlier=len(pairs)),
+        out_shape=jax.ShapeDtypeStruct((tokens, channels), bf16),
+        in_specs=[smem()] + [vmem()] * (10 + len(pairs)),
         out_specs=vmem(),
         scratch_shapes=[
             pltpu.VMEM((tiles, tokens, LANES), f32),
@@ -290,13 +328,24 @@
             pltpu.VMEM((turns, prompts * states, SUBS, LANES), f32),
             pltpu.VMEM((turns, prompts * states, SUBS, LANES), f32),
             pltpu.VMEM((states, LANES), f32),
-            pltpu.VMEM((tokens, channels), bf16),
-            pltpu.VMEM(proj.shape, bf16),
-            pltpu.SemaphoreType.DMA,
         ],
-        compiler_params=params(32),
+        compiler_params=params(16),
+        cost_estimate=pl.CostEstimate(flops=2 * 10**9, bytes_accessed=2 * MIB, transcendentals=0),
         name="scan_second",
-    )(mine, step, sig, gate, into, outof, rate, skip, before, pre, ends, proj)
+    )(core, step, sig, gate, into, outof, rate, skip, before, pre, sib, *pairs)
+
+
+def run_project(mixed, proj, share):
+    tokens = mixed.shape[0]
+    return pl.pallas_call(
+        project,
+        out_shape=jax.ShapeDtypeStruct((proj.shape[0] * proj.shape[2] // share, tokens, share), bf16),
+        in_specs=[vmem(), anywhere()],
+        out_specs=vmem(),
+        scratch_shapes=[pltpu.VMEM(proj.shape, bf16), pltpu.SemaphoreType.DMA((proj.shape[0],))],
+        compiler_params=params(16),
+        name="project",
+    )(mixed, proj)
 
 
 def run_dispatch(recv, hidden, ids, experts, slots):
@@ -327,28 +376,49 @@
     )(recv, gain)
 
 
-def run_ffn(x, w_gate, w_up, w_down, slabs, share):
-    rows, depth = x.shape
-    hidden = w_gate.shape[1]
-    wide = LANES
-    pieces, blocks = hidden // wide, w_down.shape[1] // share
-    return pl.pallas_call(
-        feed_forward,
-        out_shape=jax.ShapeDtypeStruct((slabs, blocks, rows // slabs, share), bf16),
-        in_specs=[vmem()] + [anywhere()] * 3,
+def run_load(after, *weights):
+    return pl.pallas_call(
+        load_weights,
+        out_shape=[pltpu.VMEM(w.shape, w.dtype) for w in weights] + [jax.ShapeDtypeStruct((8, LANES), f32)],
+        in_specs=[vmem()] + [pl.BlockSpec(memory_space=pltpu.HBM)] * len(weights),
+        out_specs=[vmem()] * (len(weights) + 1),
+        scratch_shapes=[pltpu.SemaphoreType.DMA((len(weights),))],
+        compiler_params=params(8),
+        cost_estimate=pl.CostEstimate(flops=0, bytes_accessed=2 * sum(w.nbytes for w in weights), transcendentals=0),
+        name="load_weights",
+    )(after, *[pltpu.with_memory_space_constraint(w, pltpu.HBM) for w in weights])
+
+
+def run_ffn(groups, weights, turn, share):
+    pieces = [p for own, other in groups for p in (*own, *other)]
+    rows = sum(p.shape[0] for p in groups[0][0])
+    depth, hidden = weights[0].shape
+    total = 2 * rows * len(groups)
+    part = jax.ShapeDtypeStruct((depth // share, rows, share), bf16)
+    weights = [pltpu.with_memory_space_constraint(w, pltpu.VMEM) for w in weights]
+    return pl.pallas_call(
+        functools.partial(feed_forward, groups=tuple((len(own), len(other)) for own, other in groups)),
+        out_shape=(part,) * (2 * len(groups)) + (jax.ShapeDtypeStruct(turn.shape, turn.dtype),),
+        in_specs=[vmem()] * (len(pieces) + 4),
+        out_specs=(vmem(),) * (2 * len(groups) + 1),
+        scratch_shapes=[pltpu.VMEM((total, depth), bf16), pltpu.VMEM((total, hidden), bf16)],
+        compiler_params=params(12),
+        cost_estimate=pl.CostEstimate(
+            flops=6 * total * depth * hidden, bytes_accessed=4 * total * depth, transcendentals=0
+        ),
+        name="feed_forward",
+    )(*pieces, *weights, turn)
+
+
+def run_add(*parts):
+    return pl.pallas_call(
+        add_up,
+        out_shape=jax.ShapeDtypeStruct(parts[0].shape, bf16),
+        in_specs=[vmem()] * len(parts),
         out_specs=vmem(),
-        scratch_shapes=[
-            pltpu.VMEM((pieces, depth, wide), bf16),
-            pltpu.VMEM((pieces, depth, wide), bf16),
-            pltpu.VMEM((blocks, hidden, share), bf16),
-            pltpu.VMEM((rows, hidden), bf16),
-            pltpu.SemaphoreType.DMA((pieces,)),
-            pltpu.SemaphoreType.DMA((pieces,)),
-            pltpu.SemaphoreType.DMA((blocks,)),
-        ],
-        compiler_params=params(48),
-        name="feed_forward",
-    )(x, w_gate, w_up, w_down)
+        compiler_params=params(8),
+        name="add_up",
+    )(*parts)
 
 
 def run_combine(recv, ids, weights, res):
@@ -369,53 +439,87 @@
     slab_len, prompts, channels = mixer_input.shape
     tokens = slab_len * prompts
     share = hidden_in.shape[2]
-    slabs = lax.axis_size("ctx")
-    experts = lax.axis_size("exp") * w_gate.shape[0]
+    chips = lax.axis_size("y")
+    exp = ("x", "z")
+    experts = lax.axis_size(exp) * w_gate.shape[0]
     slots = 4 * tokens // experts
     turns = slab_len // SUBS
-    proj = lax.all_gather(out_proj, "ctx")
+
+    def swap(value):
+        return lax.ppermute(value, "core", [(0, 1), (1, 0)])
+
+    def ring(value, d):
+        return lax.ppermute(value, "y", [(i, (i + d) % chips) for i in range(chips)])
+
+    proj = lax.all_gather(out_proj, ("y", "core"))
     sig = mixer_input.reshape(tokens, channels)
     step = step_size.reshape(tokens, channels)
     into = scan_tables(state_in, turns)
+    end, before, pre = run_first(step, sig, into, decay_rate, prompts)
+    core = lax.axis_index("core").astype(jnp.int32).reshape(1)
+    sib = swap(end)
+    pair = run_pair(core, end, sib, decay_rate)
+    pairs = [
+        lax.ppermute(pair, "y", [(i, i + d) for i in range(chips - d)]) for d in range(chips - 1, 0, -1)
+    ]
+    gate = gate_in.reshape(tokens, channels)
     outof = scan_tables(state_out, turns)
-    end, before, pre = run_first(step, sig, into, decay_rate, prompts)
-    ends = lax.all_gather(end, "ctx")
-    mine = lax.axis_index("ctx").astype(jnp.int32).reshape(1)
-    gate = gate_in.reshape(tokens, channels)
-    partial_value = run_second(
-        mine, step, sig, gate, into, outof, decay_rate, skip.reshape(1, channels), before, pre, ends, proj, share
+    mixed = run_second(
+        core, step, sig, gate, into, outof, decay_rate, skip.reshape(1, channels), before, pre, sib, pairs
     )
-    recv = lax.all_to_all(partial_value, "exp", 0, 0, tiled=True)
+    partial_value = run_project(mixed, proj, share)
+    recv = lax.all_to_all(partial_value, exp, 0, 0, tiled=True)
     ids = route_ids.reshape(tokens, -1)
     residual, slot_rows = run_dispatch(recv, hidden_in.reshape(tokens, share), ids.T, experts, slots)
-    whole = lax.all_to_all(slot_rows, "exp", 0, 0, tiled=True)
-    normed = run_normalize(whole, norm_gain.reshape(1, -1))
-    segment = lax.all_gather(normed, "ctx", axis=0, tiled=True)
-    part = run_ffn(segment, w_gate[0], w_up[0], w_down[0], slabs, share)
-    returned = lax.psum_scatter(part, "ctx", scatter_dimension=0, tiled=True)[0]
-    back = lax.all_to_all(returned, "exp", 0, 0, tiled=True)
+    whole = lax.all_to_all(slot_rows, exp, 0, 0, tiled=True)
+    own = run_normalize(whole, norm_gain.reshape(1, -1))
+
+    half = slots // 2
+    own_sib = swap(own)
+    low = ring(own, 1)
+    high = ring(own, -1)
+    *weights, turn = run_load(own, w_gate[0], w_up[0], w_down[0])
+    low, high, own_sib, turn = lax.optimization_barrier((low, high, own_sib, turn))
+    far_low, far_high = ring(low[:half], 1), ring(high[half:], -1)
+    low_sib, high_sib = swap(low), swap(high)
+    mine0, other0, turn = run_ffn([([own], [own_sib])], weights, turn, share)
+    from0 = swap(other0)
+    low_sib, high_sib, turn = lax.optimization_barrier((low_sib, high_sib, turn))
+    mine1, other1, mine3, other3, turn = run_ffn([([low], [low_sib]), ([high], [high_sib])], weights, turn, share)
+    far_low, far_high, turn = lax.optimization_barrier((far_low, far_high, turn))
+    mine2, other2, turn = run_ffn(
+        [([far_low, far_high], [swap(far_low), swap(far_high)])], weights, turn, share
+    )
+    back1 = ring(run_add(mine1, swap(other1)), -1)
+    back3 = ring(run_add(mine3, swap(other3)), 1)
+    back2 = ring(run_add(mine2, swap(other2)), 2)
+    returned = run_add(mine0, from0, back1, back3, back2)
+
+    back = lax.all_to_all(returned, exp, 0, 0, tiled=True)
     out = run_combine(back, ids, route_weight.reshape(tokens, -1), residual)
     return out.reshape(slab_len, prompts, share)
 
 
 def solution(mesh):
+    ctx, exp = ("y", "core"), ("x", "z")
+    n_ctx, n_exp = mesh.devices.shape
+    side = int(round(n_exp**0.5))
+    mesh = Mesh(mesh.devices.reshape(n_ctx // 2, 2, side, n_exp // side), ctx + exp)
     placed = (
-        P("ctx", None, "exp"),
-        P("ctx", None, "exp"),
-        P("ctx", None, "exp"),
-        P(None, "exp"),
-        P("ctx", None, None),
-        P("ctx", None, None),
-        P("exp"),
-        P("exp", "ctx"),
-        P("ctx", None, "exp"),
+        P(ctx, None, exp),
+        P(ctx, None, exp),
+        P(ctx, None, exp),
+        P(None, exp),
+        P(ctx, None, None),
+        P(ctx, None, None),
+        P(exp),
+        P(exp, ctx),
+        P(ctx, None, exp),
         P(),
-        P("exp", None, "ctx"),
-        P("exp", None, "ctx"),
-        P("exp", "ctx", None),
-        P("ctx", None, None),
-        P("ctx", None, None),
+        P(exp, None, ctx),
+        P(exp, None, ctx),
+        P(exp, ctx, None),
+        P(ctx, None, None),
+        P(ctx, None, None),
     )
-    return jax.shard_map(
-        on_device, mesh=mesh, in_specs=placed, out_specs=P("ctx", None, "exp"), check_vma=False
-    )
+    return jax.shard_map(on_device, mesh=mesh, in_specs=placed, out_specs=P(ctx, None, exp), check_vma=False)

time: 237 us -> 193 us (0.81)
  waiting for transfers between devices: 119 us -> 73.2 us
  starting transfers between devices: 14.6 us -> 36.1 us
  blocking collectives: 30.4 us -> 13.9 us
  Pallas kernels: 47.8 us -> 44.5 us
    all_gather x2 -> x1, waiting for transfers between devices: 39.8 us -> 0.2 us  [on_device(): proj = lax.all_gather(out_proj, ('y', 'core'))]
    reduce_scatter x1 -> x0, waiting for transfers between devices: 38.1 us -> none  [on_device(): returned = lax.psum_scatter(part, 'ctx', scatter_dimension=0, tiled=True)[0]]
    ppermute x0 -> x20, waiting for transfers between devices: none -> 32.5 us  [the longest x7 25.9 us: ring(): lax.ppermute(value, 'y', [(i, (i + d) % chips) for i in range(chips)])]
    ppermute x0 -> x20, starting transfers between devices: none -> 24.2 us  [the longest x7 12.9 us: ring(): lax.ppermute(value, 'y', [(i, (i + d) % chips) for i in range(chips)])]
    all_gather x1 -> x0, blocking collectives: 15.4 us -> none  [on_device(): ends = lax.all_gather(end, 'ctx')]
    all_to_all x2, starting transfers between devices: 14.3 us -> 11.9 us  [the longest x1 7.72 us: on_device(): recv = lax.all_to_all(partial_value, exp, 0, 0, tiled=True)]
    pallas_call x2 -> x11, Pallas kernels: 39.3 us -> 36.8 us  [the longest x3 15.2 us: run_ffn(): pl.pallas_call(functools.partial(feed_forward, groups=tuple(((len(own), l...]
    unnamed x20 -> x18, local copies, waits for them, and re-layouts: 5.21 us -> 4.7 us
  transfers between devices with their start and end apart: 5 -> 23, of which waited for: 5 -> 11; matrix products, arithmetic and copies ran while one was open for 2% -> 3% of each run, Pallas kernels for 3% -> 20%
where the time goes in v1:
time: 193 us; the launch traced here: 192 us
  waiting for transfers between devices  73.2 us (38%)
  Pallas kernels  44.5 us (23%)
  starting transfers between devices  36.1 us (19%)
  blocking collectives  13.9 us (7%)
  between operations  13.7 us (7%)
  local copies, waits for them, and re-layouts  10.9 us (6%)
    all_to_all x1, waiting for transfers between devices, on_device(): recv = lax.all_to_all(partial_value, exp, 0, 0, tiled=True)  29.3 us
    ppermute x7, waiting for transfers between devices, ring(): lax.ppermute(value, 'y', [(i, (i + d) % chips) for i in range(chips)])  25.9 us
    pallas_call x3, Pallas kernels, run_ffn(): pl.pallas_call(functools.partial(feed_forward, groups=tuple(((len(own), l...  15.2 us
    all_to_all x1, blocking collectives, on_device(): whole = lax.all_to_all(slot_rows, exp, 0, 0, tiled=True)  13.9 us
    ppermute x7, starting transfers between devices, ring(): lax.ppermute(value, 'y', [(i, (i + d) % chips) for i in range(chips)])  12.9 us
    all_to_all x1, waiting for transfers between devices, on_device(): back = lax.all_to_all(returned, exp, 0, 0, tiled=True)  10.5 us
    ppermute x3, starting transfers between devices, on_device(): lax.ppermute(pair, 'y', [(i, i + d) for i in range(chips - d)])  9.07 us
    pallas_call x1, Pallas kernels, run_second(): pl.pallas_call(functools.partial(second_pass, earlier=len(pairs)), out_sh...  8.67 us
  transfers between devices with their start and end apart: 23, of which 11 were waited for; matrix products, arithmetic and copies ran while one was open for 3% of the time, Pallas kernels for 20%

profile of v1, /device:TPU:0, one launch (start us, length us, event | category | flops | bytes accessed | tf_op | source)
XLA Modules:
  0.0 192.2 jit_solution(7426413038465926936)
XLA Ops:
  11.4 6.1 %scan_first.1 = (f32[2,17,512]{2,1,0:T(8,128)S(1)}, f32[2,16,8,512]{3,2,1,0:T(8,128)S(1)}, f32[2,8,512]{2,1,0:T(8,128)S(1)}) custom-call(f32[256,512]{1,0:T(8,128)S(1)} %reshape.37.step_ref, bf16[256,512]{1,0:T(8,128)(2,1)S(1)} %reshape.38.sig_ref, f32[16,8,32]{2,1,0:T(8,128)S(1)} %bitcast.21, f32[16,512]{1,0:T(8,128)S(1)} %copy-done.1), custom_call_target="tpu_custom_call" | custom-call | tf_op jit(solution)/shard_map/scan_first/pallas_call | solution.py:284
  19.0 5.0 %collective-permute-start.1 = (f32[2,17,512]{2,1,0:T(8,128)S(1)}, f32[2,17,512]{2,1,0:T(8,128)S(1)}, u32[]{:S(2)}, u32[]{:S(2)}) collective-permute-start(f32[2,17,512]{2,1,0:T(8,128)S(1)} %pair_up.1), channel_id=1, source_target_pairs={{0,96},{1,97},{2,98},{3,99},{4,100},{5,101},{6,102},{7,103},{8,104... | collective-permute-start | bytes 208904 | tf_op jit(solution)/shard_map/ppermute | solution.py:463
  25.3 2.8 %collective-permute-start.3 = (f32[2,17,512]{2,1,0:T(8,128)S(1)}, f32[2,17,512]{2,1,0:T(8,128)S(1)}, u32[]{:S(2)}, u32[]{:S(2)}) collective-permute-start(f32[2,17,512]{2,1,0:T(8,128)S(1)} %pair_up.1), channel_id=1, source_target_pairs={{0,32},{32,64},{64,96},{1,33},{33,65},{65,97},{2,34},{34,66},{66,9... | collective-permute-start | bytes 208904 | tf_op jit(solution)/shard_map/ppermute | solution.py:463
  30.9 3.6 %collective-permute-done.3.rest_3_ = f32[2,17,512]{2,1,0:T(8,128)S(1)} collective-permute-done((f32[2,17,512]{2,1,0:T(8,128)S(1)}, f32[2,17,512]{2,1,0:T(8,128)S(1)}, u32[]{:S(2)}, u32[]{:S(2)}) %collective-permute-start.3) | collective-permute-done | bytes 69664 | tf_op jit(solution)/shard_map/ppermute | solution.py:463
  35.9 8.7 %scan_second.1.mixed_ref = bf16[256,512]{1,0:T(8,128)(2,1)S(1)} custom-call(s32[1]{0:T(128)} %bitcast.core_ref, f32[256,512]{1,0:T(8,128)S(1)} %reshape.37.step_ref, bf16[256,512]{1,0:T(8,128)(2,1)S(1)} %reshape.38.sig_ref, bf16[256,512]{1,0:T(8,128)(2,1)S(1)} %reshape.39.gate_ref, f32[16,8,32]{2,1,0:T(8,128)S(1)} %bitcast.22, f32[16,8,32]{2,1,0:T(8,128)S(1)} %bitcast.23, ...), custom_call_target="tpu_custom_call" | custom-call | flops 2000000000 | bytes 2097152 | tf_op jit(solution)/shard_map/scan_second/pallas_call | solution.py:319
  44.8 2.2 %copy-done = bf16[4096,512]{1,0:T(8,128)(2,1)S(1)} copy-done((bf16[4096,512]{1,0:T(8,128)(2,1)S(1)}, bf16[4096,512]{1,0:T(8,128)(2,1)}, u32[]{:S(2)}) %copy-start) | copy-done | bytes 4194328
  47.0 4.1 %project.1 = bf16[16,256,256]{2,1,0:T(8,128)(2,1)} custom-call(bf16[256,512]{1,0:T(8,128)(2,1)S(1)} %scan_second.1.mixed_ref, bf16[8,512,512]{2,1,0:T(8,128)(2,1)S(1)} %bitcast.17), custom_call_target="tpu_custom_call" | custom-call | tf_op jit(solution)/shard_map/project/pallas_call | solution.py:340
  51.1 7.7 %all-to-all-start = ((bf16[16,256,256]{2,1,0:T(8,128)(2,1)}), bf16[16,256,256]{2,1,0:T(8,128)(2,1)S(1)}, u32[]{:S(2)}, u32[]{:S(2)}) async-start(bf16[16,256,256]{2,1,0:T(8,128)(2,1)} %project.1), calls=%async_computation | async-start | bytes 4194304 | tf_op jit(solution)/shard_map/all_to_all | solution.py:471
  59.2 29.3 %all-to-all-done.recv_ref = bf16[16,256,256]{2,1,0:T(8,128)(2,1)S(1)} async-done(((bf16[16,256,256]{2,1,0:T(8,128)(2,1)}), bf16[16,256,256]{2,1,0:T(8,128)(2,1)S(1)}, u32[]{:S(2)}, u32[]{:S(2)}) %all-to-all-start) | async-done | bytes 2097184 | tf_op jit(solution)/shard_map/all_to_all | solution.py:471
  89.1 13.9 %all_to_all.15.recv_ref = bf16[16,64,256]{2,1,0:T(8,128)(2,1)S(1)} all-to-all(bf16[16,64,256]{2,1,0:T(8,128)(2,1)S(1)} %get-tuple-element.37), channel_id=1, replica_groups=mesh['y'=4,'core'=2,'x'=4,'z'=4] {'x','z'}, dimensions={0} | all-to-all | bytes 1048576 | tf_op jit(solution)/shard_map/all_to_all | solution.py:474
  103.1 2.5 %collective-permute-start.4 = (bf16[64,4096]{1,0:T(8,128)(2,1)S(1)}, bf16[64,4096]{1,0:T(8,128)(2,1)S(1)}, u32[]{:S(2)}, u32[]{:S(2)}) collective-permute-start(bf16[64,4096]{1,0:T(8,128)(2,1)S(1)} %normalize.1.after_ref.refs_0_), channel_id=1, source_target_pairs={{0,32},{32,64},{64,96},{96,0},{1,33},{33,65},{65,97},{97,1},{2,34}... | collective-permute-start | bytes 1572872 | tf_op jit(solution)/shard_map/ppermute | solution.py:452
  105.6 3.2 %collective-permute-start.5 = (bf16[64,4096]{1,0:T(8,128)(2,1)S(1)}, bf16[64,4096]{1,0:T(8,128)(2,1)S(1)}, u32[]{:S(2)}, u32[]{:S(2)}) collective-permute-start(bf16[64,4096]{1,0:T(8,128)(2,1)S(1)} %normalize.1.after_ref.refs_0_), channel_id=1, source_target_pairs={{0,96},{32,0},{64,32},{96,64},{1,97},{33,1},{65,33},{97,65},{2,98}... | collective-permute-start | bytes 1572872 | tf_op jit(solution)/shard_map/ppermute | solution.py:452
  108.8 7.3 %load_weights.1 = (bf16[4096,896]{1,0:T(8,128)(2,1)S(1)}, bf16[4096,896]{1,0:T(8,128)(2,1)S(1)}, bf16[896,4096]{1,0:T(8,128)(2,1)S(1)}, f32[8,128]{1,0:T(8,128)S(1)}) custom-call(bf16[64,4096]{1,0:T(8,128)(2,1)S(1)} %normalize.1.after_ref.refs_0_, bf16[4096,896]{1,0:T(8,128)(2,1)} %bitcast.26, bf16[4096,896]{1,0:T(8,128)(2,1)} %bitcast.27, ...), custom_call_target="tpu_custom_call" | custom-call | bytes 44040192 | tf_op jit(solution)/shard_map/load_weights/pallas_call | solution.py:380
  116.1 1.9 collective-permute-done.4.refs_0_
  120.2 1.7 collective-permute-start.15
  121.9 3.8 %feed_forward.3 = (bf16[16,64,256]{2,1,0:T(8,128)(2,1)S(1)}, bf16[16,64,256]{2,1,0:T(8,128)(2,1)S(1)}, f32[8,128]{1,0:T(8,128)S(1)}) custom-call(bf16[64,4096]{1,0:T(8,128)(2,1)S(1)} %normalize.1.after_ref.refs_0_, bf16[64,4096]{1,0:T(8,128)(2,1)S(1)} %collective-permute-done.6.refs_1_, bf16[4096,896]{1,0:T(8,128)(2,1)S(1)} %get-tuple-element.40.refs_2_.refs_4_, ...), custom_call_target="tpu_custom_call" | custom-call | flops 2818572288 | bytes 2097152 | tf_op jit(solution)/shard_map/feed_forward/pallas_call | solution.py:399
  125.7 7.2 %feed_forward.4 = (bf16[16,64,256]{2,1,0:T(8,128)(2,1)S(1)}, bf16[16,64,256]{2,1,0:T(8,128)(2,1)S(1)}, bf16[16,64,256]{2,1,0:T(8,128)(2,1)S(1)}, bf16[16,64,256]{2,1,0:T(8,128)(2,1)S(1)}, f32[8,128]{1,0:T(8,128)S(1)}) custom-call(bf16[64,4096]{1,0:T(8,128)(2,1)S(1)} %collective-permute-done.4.refs_0_, bf16[64,4096]{1,0:T(8,128)(2,1)S(1)} %collective-permute-done.8.refs_1_, ...), custom_call_target="tpu_custom_call" | custom-call | flops 5637144576 | bytes 4194304 | tf_op jit(solution)/shard_map/feed_forward/pallas_call | solution.py:399
  134.9 4.3 %feed_forward.5 = (bf16[16,64,256]{2,1,0:T(8,128)(2,1)S(1)}, bf16[16,64,256]{2,1,0:T(8,128)(2,1)S(1)}, f32[8,128]{1,0:T(8,128)}) custom-call(bf16[32,4096]{1,0:T(8,128)(2,1)S(1)} %collective-permute-done.14.refs_0_, bf16[32,4096]{1,0:T(8,128)(2,1)S(1)} %collective-permute-done.15.refs_1_, bf16[32,4096]{1,0:T(8,128)(2,1)S(1)} %collective-permute-done.16.refs_2_, ...), custom_call_target="tpu_custom_call" | custom-call | flops 2818572288 | bytes 2097152 | tf_op jit(solution)/shard_map/feed_forward/pallas_call | solution.py:399
  139.8 1.8 collective-permute-start.11
  142.3 1.7 collective-permute-start.19
  144.0 20.4 %collective-permute-done.11.refs_2_ = bf16[16,64,256]{2,1,0:T(8,128)(2,1)S(1)} collective-permute-done((bf16[16,64,256]{2,1,0:T(8,128)(2,1)S(1)}, bf16[16,64,256]{2,1,0:T(8,128)(2,1)S(1)}, u32[]{:S(2)}, u32[]{:S(2)}) %collective-permute-start.11) | collective-permute-done | bytes 524320 | tf_op jit(solution)/shard_map/ppermute | solution.py:452
  164.4 3.6 %collective-permute-done.13.refs_3_ = bf16[16,64,256]{2,1,0:T(8,128)(2,1)S(1)} collective-permute-done((bf16[16,64,256]{2,1,0:T(8,128)(2,1)S(1)}, bf16[16,64,256]{2,1,0:T(8,128)(2,1)S(1)}, u32[]{:S(2)}, u32[]{:S(2)}) %collective-permute-start.13) | collective-permute-done | bytes 524320 | tf_op jit(solution)/shard_map/ppermute | solution.py:452
  169.1 4.1 %all-to-all-start.2 = ((bf16[16,64,256]{2,1,0:T(8,128)(2,1)}), bf16[16,64,256]{2,1,0:T(8,128)(2,1)S(1)}, u32[]{:S(2)}, u32[]{:S(2)}) async-start(bf16[16,64,256]{2,1,0:T(8,128)(2,1)} %add_up.7), calls=%async_computation.2 | async-start | bytes 1048576 | tf_op jit(solution)/shard_map/all_to_all | solution.py:498
  173.5 10.5 %all-to-all-done.2.recv_ref = bf16[16,64,256]{2,1,0:T(8,128)(2,1)S(1)} async-done(((bf16[16,64,256]{2,1,0:T(8,128)(2,1)}), bf16[16,64,256]{2,1,0:T(8,128)(2,1)S(1)}, u32[]{:S(2)}, u32[]{:S(2)}) %all-to-all-start.2) | async-done | bytes 524320 | tf_op jit(solution)/shard_map/all_to_all | solution.py:498
  (69 shorter events, 21.2 us)
Async XLA Ops:
  6.5 38.2 %all-gather.3.cloned.1.call-start = ((), (), s32[]{:S(2)}) async-start(), calls=%async_computation.3 | async-start | bytes 4718592 | tf_op jit(solution)/shard_map/all_gather | solution.py:454
  17.6 1.4 collective-permute-start
  19.0 11.9 %collective-permute-start.1 = (f32[2,17,512]{2,1,0:T(8,128)S(1)}, f32[2,17,512]{2,1,0:T(8,128)S(1)}, u32[]{:S(2)}, u32[]{:S(2)}) collective-permute-start(f32[2,17,512]{2,1,0:T(8,128)S(1)} %pair_up.1), channel_id=1, source_target_pairs={{0,96},{1,97},{2,98},{3,99},{4,100},{5,101},{6,102},{7,103},{8,104... | collective-permute-start | bytes 208904 | tf_op jit(solution)/shard_map/ppermute | solution.py:463
  24.0 6.9 %collective-permute-start.2 = (f32[2,17,512]{2,1,0:T(8,128)S(1)}, f32[2,17,512]{2,1,0:T(8,128)S(1)}, u32[]{:S(2)}, u32[]{:S(2)}) collective-permute-start(f32[2,17,512]{2,1,0:T(8,128)S(1)} %pair_up.1), channel_id=1, source_target_pairs={{0,64},{32,96},{1,65},{33,97},{2,66},{34,98},{3,67},{35,99},{4,68}... | collective-permute-start | bytes 208904 | tf_op jit(solution)/shard_map/ppermute | solution.py:463
  25.3 9.2 %collective-permute-start.3 = (f32[2,17,512]{2,1,0:T(8,128)S(1)}, f32[2,17,512]{2,1,0:T(8,128)S(1)}, u32[]{:S(2)}, u32[]{:S(2)}) collective-permute-start(f32[2,17,512]{2,1,0:T(8,128)S(1)} %pair_up.1), channel_id=1, source_target_pairs={{0,32},{32,64},{64,96},{1,33},{33,65},{65,97},{2,34},{34,66},{66,9... | collective-permute-start | bytes 208904 | tf_op jit(solution)/shard_map/ppermute | solution.py:463
  35.9 67.0 %copy-start.3 = (f32[4096]{0:T(1024)S(1)}, f32[4096]{0:T(1024)}, u32[]{:S(2)}) copy-start(f32[4096]{0:T(1024)} %param.24) | copy-start | bytes 49156
  51.1 37.4 %all-to-all-start = ((bf16[16,256,256]{2,1,0:T(8,128)(2,1)}), bf16[16,256,256]{2,1,0:T(8,128)(2,1)S(1)}, u32[]{:S(2)}, u32[]{:S(2)}) async-start(bf16[16,256,256]{2,1,0:T(8,128)(2,1)} %project.1), calls=%async_computation | async-start | bytes 4194304 | tf_op jit(solution)/shard_map/all_to_all | solution.py:471
  103.1 14.8 %collective-permute-start.4 = (bf16[64,4096]{1,0:T(8,128)(2,1)S(1)}, bf16[64,4096]{1,0:T(8,128)(2,1)S(1)}, u32[]{:S(2)}, u32[]{:S(2)}) collective-permute-start(bf16[64,4096]{1,0:T(8,128)(2,1)S(1)} %normalize.1.after_ref.refs_0_), channel_id=1, source_target_pairs={{0,32},{32,64},{64,96},{96,0},{1,33},{33,65},{65,97},{97,1},{2,34}... | collective-permute-start | bytes 1572872 | tf_op jit(solution)/shard_map/ppermute | solution.py:452
  105.6 12.4 %collective-permute-start.5 = (bf16[64,4096]{1,0:T(8,128)(2,1)S(1)}, bf16[64,4096]{1,0:T(8,128)(2,1)S(1)}, u32[]{:S(2)}, u32[]{:S(2)}) collective-permute-start(bf16[64,4096]{1,0:T(8,128)(2,1)S(1)} %normalize.1.after_ref.refs_0_), channel_id=1, source_target_pairs={{0,96},{32,0},{64,32},{96,64},{1,97},{33,1},{65,33},{97,65},{2,98}... | collective-permute-start | bytes 1572872 | tf_op jit(solution)/shard_map/ppermute | solution.py:452
  108.8 9.2 %collective-permute-start.6 = (bf16[64,4096]{1,0:T(8,128)(2,1)S(1)}, bf16[64,4096]{1,0:T(8,128)(2,1)S(1)}, u32[]{:S(2)}, u32[]{:S(2)}) collective-permute-start(bf16[64,4096]{1,0:T(8,128)(2,1)S(1)} %normalize.1.after_ref.refs_0_), channel_id=1, source_target_pairs={{0,16},{16,0},{1,17},{17,1},{2,18},{18,2},{3,19},{19,3},{4,20},{20... | collective-permute-start | bytes 1572872 | tf_op jit(solution)/shard_map/ppermute | solution.py:449
  118.0 7.7 %collective-permute-start.8 = (bf16[64,4096]{1,0:T(8,128)(2,1)S(1)}, bf16[64,4096]{1,0:T(8,128)(2,1)S(1)}, u32[]{:S(2)}, u32[]{:S(2)}) collective-permute-start(bf16[64,4096]{1,0:T(8,128)(2,1)S(1)} %collective-permute-done.4.refs_0_), channel_id=1, source_target_pairs={{0,16},{16,0},{1,17},{17,1},{2,18},{18,2},{3,19},{19,3},{4,20},{20... | collective-permute-start | bytes 1572872 | tf_op jit(solution)/shard_map/ppermute | solution.py:449
  118.0 7.7 %collective-permute-start.9 = (bf16[64,4096]{1,0:T(8,128)(2,1)S(1)}, bf16[64,4096]{1,0:T(8,128)(2,1)S(1)}, u32[]{:S(2)}, u32[]{:S(2)}) collective-permute-start(bf16[64,4096]{1,0:T(8,128)(2,1)S(1)} %collective-permute-done.5.refs_2_), channel_id=1, source_target_pairs={{0,16},{16,0},{1,17},{17,1},{2,18},{18,2},{3,19},{19,3},{4,20},{20... | collective-permute-start | bytes 1572872 | tf_op jit(solution)/shard_map/ppermute | solution.py:449
  118.6 14.4 %collective-permute-start.14 = (bf16[32,4096]{1,0:T(8,128)(2,1)S(1)}, bf16[32,4096]{1,0:T(8,128)(2,1)S(1)}, u32[]{:S(2)}, u32[]{:S(2)}) collective-permute-start(bf16[32,4096]{1,0:T(8,128)(2,1)S(1)} %slice.6), channel_id=1, source_target_pairs={{0,32},{32,64},{64,96},{96,0},{1,33},{33,65},{65,97},{97,1},{2,34}... | collective-permute-start | bytes 786440 | tf_op jit(solution)/shard_map/ppermute | solution.py:452
  120.2 12.7 %collective-permute-start.15 = (bf16[32,4096]{1,0:T(8,128)(2,1)S(1)}, bf16[32,4096]{1,0:T(8,128)(2,1)S(1)}, u32[]{:S(2)}, u32[]{:S(2)}) collective-permute-start(bf16[32,4096]{1,0:T(8,128)(2,1)S(1)} %slice.7), channel_id=1, source_target_pairs={{0,96},{32,0},{64,32},{96,64},{1,97},{33,1},{65,33},{97,65},{2,98}... | collective-permute-start | bytes 786440 | tf_op jit(solution)/shard_map/ppermute | solution.py:452
  132.9 1.6 collective-permute-start.16
  133.0 1.9 collective-permute-start.17
  133.5 6.2 %collective-permute-start.10 = (bf16[16,64,256]{2,1,0:T(8,128)(2,1)S(1)}, bf16[16,64,256]{2,1,0:T(8,128)(2,1)S(1)}, u32[]{:S(2)}, u32[]{:S(2)}) collective-permute-start(bf16[16,64,256]{2,1,0:T(8,128)(2,1)S(1)} %get-tuple-element.53), channel_id=1, source_target_pairs={{0,16},{16,0},{1,17},{17,1},{2,18},{18,2},{3,19},{19,3},{4,20},{20... | collective-permute-start | bytes 1572872 | tf_op jit(solution)/shard_map/ppermute | solution.py:449
  133.6 8.0 %collective-permute-start.12 = (bf16[16,64,256]{2,1,0:T(8,128)(2,1)S(1)}, bf16[16,64,256]{2,1,0:T(8,128)(2,1)S(1)}, u32[]{:S(2)}, u32[]{:S(2)}) collective-permute-start(bf16[16,64,256]{2,1,0:T(8,128)(2,1)S(1)} %get-tuple-element.55), channel_id=1, source_target_pairs={{0,16},{16,0},{1,17},{17,1},{2,18},{18,2},{3,19},{19,3},{4,20},{20... | collective-permute-start | bytes 1572872 | tf_op jit(solution)/shard_map/ppermute | solution.py:449
  139.2 2.9 %collective-permute-start.18 = (bf16[16,64,256]{2,1,0:T(8,128)(2,1)S(1)}, bf16[16,64,256]{2,1,0:T(8,128)(2,1)S(1)}, u32[]{:S(2)}, u32[]{:S(2)}) collective-permute-start(bf16[16,64,256]{2,1,0:T(8,128)(2,1)S(1)} %get-tuple-element.61), channel_id=1, source_target_pairs={{0,16},{16,0},{1,17},{17,1},{2,18},{18,2},{3,19},{19,3},{4,20},{20... | collective-permute-start | bytes 1572872 | tf_op jit(solution)/shard_map/ppermute | solution.py:449
  139.3 4.7 %collective-permute-start.7 = (bf16[16,64,256]{2,1,0:T(8,128)(2,1)S(1)}, bf16[16,64,256]{2,1,0:T(8,128)(2,1)S(1)}, u32[]{:S(2)}, u32[]{:S(2)}) collective-permute-start(bf16[16,64,256]{2,1,0:T(8,128)(2,1)S(1)} %get-tuple-element.45), channel_id=1, source_target_pairs={{0,16},{16,0},{1,17},{17,1},{2,18},{18,2},{3,19},{19,3},{4,20},{20... | collective-permute-start | bytes 1572872 | tf_op jit(solution)/shard_map/ppermute | solution.py:449
  139.8 24.6 %collective-permute-start.11 = (bf16[16,64,256]{2,1,0:T(8,128)(2,1)S(1)}, bf16[16,64,256]{2,1,0:T(8,128)(2,1)S(1)}, u32[]{:S(2)}, u32[]{:S(2)}) collective-permute-start(bf16[16,64,256]{2,1,0:T(8,128)(2,1)S(1)} %add_up.4), channel_id=1, source_target_pairs={{0,96},{32,0},{64,32},{96,64},{1,97},{33,1},{65,33},{97,65},{2,98}... | collective-permute-start | bytes 1572872 | tf_op jit(solution)/shard_map/ppermute | solution.py:452
  141.8 26.2 %collective-permute-start.13 = (bf16[16,64,256]{2,1,0:T(8,128)(2,1)S(1)}, bf16[16,64,256]{2,1,0:T(8,128)(2,1)S(1)}, u32[]{:S(2)}, u32[]{:S(2)}) collective-permute-start(bf16[16,64,256]{2,1,0:T(8,128)(2,1)S(1)} %add_up.5), channel_id=1, source_target_pairs={{0,32},{32,64},{64,96},{96,0},{1,33},{33,65},{65,97},{97,1},{2,34}... | collective-permute-start | bytes 1572872 | tf_op jit(solution)/shard_map/ppermute | solution.py:452
  142.3 25.7 %collective-permute-start.19 = (bf16[16,64,256]{2,1,0:T(8,128)(2,1)S(1)}, bf16[16,64,256]{2,1,0:T(8,128)(2,1)S(1)}, u32[]{:S(2)}, u32[]{:S(2)}) collective-permute-start(bf16[16,64,256]{2,1,0:T(8,128)(2,1)S(1)} %add_up.6), channel_id=1, source_target_pairs={{0,64},{32,96},{64,0},{96,32},{1,65},{33,97},{65,1},{97,33},{2,66}... | collective-permute-start | bytes 1572872 | tf_op jit(solution)/shard_map/ppermute | solution.py:452
  169.1 14.8 %all-to-all-start.2 = ((bf16[16,64,256]{2,1,0:T(8,128)(2,1)}), bf16[16,64,256]{2,1,0:T(8,128)(2,1)S(1)}, u32[]{:S(2)}, u32[]{:S(2)}) async-start(bf16[16,64,256]{2,1,0:T(8,128)(2,1)} %add_up.7), calls=%async_computation.2 | async-start | bytes 1048576 | tf_op jit(solution)/shard_map/all_to_all | solution.py:498
  (7 other events, 84.4 us)
Sparse Core Ops, SparseCore 0:
  9.1 35.6 all-gather.2

commit v2 on v1

--- a/solution.py
+++ b/solution.py
@@ -12,6 +12,7 @@
 LOG2E = 1.4426950408889634
 SUBS = 8
 LANES = 128
+UNROLL = 16
 MIB = 1 << 20
 f32, bf16 = jnp.float32, jnp.bfloat16
 
@@ -148,15 +149,18 @@
                 y4[q, rows, :] = (sums[0] + sums[1]) + (sums[2] + sums[3])
                 return tuple(new)
 
-            lax.fori_loop(0, turns, turn, hs)
+            lax.fori_loop(0, turns, turn, hs, unroll=UNROLL)
         sig = sig_ref[:, lanes].astype(f32)
         gate = gate_ref[:, lanes].astype(f32)
         y = y4[q] + skip_ref[:, lanes] * sig
         mixed_ref[:, lanes] = (y * (gate / (1.0 + jnp.exp(-gate)))).astype(bf16)
 
 
-def project(mixed_ref, proj_hbm, out_ref, proj, sem):
-    width = out_ref.shape[2]
+def project(coords_ref, mixed_ref, ids_ref, proj_hbm, *rest, sides):
+    nx, nz = sides
+    z_refs, x_refs = rest[:nz], rest[nz : nz + nx]
+    ids_out, turn_out, whole, proj, sem = rest[nz + nx :]
+    _, half, width = z_refs[0].shape
     blocks, _, columns = proj.shape
     for c in range(blocks):
         pltpu.make_async_copy(proj_hbm.at[c], proj.at[c], sem.at[c]).start()
@@ -164,16 +168,43 @@
         pltpu.make_async_copy(proj_hbm.at[c], proj.at[c], sem.at[c]).wait()
         part = jnp.dot(mixed_ref[...], proj[c], preferred_element_type=f32).astype(bf16)
         for i in range(columns // width):
-            out_ref[c * (columns // width) + i] = part[:, i * width : (i + 1) * width]
-
-
-def dispatch(recv_ref, hidden_ref, ids_ref, res_ref, slots_ref, pick):
+            whole[c * (columns // width) + i] = part[:, i * width : (i + 1) * width]
+    x, z = coords_ref[1], coords_ref[2]
+    for d, out in enumerate(z_refs):
+        for i in range(nx):
+            out[i] = whole[i * nz + lax.rem(z + d, nz), :half]
+    for d, out in enumerate(x_refs):
+        for i in range(nz):
+            out[i] = whole[lax.rem(x + d, nx) * nz + i, half:]
+    ids_out[...] = ids_ref[...]
+    turn_out[...] = jnp.zeros_like(turn_out)
+
+
+def fold(coords_ref, *rest, sides):
+    nx, nz = sides
+    z_refs, x_refs = rest[:nz], rest[nz : nz + nx]
+    first_refs, last_refs = rest[nz + nx : nz + 2 * nx], rest[nz + 2 * nx :]
+    x, z = coords_ref[1], coords_ref[2]
+    for parts, outs, at, count in ((z_refs, first_refs, x, nx), (x_refs, last_refs, z, nz)):
+        for d, out in enumerate(outs):
+            block = lax.rem(at + d, count)
+            total = parts[0][block].astype(f32)
+            for p in parts[1:]:
+                total = total + p[block].astype(f32)
+            out[...] = total.astype(bf16)
+
+
+def dispatch(*refs, sides):
+    *recvs, hidden_ref, ids_ref, res_ref, slots_ref, pick = refs
     experts, slots, width = slots_ref.shape
     tokens = hidden_ref.shape[0]
-    total = hidden_ref[...].astype(f32)
-    for i in range(recv_ref.shape[0]):
-        total = total + recv_ref[i].astype(f32)
-    res_ref[...] = total
+    half = tokens // 2
+    for rows, parts in ((slice(0, half), recvs[: sides[0]]), (slice(half, tokens), recvs[sides[0] :])):
+        part = hidden_ref[rows].astype(f32)
+        for p in parts:
+            part = part + p[...].astype(f32)
+        res_ref[rows] = part
+    total = res_ref[...]
     expert = lax.broadcasted_iota(jnp.int32, (experts, tokens), 0)
     chosen = jnp.zeros((experts, tokens), f32)
     for k in range(ids_ref.shape[0]):
@@ -209,7 +240,7 @@
     copies = [pltpu.make_async_copy(s, t, sem.at[i]) for i, (s, t) in enumerate(zip(sources, targets))]
     for c in copies:
         c.start()
-    turn_out[...] = after_ref[: turn_out.shape[0], : turn_out.shape[1]].astype(f32) * 0.0
+    turn_out[...] = after_ref[...]
     for c in copies:
         c.wait()
 
@@ -335,33 +366,54 @@
     )(core, step, sig, gate, into, outof, rate, skip, before, pre, sib, *pairs)
 
 
-def run_project(mixed, proj, share):
+def run_project(coords, mixed, ids, proj, share, sides):
     tokens = mixed.shape[0]
-    return pl.pallas_call(
-        project,
-        out_shape=jax.ShapeDtypeStruct((proj.shape[0] * proj.shape[2] // share, tokens, share), bf16),
-        in_specs=[vmem(), anywhere()],
-        out_specs=vmem(),
-        scratch_shapes=[pltpu.VMEM(proj.shape, bf16), pltpu.SemaphoreType.DMA((proj.shape[0],))],
+    nx, nz = sides
+    blocks = proj.shape[0] * proj.shape[2] // share
+    return pl.pallas_call(
+        functools.partial(project, sides=sides),
+        out_shape=[jax.ShapeDtypeStruct((nx, tokens // 2, share), bf16)] * nz
+        + [jax.ShapeDtypeStruct((nz, tokens // 2, share), bf16)] * nx
+        + [jax.ShapeDtypeStruct(ids.shape, ids.dtype), jax.ShapeDtypeStruct((8, LANES), f32)],
+        in_specs=[smem(), vmem(), vmem(), anywhere()],
+        out_specs=[vmem()] * (nx + nz + 2),
+        scratch_shapes=[
+            pltpu.VMEM((blocks, tokens, share), bf16),
+            pltpu.VMEM(proj.shape, bf16),
+            pltpu.SemaphoreType.DMA((proj.shape[0],)),
+        ],
         compiler_params=params(16),
         name="project",
-    )(mixed, proj)
-
-
-def run_dispatch(recv, hidden, ids, experts, slots):
+    )(coords, mixed, ids, pltpu.with_memory_space_constraint(proj, pltpu.HBM))
+
+
+def run_fold(coords, parts, sides):
+    nx, nz = sides
+    _, half, share = parts[0].shape
+    return pl.pallas_call(
+        functools.partial(fold, sides=sides),
+        out_shape=[jax.ShapeDtypeStruct((half, share), bf16)] * (nx + nz),
+        in_specs=[smem()] + [vmem()] * (nx + nz),
+        out_specs=[vmem()] * (nx + nz),
+        compiler_params=params(8),
+        name="fold",
+    )(coords, *parts)
+
+
+def run_dispatch(recvs, hidden, ids, experts, slots, sides):
     tokens, share = hidden.shape
     return pl.pallas_call(
-        dispatch,
+        functools.partial(dispatch, sides=sides),
         out_shape=(
             jax.ShapeDtypeStruct((tokens, share), f32),
             jax.ShapeDtypeStruct((experts, slots, share), bf16),
         ),
-        in_specs=[vmem()] * 3,
+        in_specs=[vmem()] * (len(recvs) + 2),
         out_specs=(vmem(),) * 2,
         scratch_shapes=[pltpu.VMEM((experts * slots, tokens), bf16)],
-        compiler_params=params(16),
+        compiler_params=params(8),
         name="dispatch",
-    )(recv, hidden, ids)
+    )(*recvs, hidden, ids)
 
 
 def run_normalize(recv, gain):
@@ -467,10 +519,24 @@
     mixed = run_second(
         core, step, sig, gate, into, outof, decay_rate, skip.reshape(1, channels), before, pre, sib, pairs
     )
-    partial_value = run_project(mixed, proj, share)
-    recv = lax.all_to_all(partial_value, exp, 0, 0, tiled=True)
+    sides = (lax.axis_size("x"), lax.axis_size("z"))
+    coords = jnp.stack([lax.axis_index(a).astype(jnp.int32) for a in ("core", "x", "z")])
+
+    def shift(value, axis, d):
+        n = lax.axis_size(axis)
+        return lax.ppermute(value, axis, [(i, (i + d) % n) for i in range(n)]) if d else value
+
+    nx, nz = sides
     ids = route_ids.reshape(tokens, -1)
-    residual, slot_rows = run_dispatch(recv, hidden_in.reshape(tokens, share), ids.T, experts, slots)
+    *parts, by_choice, turn = run_project(coords, mixed, ids.T, proj, share, sides)
+    hidden = hidden_in.reshape(tokens, share)
+    hidden, ids, turn = lax.optimization_barrier((hidden, ids, turn))
+    *weights, turn = run_load(turn, w_gate[0], w_up[0], w_down[0])
+    parts = [shift(p, "z", d) for d, p in enumerate(parts[:nz])] + [shift(p, "x", d) for d, p in enumerate(parts[nz:])]
+    *parts, turn = lax.optimization_barrier((*parts, turn))
+    parts = run_fold(coords, parts, sides)
+    parts = [shift(p, "x", d) for d, p in enumerate(parts[:nx])] + [shift(p, "z", d) for d, p in enumerate(parts[nx:])]
+    residual, slot_rows = run_dispatch(parts, hidden, by_choice, experts, slots, sides)
     whole = lax.all_to_all(slot_rows, exp, 0, 0, tiled=True)
     own = run_normalize(whole, norm_gain.reshape(1, -1))
 
@@ -478,15 +544,13 @@
     own_sib = swap(own)
     low = ring(own, 1)
     high = ring(own, -1)
-    *weights, turn = run_load(own, w_gate[0], w_up[0], w_down[0])
-    low, high, own_sib, turn = lax.optimization_barrier((low, high, own_sib, turn))
+    mine0, other0, turn = run_ffn([([own], [own_sib])], weights, turn, share)
+    low, high, turn = lax.optimization_barrier((low, high, turn))
+    from0 = swap(other0)
     far_low, far_high = ring(low[:half], 1), ring(high[half:], -1)
     low_sib, high_sib = swap(low), swap(high)
-    mine0, other0, turn = run_ffn([([own], [own_sib])], weights, turn, share)
-    from0 = swap(other0)
-    low_sib, high_sib, turn = lax.optimization_barrier((low_sib, high_sib, turn))
     mine1, other1, mine3, other3, turn = run_ffn([([low], [low_sib]), ([high], [high_sib])], weights, turn, share)
-    far_low, far_high, turn = lax.optimization_barrier((far_low, far_high, turn))
+    far_low, far_high, turn, other1, other3 = lax.optimization_barrier((far_low, far_high, turn, other1, other3))
     mine2, other2, turn = run_ffn(
         [([far_low, far_high], [swap(far_low), swap(far_high)])], weights, turn, share
     )

time: 193 us -> 192 us (level)
  waiting for transfers between devices: 73.2 us -> 53.7 us
  starting transfers between devices: 36.1 us -> 52.1 us
  blocking collectives: 13.9 us -> 16.9 us
    all_to_all x1 -> x0, waiting for transfers between devices: 29.3 us -> none  [on_device(): recv = lax.all_to_all(partial_value, exp, 0, 0, tiled=True)]
    ppermute x0 -> x12, starting transfers between devices: none -> 26.3 us  [shift(): lax.ppermute(value, axis, [(i, (i + d) % n) for i in range(n)])]
    all_to_all x1 -> x0, starting transfers between devices: 7.72 us -> none  [on_device(): recv = lax.all_to_all(partial_value, exp, 0, 0, tiled=True)]
    ppermute x7, waiting for transfers between devices: 25.9 us -> 33.2 us  [ring(): lax.ppermute(value, 'y', [(i, (i + d) % chips) for i in range(chips)])]
    all_to_all x1, blocking collectives: 13.9 us -> 16.9 us  [on_device(): whole = lax.all_to_all(slot_rows, exp, 0, 0, tiled=True)]
    pallas_call x1, Pallas kernels: 8.67 us -> 6.62 us  [run_second(): pl.pallas_call(functools.partial(second_pass, earlier=len(pairs)), out_sh...]
    ppermute x0 -> x12, waiting for transfers between devices: none -> 2.02 us  [shift(): lax.ppermute(value, axis, [(i, (i + d) % n) for i in range(n)])]
    ppermute x7, starting transfers between devices: 12.9 us -> 10.9 us  [ring(): lax.ppermute(value, 'y', [(i, (i + d) % chips) for i in range(chips)])]
  transfers between devices with their start and end apart: 23 -> 34, of which waited for: 11 -> 11; matrix products, arithmetic and copies ran while one was open for 3% -> 4% of each run, Pallas kernels for 20% -> 19%
where the time goes in v2:
time: 192 us; the launch traced here: 191 us
  waiting for transfers between devices  53.7 us (28%)
  starting transfers between devices  52.1 us (27%)
  Pallas kernels  43.8 us (23%)
  blocking collectives  16.9 us (9%)
  between operations  13.7 us (7%)
  local copies, waits for them, and re-layouts  11.1 us (6%)
    ppermute x7, waiting for transfers between devices, ring(): lax.ppermute(value, 'y', [(i, (i + d) % chips) for i in range(chips)])  33.2 us
    ppermute x12, starting transfers between devices, shift(): lax.ppermute(value, axis, [(i, (i + d) % n) for i in range(n)])  26.3 us
    all_to_all x1, blocking collectives, on_device(): whole = lax.all_to_all(slot_rows, exp, 0, 0, tiled=True)  16.9 us
    pallas_call x3, Pallas kernels, run_ffn(): pl.pallas_call(functools.partial(feed_forward, groups=tuple(((len(own), l...  15.2 us
    ppermute x7, starting transfers between devices, ring(): lax.ppermute(value, 'y', [(i, (i + d) % chips) for i in range(chips)])  10.9 us
    all_to_all x1, waiting for transfers between devices, on_device(): back = lax.all_to_all(returned, exp, 0, 0, tiled=True)  10.7 us
    ppermute x3, starting transfers between devices, on_device(): lax.ppermute(pair, 'y', [(i, i + d) for i in range(chips - d)])  9.07 us
    pallas_call x1, Pallas kernels, run_load(): pl.pallas_call(load_weights, out_shape=[pltpu.VMEM(w.shape, w.dtype) for...  7.29 us
  transfers between devices with their start and end apart: 34, of which 11 were waited for; matrix products, arithmetic and copies ran while one was open for 4% of the time, Pallas kernels for 19%

profile of v2, /device:TPU:0, one launch (start us, length us, event | category | flops | bytes accessed | tf_op | source)
XLA Modules:
  0.0 191.5 jit_solution(17004469465871138084)
XLA Ops:
  11.4 6.1 %scan_first.1 = (f32[2,17,512]{2,1,0:T(8,128)S(1)}, f32[2,16,8,512]{3,2,1,0:T(8,128)S(1)}, f32[2,8,512]{2,1,0:T(8,128)S(1)}) custom-call(f32[256,512]{1,0:T(8,128)S(1)} %reshape.34.step_ref, bf16[256,512]{1,0:T(8,128)(2,1)S(1)} %reshape.35.sig_ref, f32[16,8,32]{2,1,0:T(8,128)S(1)} %bitcast.22, f32[16,512]{1,0:T(8,128)S(1)} %copy-done), custom_call_target="tpu_custom_call" | custom-call | tf_op jit(solution)/shard_map/scan_first/pallas_call | solution.py:315
  21.4 5.0 %collective-permute-start.1 = (f32[2,17,512]{2,1,0:T(8,128)S(1)}, f32[2,17,512]{2,1,0:T(8,128)S(1)}, u32[]{:S(2)}, u32[]{:S(2)}) collective-permute-start(f32[2,17,512]{2,1,0:T(8,128)S(1)} %pair_up.1), channel_id=1, source_target_pairs={{0,96},{1,97},{2,98},{3,99},{4,100},{5,101},{6,102},{7,103},{8,104... | collective-permute-start | bytes 208904 | tf_op jit(solution)/shard_map/ppermute | solution.py:515
  27.7 2.8 %collective-permute-start.3 = (f32[2,17,512]{2,1,0:T(8,128)S(1)}, f32[2,17,512]{2,1,0:T(8,128)S(1)}, u32[]{:S(2)}, u32[]{:S(2)}) collective-permute-start(f32[2,17,512]{2,1,0:T(8,128)S(1)} %pair_up.1), channel_id=1, source_target_pairs={{0,32},{32,64},{64,96},{1,33},{33,65},{65,97},{2,34},{34,66},{66,9... | collective-permute-start | bytes 208904 | tf_op jit(solution)/shard_map/ppermute | solution.py:515
  30.5 2.7 %collective-permute-done.1.rest_1_ = f32[2,17,512]{2,1,0:T(8,128)S(1)} collective-permute-done((f32[2,17,512]{2,1,0:T(8,128)S(1)}, f32[2,17,512]{2,1,0:T(8,128)S(1)}, u32[]{:S(2)}, u32[]{:S(2)}) %collective-permute-start.1) | collective-permute-done | bytes 69664 | tf_op jit(solution)/shard_map/ppermute | solution.py:515
  33.3 3.4 %collective-permute-done.3.rest_3_ = f32[2,17,512]{2,1,0:T(8,128)S(1)} collective-permute-done((f32[2,17,512]{2,1,0:T(8,128)S(1)}, f32[2,17,512]{2,1,0:T(8,128)S(1)}, u32[]{:S(2)}, u32[]{:S(2)}) %collective-permute-start.3) | collective-permute-done | bytes 69664 | tf_op jit(solution)/shard_map/ppermute | solution.py:515
  38.1 6.6 %scan_second.1.mixed_ref = bf16[256,512]{1,0:T(8,128)(2,1)S(1)} custom-call(s32[1]{0:T(128)} %bitcast.core_ref, f32[256,512]{1,0:T(8,128)S(1)} %reshape.34.step_ref, bf16[256,512]{1,0:T(8,128)(2,1)S(1)} %reshape.35.sig_ref, bf16[256,512]{1,0:T(8,128)(2,1)S(1)} %reshape.36.gate_ref, f32[16,8,32]{2,1,0:T(8,128)S(1)} %bitcast.23, f32[16,8,32]{2,1,0:T(8,128)S(1)} %bitcast.24, ...), custom_call_target="tpu_custom_call" | custom-call | flops 2000000000 | bytes 2097152 | tf_op jit(solution)/shard_map/scan_second/pallas_call | solution.py:350
  44.8 4.8 %project.1 = (bf16[4,128,256]{2,1,0:T(8,128)(2,1)S(1)}, bf16[4,128,256]{2,1,0:T(8,128)(2,1)S(1)}, bf16[4,128,256]{2,1,0:T(8,128)(2,1)}, bf16[4,128,256]{2,1,0:T(...) custom-call(s32[3]{0:T(128)S(1)} %pad_add_fusion.coords_ref, ...), custom_call_target="tpu_custom_call" | custom-call | tf_op jit(solution)/shard_map/project/pallas_call | solution.py:373
  51.5 3.8 %collective-permute-start.5 = (bf16[4,128,256]{2,1,0:T(8,128)(2,1)}, bf16[4,128,256]{2,1,0:T(8,128)(2,1)S(1)}, u32[]{:S(2)}, u32[]{:S(2)}) collective-permute-start(bf16[4,128,256]{2,1,0:T(8,128)(2,1)} %get-tuple-element.67), channel_id=1, source_target_pairs={{0,2},{1,3},{2,0},{3,1},{4,6},{5,7},{6,4},{7,5},{8,10},{9,11},{10,... | collective-permute-start | bytes 786440 | tf_op jit(solution)/shard_map/ppermute | solution.py:527
  57.7 2.8 %collective-permute-start.8 = (bf16[4,128,256]{2,1,0:T(8,128)(2,1)S(1)}, bf16[4,128,256]{2,1,0:T(8,128)(2,1)S(1)}, u32[]{:S(2)}, u32[]{:S(2)}) collective-permute-start(bf16[4,128,256]{2,1,0:T(8,128)(2,1)S(1)} %get-tuple-element.71), channel_id=1, source_target_pairs={{0,8},{4,12},{8,0},{12,4},{1,9},{5,13},{9,1},{13,5},{2,10},{6,14},... | collective-permute-start | bytes 786440 | tf_op jit(solution)/shard_map/ppermute | solution.py:527
  60.4 2.5 %collective-permute-start.9 = (bf16[4,128,256]{2,1,0:T(8,128)(2,1)S(1)}, bf16[4,128,256]{2,1,0:T(8,128)(2,1)S(1)}, u32[]{:S(2)}, u32[]{:S(2)}) collective-permute-start(bf16[4,128,256]{2,1,0:T(8,128)(2,1)S(1)} %get-tuple-element.72), channel_id=1, source_target_pairs={{0,12},{4,0},{8,4},{12,8},{1,13},{5,1},{9,5},{13,9},{2,14},{6,2},{... | collective-permute-start | bytes 786440 | tf_op jit(solution)/shard_map/ppermute | solution.py:527
  63.9 7.3 %load_weights.1 = (bf16[4096,896]{1,0:T(8,128)(2,1)S(1)}, bf16[4096,896]{1,0:T(8,128)(2,1)S(1)}, bf16[896,4096]{1,0:T(8,128)(2,1)S(1)}, f32[8,128]{1,0:T(8,128)S(1)}) custom-call(f32[8,128]{1,0:T(8,128)S(1)} %get-tuple-element.74.after_ref, bf16[4096,896]{1,0:T(8,128)(2,1)} %bitcast.27, bf16[4096,896]{1,0:T(8,128)(2,1)} %bitcast.28, bf16[896,4096]{1,0:T(8,128)(2,1)} %bitcast.29), custom_call_target="tpu_custom_call" | custom-call | bytes 44040192 | tf_op jit(solution)/shard_map/load_weights/pallas_call | solution.py:432
  78.3 4.1 %collective-permute-start.14 = (bf16[128,256]{1,0:T(8,128)(2,1)S(1)}, bf16[128,256]{1,0:T(8,128)(2,1)S(1)}, u32[]{:S(2)}, u32[]{:S(2)}) collective-permute-start(bf16[128,256]{1,0:T(8,128)(2,1)S(1)} %get-tuple-element.90), channel_id=1, source_target_pairs={{0,2},{1,3},{2,0},{3,1},{4,6},{5,7},{6,4},{7,5},{8,10},{9,11},{10,... | collective-permute-start | bytes 196616 | tf_op jit(solution)/shard_map/ppermute | solution.py:527
  82.4 2.6 %collective-permute-start.15 = (bf16[128,256]{1,0:T(8,128)(2,1)S(1)}, bf16[128,256]{1,0:T(8,128)(2,1)S(1)}, u32[]{:S(2)}, u32[]{:S(2)}) collective-permute-start(bf16[128,256]{1,0:T(8,128)(2,1)S(1)} %get-tuple-element.91), channel_id=1, source_target_pairs={{0,3},{1,0},{2,1},{3,2},{4,7},{5,4},{6,5},{7,6},{8,11},{9,8},{10,9... | collective-permute-start | bytes 196616 | tf_op jit(solution)/shard_map/ppermute | solution.py:527
  87.5 16.9 %all_to_all.10.recv_ref = bf16[16,64,256]{2,1,0:T(8,128)(2,1)S(1)} all-to-all(bf16[16,64,256]{2,1,0:T(8,128)(2,1)S(1)} %get-tuple-element.94), channel_id=1, replica_groups=mesh['y'=4,'core'=2,'x'=4,'z'=4] {'x','z'}, dimensions={0} | all-to-all | bytes 1048576 | tf_op jit(solution)/shard_map/all_to_all | solution.py:540
  104.7 2.7 %collective-permute-start.18 = (bf16[64,4096]{1,0:T(8,128)(2,1)S(1)}, bf16[64,4096]{1,0:T(8,128)(2,1)S(1)}, u32[]{:S(2)}, u32[]{:S(2)}) collective-permute-start(bf16[64,4096]{1,0:T(8,128)(2,1)S(1)} %normalize.1.refs_0_), channel_id=1, source_target_pairs={{0,32},{32,64},{64,96},{96,0},{1,33},{33,65},{65,97},{97,1},{2,34}... | collective-permute-start | bytes 1572872 | tf_op jit(solution)/shard_map/ppermute | solution.py:504
  108.6 3.8 %feed_forward.3 = (bf16[16,64,256]{2,1,0:T(8,128)(2,1)S(1)}, bf16[16,64,256]{2,1,0:T(8,128)(2,1)S(1)}, f32[8,128]{1,0:T(8,128)S(1)}) custom-call(bf16[64,4096]{1,0:T(8,128)(2,1)S(1)} %normalize.1.refs_0_, bf16[64,4096]{1,0:T(8,128)(2,1)S(1)} %collective-permute-done.16.refs_1_, bf16[4096,896]{1,0:T(8,128)(2,1)S(1)} %get-tuple-element.95.refs_2_.refs_4_, ...), custom_call_target="tpu_custom_call" | custom-call | flops 2818572288 | bytes 2097152 | tf_op jit(solution)/shard_map/feed_forward/pallas_call | solution.py:451
  112.4 8.6 %collective-permute-done.18.refs_0_ = bf16[64,4096]{1,0:T(8,128)(2,1)S(1)} collective-permute-done((bf16[64,4096]{1,0:T(8,128)(2,1)S(1)}, bf16[64,4096]{1,0:T(8,128)(2,1)S(1)}, u32[]{:S(2)}, u32[]{:S(2)}) %collective-permute-start.18) | collective-permute-done | bytes 524320 | tf_op jit(solution)/shard_map/ppermute | solution.py:504
  122.8 2.4 %collective-permute-start.23 = (bf16[32,4096]{1,0:T(8,128)(2,1)S(1)}, bf16[32,4096]{1,0:T(8,128)(2,1)S(1)}, u32[]{:S(2)}, u32[]{:S(2)}) collective-permute-start(bf16[32,4096]{1,0:T(8,128)(2,1)S(1)} %slice.7), channel_id=1, source_target_pairs={{0,96},{32,0},{64,32},{96,64},{1,97},{33,1},{65,33},{97,65},{2,98}... | collective-permute-start | bytes 786440 | tf_op jit(solution)/shard_map/ppermute | solution.py:504
  125.2 7.2 %feed_forward.4 = (bf16[16,64,256]{2,1,0:T(8,128)(2,1)S(1)}, bf16[16,64,256]{2,1,0:T(8,128)(2,1)S(1)}, bf16[16,64,256]{2,1,0:T(8,128)(2,1)S(1)}, bf16[16,64,256]{2,1,0:T(8,128)(2,1)S(1)}, f32[8,128]{1,0:T(8,128)S(1)}) custom-call(bf16[64,4096]{1,0:T(8,128)(2,1)S(1)} %collective-permute-done.18.refs_0_, bf16[64,4096]{1,0:T(8,128)(2,1)S(1)} %collective-permute-done.20.refs_1_, ...), custom_call_target="tpu_custom_call" | custom-call | flops 5637144576 | bytes 4194304 | tf_op jit(solution)/shard_map/feed_forward/pallas_call | solution.py:451
  134.4 4.2 %feed_forward.5 = (bf16[16,64,256]{2,1,0:T(8,128)(2,1)S(1)}, bf16[16,64,256]{2,1,0:T(8,128)(2,1)S(1)}, f32[8,128]{1,0:T(8,128)}) custom-call(bf16[32,4096]{1,0:T(8,128)(2,1)S(1)} %collective-permute-done.22.refs_0_, bf16[32,4096]{1,0:T(8,128)(2,1)S(1)} %collective-permute-done.23.refs_1_, bf16[32,4096]{1,0:T(8,128)(2,1)S(1)} %collective-permute-done.28.refs_2_, ...), custom_call_target="tpu_custom_call" | custom-call | flops 2818572288 | bytes 2097152 | tf_op jit(solution)/shard_map/feed_forward/pallas_call | solution.py:451
  143.3 20.7 %collective-permute-done.25.refs_2_ = bf16[16,64,256]{2,1,0:T(8,128)(2,1)S(1)} collective-permute-done((bf16[16,64,256]{2,1,0:T(8,128)(2,1)S(1)}, bf16[16,64,256]{2,1,0:T(8,128)(2,1)S(1)}, u32[]{:S(2)}, u32[]{:S(2)}) %collective-permute-start.25) | collective-permute-done | bytes 524320 | tf_op jit(solution)/shard_map/ppermute | solution.py:504
  164.0 3.6 %collective-permute-done.27.refs_3_ = bf16[16,64,256]{2,1,0:T(8,128)(2,1)S(1)} collective-permute-done((bf16[16,64,256]{2,1,0:T(8,128)(2,1)S(1)}, bf16[16,64,256]{2,1,0:T(8,128)(2,1)S(1)}, u32[]{:S(2)}, u32[]{:S(2)}) %collective-permute-start.27) | collective-permute-done | bytes 524320 | tf_op jit(solution)/shard_map/ppermute | solution.py:504
  168.7 3.6 %all-to-all-start.1 = ((bf16[16,64,256]{2,1,0:T(8,128)(2,1)}), bf16[16,64,256]{2,1,0:T(8,128)(2,1)S(1)}, u32[]{:S(2)}, u32[]{:S(2)}) async-start(bf16[16,64,256]{2,1,0:T(8,128)(2,1)} %add_up.7), calls=%async_computation.1 | async-start | bytes 1048576 | tf_op jit(solution)/shard_map/all_to_all | solution.py:562
  172.4 10.7 %all-to-all-done.1.recv_ref = bf16[16,64,256]{2,1,0:T(8,128)(2,1)S(1)} async-done(((bf16[16,64,256]{2,1,0:T(8,128)(2,1)}), bf16[16,64,256]{2,1,0:T(8,128)(2,1)S(1)}, u32[]{:S(2)}, u32[]{:S(2)}) %all-to-all-start.1) | async-done | bytes 524320 | tf_op jit(solution)/shard_map/all_to_all | solution.py:562
  (89 shorter events, 38.9 us)
Async XLA Ops:
  6.5 38.2 %all-gather.3.cloned.1.call-start = ((), (), s32[]{:S(2)}) async-start(), calls=%async_computation.2 | async-start | bytes 4718592 | tf_op jit(solution)/shard_map/all_gather | solution.py:506
  21.4 11.9 %collective-permute-start.1 = (f32[2,17,512]{2,1,0:T(8,128)S(1)}, f32[2,17,512]{2,1,0:T(8,128)S(1)}, u32[]{:S(2)}, u32[]{:S(2)}) collective-permute-start(f32[2,17,512]{2,1,0:T(8,128)S(1)} %pair_up.1), channel_id=1, source_target_pairs={{0,96},{1,97},{2,98},{3,99},{4,100},{5,101},{6,102},{7,103},{8,104... | collective-permute-start | bytes 208904 | tf_op jit(solution)/shard_map/ppermute | solution.py:515
  26.4 6.9 %collective-permute-start.2 = (f32[2,17,512]{2,1,0:T(8,128)S(1)}, f32[2,17,512]{2,1,0:T(8,128)S(1)}, u32[]{:S(2)}, u32[]{:S(2)}) collective-permute-start(f32[2,17,512]{2,1,0:T(8,128)S(1)} %pair_up.1), channel_id=1, source_target_pairs={{0,64},{32,96},{1,65},{33,97},{2,66},{34,98},{3,67},{35,99},{4,68}... | collective-permute-start | bytes 208904 | tf_op jit(solution)/shard_map/ppermute | solution.py:515
  27.7 9.0 %collective-permute-start.3 = (f32[2,17,512]{2,1,0:T(8,128)S(1)}, f32[2,17,512]{2,1,0:T(8,128)S(1)}, u32[]{:S(2)}, u32[]{:S(2)}) collective-permute-start(f32[2,17,512]{2,1,0:T(8,128)S(1)} %pair_up.1), channel_id=1, source_target_pairs={{0,32},{32,64},{64,96},{1,33},{33,65},{65,97},{2,34},{34,66},{66,9... | collective-permute-start | bytes 208904 | tf_op jit(solution)/shard_map/ppermute | solution.py:515
  49.6 10.8 %collective-permute-start.4 = (bf16[4,128,256]{2,1,0:T(8,128)(2,1)S(1)}, bf16[4,128,256]{2,1,0:T(8,128)(2,1)S(1)}, u32[]{:S(2)}, u32[]{:S(2)}) collective-permute-start(bf16[4,128,256]{2,1,0:T(8,128)(2,1)S(1)} %get-tuple-element.66), channel_id=1, source_target_pairs={{0,1},{1,2},{2,3},{3,0},{4,5},{5,6},{6,7},{7,4},{8,9},{9,10},{10,1... | collective-permute-start | bytes 786440 | tf_op jit(solution)/shard_map/ppermute | solution.py:527
  51.5 19.6 %collective-permute-start.5 = (bf16[4,128,256]{2,1,0:T(8,128)(2,1)}, bf16[4,128,256]{2,1,0:T(8,128)(2,1)S(1)}, u32[]{:S(2)}, u32[]{:S(2)}) collective-permute-start(bf16[4,128,256]{2,1,0:T(8,128)(2,1)} %get-tuple-element.67), channel_id=1, source_target_pairs={{0,2},{1,3},{2,0},{3,1},{4,6},{5,7},{6,4},{7,5},{8,10},{9,11},{10,... | collective-permute-start | bytes 786440 | tf_op jit(solution)/shard_map/ppermute | solution.py:527
  55.3 15.9 %collective-permute-start.6 = (bf16[4,128,256]{2,1,0:T(8,128)(2,1)S(1)}, bf16[4,128,256]{2,1,0:T(8,128)(2,1)S(1)}, u32[]{:S(2)}, u32[]{:S(2)}) collective-permute-start(bf16[4,128,256]{2,1,0:T(8,128)(2,1)S(1)} %get-tuple-element.68), channel_id=1, source_target_pairs={{0,3},{1,0},{2,1},{3,2},{4,7},{5,4},{6,5},{7,6},{8,11},{9,8},{10,9... | collective-permute-start | bytes 786440 | tf_op jit(solution)/shard_map/ppermute | solution.py:527
  56.2 15.0 %collective-permute-start.7 = (bf16[4,128,256]{2,1,0:T(8,128)(2,1)S(1)}, bf16[4,128,256]{2,1,0:T(8,128)(2,1)S(1)}, u32[]{:S(2)}, u32[]{:S(2)}) collective-permute-start(bf16[4,128,256]{2,1,0:T(8,128)(2,1)S(1)} %get-tuple-element.70), channel_id=1, source_target_pairs={{0,4},{4,8},{8,12},{12,0},{1,5},{5,9},{9,13},{13,1},{2,6},{6,10},{... | collective-permute-start | bytes 786440 | tf_op jit(solution)/shard_map/ppermute | solution.py:527
  57.7 13.5 %collective-permute-start.8 = (bf16[4,128,256]{2,1,0:T(8,128)(2,1)S(1)}, bf16[4,128,256]{2,1,0:T(8,128)(2,1)S(1)}, u32[]{:S(2)}, u32[]{:S(2)}) collective-permute-start(bf16[4,128,256]{2,1,0:T(8,128)(2,1)S(1)} %get-tuple-element.71), channel_id=1, source_target_pairs={{0,8},{4,12},{8,0},{12,4},{1,9},{5,13},{9,1},{13,5},{2,10},{6,14},... | collective-permute-start | bytes 786440 | tf_op jit(solution)/shard_map/ppermute | solution.py:527
  60.4 10.8 %collective-permute-start.9 = (bf16[4,128,256]{2,1,0:T(8,128)(2,1)S(1)}, bf16[4,128,256]{2,1,0:T(8,128)(2,1)S(1)}, u32[]{:S(2)}, u32[]{:S(2)}) collective-permute-start(bf16[4,128,256]{2,1,0:T(8,128)(2,1)S(1)} %get-tuple-element.72), channel_id=1, source_target_pairs={{0,12},{4,0},{8,4},{12,8},{1,13},{5,1},{9,5},{13,9},{2,14},{6,2},{... | collective-permute-start | bytes 786440 | tf_op jit(solution)/shard_map/ppermute | solution.py:527
  72.0 10.4 %collective-permute-start.10 = (bf16[128,256]{1,0:T(8,128)(2,1)S(1)}, bf16[128,256]{1,0:T(8,128)(2,1)S(1)}, u32[]{:S(2)}, u32[]{:S(2)}) collective-permute-start(bf16[128,256]{1,0:T(8,128)(2,1)S(1)} %get-tuple-element.85), channel_id=1, source_target_pairs={{0,4},{4,8},{8,12},{12,0},{1,5},{5,9},{9,13},{13,1},{2,6},{6,10},{... | collective-permute-start | bytes 196616 | tf_op jit(solution)/shard_map/ppermute | solution.py:527
  73.9 11.2 %collective-permute-start.11 = (bf16[128,256]{1,0:T(8,128)(2,1)S(1)}, bf16[128,256]{1,0:T(8,128)(2,1)S(1)}, u32[]{:S(2)}, u32[]{:S(2)}) collective-permute-start(bf16[128,256]{1,0:T(8,128)(2,1)S(1)} %get-tuple-element.86), channel_id=1, source_target_pairs={{0,8},{4,12},{8,0},{12,4},{1,9},{5,13},{9,1},{13,5},{2,10},{6,14},... | collective-permute-start | bytes 196616 | tf_op jit(solution)/shard_map/ppermute | solution.py:527
  75.8 9.3 %collective-permute-start.12 = (bf16[128,256]{1,0:T(8,128)(2,1)S(1)}, bf16[128,256]{1,0:T(8,128)(2,1)S(1)}, u32[]{:S(2)}, u32[]{:S(2)}) collective-permute-start(bf16[128,256]{1,0:T(8,128)(2,1)S(1)} %get-tuple-element.87), channel_id=1, source_target_pairs={{0,12},{4,0},{8,4},{12,8},{1,13},{5,1},{9,5},{13,9},{2,14},{6,2},{... | collective-permute-start | bytes 196616 | tf_op jit(solution)/shard_map/ppermute | solution.py:527
  77.1 7.9 %collective-permute-start.13 = (bf16[128,256]{1,0:T(8,128)(2,1)S(1)}, bf16[128,256]{1,0:T(8,128)(2,1)S(1)}, u32[]{:S(2)}, u32[]{:S(2)}) collective-permute-start(bf16[128,256]{1,0:T(8,128)(2,1)S(1)} %get-tuple-element.89), channel_id=1, source_target_pairs={{0,1},{1,2},{2,3},{3,0},{4,5},{5,6},{6,7},{7,4},{8,9},{9,10},{10,1... | collective-permute-start | bytes 196616 | tf_op jit(solution)/shard_map/ppermute | solution.py:527
  78.3 7.1 %collective-permute-start.14 = (bf16[128,256]{1,0:T(8,128)(2,1)S(1)}, bf16[128,256]{1,0:T(8,128)(2,1)S(1)}, u32[]{:S(2)}, u32[]{:S(2)}) collective-permute-start(bf16[128,256]{1,0:T(8,128)(2,1)S(1)} %get-tuple-element.90), channel_id=1, source_target_pairs={{0,2},{1,3},{2,0},{3,1},{4,6},{5,7},{6,4},{7,5},{8,10},{9,11},{10,... | collective-permute-start | bytes 196616 | tf_op jit(solution)/shard_map/ppermute | solution.py:527
  104.7 16.3 %collective-permute-start.18 = (bf16[64,4096]{1,0:T(8,128)(2,1)S(1)}, bf16[64,4096]{1,0:T(8,128)(2,1)S(1)}, u32[]{:S(2)}, u32[]{:S(2)}) collective-permute-start(bf16[64,4096]{1,0:T(8,128)(2,1)S(1)} %normalize.1.refs_0_), channel_id=1, source_target_pairs={{0,32},{32,64},{64,96},{96,0},{1,33},{33,65},{65,97},{97,1},{2,34}... | collective-permute-start | bytes 1572872 | tf_op jit(solution)/shard_map/ppermute | solution.py:504
  107.4 14.0 %collective-permute-start.19 = (bf16[64,4096]{1,0:T(8,128)(2,1)S(1)}, bf16[64,4096]{1,0:T(8,128)(2,1)S(1)}, u32[]{:S(2)}, u32[]{:S(2)}) collective-permute-start(bf16[64,4096]{1,0:T(8,128)(2,1)S(1)} %normalize.1.refs_0_), channel_id=1, source_target_pairs={{0,96},{32,0},{64,32},{96,64},{1,97},{33,1},{65,33},{97,65},{2,98}... | collective-permute-start | bytes 1572872 | tf_op jit(solution)/shard_map/ppermute | solution.py:504
  121.9 10.5 %collective-permute-start.22 = (bf16[32,4096]{1,0:T(8,128)(2,1)S(1)}, bf16[32,4096]{1,0:T(8,128)(2,1)S(1)}, u32[]{:S(2)}, u32[]{:S(2)}) collective-permute-start(bf16[32,4096]{1,0:T(8,128)(2,1)S(1)} %slice.6), channel_id=1, source_target_pairs={{0,32},{32,64},{64,96},{96,0},{1,33},{33,65},{65,97},{97,1},{2,34}... | collective-permute-start | bytes 786440 | tf_op jit(solution)/shard_map/ppermute | solution.py:504
  122.8 9.6 %collective-permute-start.23 = (bf16[32,4096]{1,0:T(8,128)(2,1)S(1)}, bf16[32,4096]{1,0:T(8,128)(2,1)S(1)}, u32[]{:S(2)}, u32[]{:S(2)}) collective-permute-start(bf16[32,4096]{1,0:T(8,128)(2,1)S(1)} %slice.7), channel_id=1, source_target_pairs={{0,96},{32,0},{64,32},{96,64},{1,97},{33,1},{65,33},{97,65},{2,98}... | collective-permute-start | bytes 786440 | tf_op jit(solution)/shard_map/ppermute | solution.py:504
  133.1 8.1 %collective-permute-start.26 = (bf16[16,64,256]{2,1,0:T(8,128)(2,1)S(1)}, bf16[16,64,256]{2,1,0:T(8,128)(2,1)S(1)}, u32[]{:S(2)}, u32[]{:S(2)}) collective-permute-start(bf16[16,64,256]{2,1,0:T(8,128)(2,1)S(1)} %get-tuple-element.111), channel_id=1, source_target_pairs={{0,16},{16,0},{1,17},{17,1},{2,18},{18,2},{3,19},{19,3},{4,20},{20... | collective-permute-start | bytes 1572872 | tf_op jit(solution)/shard_map/ppermute | solution.py:501
  139.3 24.7 %collective-permute-start.25 = (bf16[16,64,256]{2,1,0:T(8,128)(2,1)S(1)}, bf16[16,64,256]{2,1,0:T(8,128)(2,1)S(1)}, u32[]{:S(2)}, u32[]{:S(2)}) collective-permute-start(bf16[16,64,256]{2,1,0:T(8,128)(2,1)S(1)} %add_up.4), channel_id=1, source_target_pairs={{0,96},{32,0},{64,32},{96,64},{1,97},{33,1},{65,33},{97,65},{2,98}... | collective-permute-start | bytes 1572872 | tf_op jit(solution)/shard_map/ppermute | solution.py:504
  141.4 26.2 %collective-permute-start.27 = (bf16[16,64,256]{2,1,0:T(8,128)(2,1)S(1)}, bf16[16,64,256]{2,1,0:T(8,128)(2,1)S(1)}, u32[]{:S(2)}, u32[]{:S(2)}) collective-permute-start(bf16[16,64,256]{2,1,0:T(8,128)(2,1)S(1)} %add_up.5), channel_id=1, source_target_pairs={{0,32},{32,64},{64,96},{96,0},{1,33},{33,65},{65,97},{97,1},{2,34}... | collective-permute-start | bytes 1572872 | tf_op jit(solution)/shard_map/ppermute | solution.py:504
  141.7 25.8 %collective-permute-start.31 = (bf16[16,64,256]{2,1,0:T(8,128)(2,1)S(1)}, bf16[16,64,256]{2,1,0:T(8,128)(2,1)S(1)}, u32[]{:S(2)}, u32[]{:S(2)}) collective-permute-start(bf16[16,64,256]{2,1,0:T(8,128)(2,1)S(1)} %add_up.6), channel_id=1, source_target_pairs={{0,64},{32,96},{64,0},{96,32},{1,65},{33,97},{65,1},{97,33},{2,66}... | collective-permute-start | bytes 1572872 | tf_op jit(solution)/shard_map/ppermute | solution.py:504
  168.7 14.4 %all-to-all-start.1 = ((bf16[16,64,256]{2,1,0:T(8,128)(2,1)}), bf16[16,64,256]{2,1,0:T(8,128)(2,1)S(1)}, u32[]{:S(2)}, u32[]{:S(2)}) async-start(bf16[16,64,256]{2,1,0:T(8,128)(2,1)} %add_up.7), calls=%async_computation.1 | async-start | bytes 1048576 | tf_op jit(solution)/shard_map/all_to_all | solution.py:562
  (16 other events, 113.6 us)
Sparse Core Ops, SparseCore 0:
  9.1 35.6 all-gather.2

commit v3 on v2

--- a/solution.py
+++ b/solution.py
@@ -12,6 +12,7 @@
 LOG2E = 1.4426950408889634
 SUBS = 8
 LANES = 128
+CUT = 1
 UNROLL = 16
 MIB = 1 << 20
 f32, bf16 = jnp.float32, jnp.bfloat16
@@ -93,24 +94,10 @@
             pre_ref[b, :, lanes] = jnp.where(sub >= 1, pltpu.roll(width, 1, 0), 0.0)
 
 
-def pair_up(core_ref, own_ref, sib_ref, rate_ref, out_ref):
-    states = rate_ref.shape[0]
-    low = core_ref[0] == 0
-    rate = rate_ref[...] * -LOG2E
-    for b in range(own_ref.shape[0]):
-        first = jnp.where(low, own_ref[b], sib_ref[b])
-        second = jnp.where(low, sib_ref[b], own_ref[b])
-        decay = jnp.exp2(rate * second[states:])
-        out_ref[b, :states] = decay * first[:states] + second[:states]
-        out_ref[b, states:] = first[states:] + second[states:]
-
-
 def second_pass(
-    core_ref, step_ref, sig_ref, gate_ref, into_ref, outof_ref, rate_ref, skip_ref, before_ref, pre_ref,
-    *rest, earlier,
+    coords_ref, step_ref, sig_ref, gate_ref, into_ref, outof_ref, rate_ref, skip_ref, before_ref, pre_ref,
+    ends_ref, mixed_ref, st4, v4, y4, into_b, outof_b, enter,
 ):
-    sib_ref, *pair_refs = rest[: earlier + 1]
-    mixed_ref, st4, v4, y4, into_b, outof_b, enter = rest[earlier + 1 :]
     states, channels = rate_ref.shape
     prompts = pre_ref.shape[0]
     turns = into_ref.shape[0]
@@ -118,17 +105,18 @@
     spread(into_ref, into_b)
     spread(outof_ref, outof_b)
     split_lanes(step_ref, sig_ref, st4, v4)
-    live = jnp.where(core_ref[0] > 0, 1.0, 0.0).astype(f32)
+    mine = coords_ref[0]
     for q in range(channels // LANES):
         lanes = slice(q * LANES, (q + 1) * LANES)
         rate_q = rate_ref[:, lanes] * -LOG2E
         rates = [jnp.broadcast_to(rate_q[n : n + 1], (SUBS, LANES)) for n in range(states)]
         for b in range(prompts):
             h0 = jnp.zeros((states, LANES), f32)
-            for pair in pair_refs:
-                h0 = jnp.exp2(rate_q * pair[b, states : states + 1, lanes]) * h0 + pair[b, :states, lanes]
-            decay = jnp.exp2(rate_q * (sib_ref[b, states : states + 1, lanes] * live))
-            enter[...] = decay * h0 + sib_ref[b, :states, lanes] * live
+            for c in range(ends_ref.shape[0] - 1):
+                live = jnp.where(c < mine, 1.0, 0.0).astype(f32)
+                decay = jnp.exp2(rate_q * (ends_ref[c, b, states : states + 1, lanes] * live))
+                h0 = decay * h0 + ends_ref[c, b, :states, lanes] * live
+            enter[...] = h0
             pre = pre_ref[b, :, lanes]
             hs = tuple(
                 before_ref[b, n, :, lanes]
@@ -156,28 +144,39 @@
         mixed_ref[:, lanes] = (y * (gate / (1.0 + jnp.exp(-gate)))).astype(bf16)
 
 
-def project(coords_ref, mixed_ref, ids_ref, proj_hbm, *rest, sides):
+def project(coords_ref, mixed_ref, ids_ref, *refs, sides, halves):
     nx, nz = sides
+    sources, rest = refs[:halves], refs[halves:]
     z_refs, x_refs = rest[:nz], rest[nz : nz + nx]
-    ids_out, turn_out, whole, proj, sem = rest[nz + nx :]
+    ids_out, proj, sem = rest[nz + nx :]
     _, half, width = z_refs[0].shape
-    blocks, _, columns = proj.shape
-    for c in range(blocks):
-        pltpu.make_async_copy(proj_hbm.at[c], proj.at[c], sem.at[c]).start()
-    for c in range(blocks):
-        pltpu.make_async_copy(proj_hbm.at[c], proj.at[c], sem.at[c]).wait()
-        part = jnp.dot(mixed_ref[...], proj[c], preferred_element_type=f32).astype(bf16)
-        for i in range(columns // width):
-            whole[c * (columns // width) + i] = part[:, i * width : (i + 1) * width]
+    _, depth, _ = proj.shape
+    per = sources[0].shape[2] // width
+    piece = depth // halves
     x, z = coords_ref[1], coords_ref[2]
-    for d, out in enumerate(z_refs):
-        for i in range(nx):
-            out[i] = whole[i * nz + lax.rem(z + d, nz), :half]
-    for d, out in enumerate(x_refs):
-        for i in range(nz):
-            out[i] = whole[lax.rem(x + d, nx) * nz + i, half:]
+    hops = [(dx, dz) for dx in range(nx) for dz in range(nz)]
+    copies = []
+    for r, (dx, dz) in enumerate(hops):
+        to_x, to_z = lax.rem(x + dx, nx), lax.rem(z + dz, nz)
+        block = to_x * nz + to_z
+        columns = pl.ds(pl.multiple_of(lax.rem(block, per) * width, width), width)
+        copies.append(
+            [
+                pltpu.make_async_copy(
+                    source.at[block // per, :, columns], proj.at[r, i * piece : (i + 1) * piece], sem.at[r, i]
+                )
+                for i, source in enumerate(sources)
+            ]
+        )
+        for c in copies[-1]:
+            c.start()
     ids_out[...] = ids_ref[...]
-    turn_out[...] = jnp.zeros_like(turn_out)
+    for r, (dx, dz) in enumerate(hops):
+        for c in copies[r]:
+            c.wait()
+        part = jnp.dot(mixed_ref[...], proj[r], preferred_element_type=f32).astype(bf16)
+        z_refs[dz][lax.rem(x + dx, nx)] = part[:half]
+        x_refs[dx][lax.rem(z + dz, nz)] = part[half:]
 
 
 def fold(coords_ref, *rest, sides):
@@ -240,12 +239,12 @@
     copies = [pltpu.make_async_copy(s, t, sem.at[i]) for i, (s, t) in enumerate(zip(sources, targets))]
     for c in copies:
         c.start()
-    turn_out[...] = after_ref[...]
+    turn_out[...] = after_ref[: turn_out.shape[0], : turn_out.shape[1]].astype(f32)
     for c in copies:
         c.wait()
 
 
-def feed_forward(*refs, groups):
+def feed_forward(*refs, groups, cut):
     count = sum(sum(g) for g in groups)
     pieces, (w_gate, w_up, w_down, turn_ref) = refs[:count], refs[count : count + 4]
     *outs, turn_out, x, act = refs[count + 4 :]
@@ -254,6 +253,7 @@
         x[at : at + p.shape[0]] = p[...]
         at += p.shape[0]
     blocks, rows, width = outs[0].shape
+    size_out = blocks // cut
     wide = 2 * LANES
     hidden = w_gate.shape[1]
     for i in range(0, hidden, wide):
@@ -266,18 +266,23 @@
     for i in range(blocks):
         part = jnp.dot(act[...], w_down[:, i * width : (i + 1) * width], preferred_element_type=f32)
         part = part.astype(bf16)
-        for j, out in enumerate(outs):
-            out[i] = part[j * rows : (j + 1) * rows]
+        for j in range(len(groups)):
+            own, *others = outs[j * (cut + 1) : (j + 1) * (cut + 1)]
+            own[i] = part[2 * j * rows : (2 * j + 1) * rows]
+            others[i // size_out][i % size_out] = part[(2 * j + 1) * rows : (2 * j + 2) * rows]
     turn_out[...] = turn_ref[...]
 
 
-def add_up(*refs):
+def add_up(*refs, pieces):
     *parts, out_ref = refs
     for i in range(out_ref.shape[0]):
-        total = parts[0][i].astype(f32)
-        for p in parts[1:]:
-            total = total + p[i].astype(f32)
-        out_ref[i] = total.astype(bf16)
+        total, at = None, 0
+        for n in pieces:
+            size = out_ref.shape[0] // n
+            term = parts[at + i // size][i % size].astype(f32)
+            total = term if total is None else total + term
+            at += n
+        out_ref[i] = total.astype(out_ref.dtype)
 
 
 def combine(recv_ref, ids_ref, weight_ref, res_ref, out_ref):
@@ -331,26 +336,15 @@
     )(step, sig, into, rate)
 
 
-def run_pair(core, own, sib, rate):
-    return pl.pallas_call(
-        pair_up,
-        out_shape=jax.ShapeDtypeStruct(own.shape, f32),
-        in_specs=[smem()] + [vmem()] * 3,
-        out_specs=vmem(),
-        compiler_params=params(8),
-        name="pair_up",
-    )(core, own, sib, rate)
-
-
-def run_second(core, step, sig, gate, into, outof, rate, skip, before, pre, sib, pairs):
+def run_second(coords, step, sig, gate, into, outof, rate, skip, before, pre, ends):
     tokens, channels = step.shape
     prompts, states = before.shape[:2]
     turns = into.shape[0]
     tiles = channels // LANES
     return pl.pallas_call(
-        functools.partial(second_pass, earlier=len(pairs)),
+        second_pass,
         out_shape=jax.ShapeDtypeStruct((tokens, channels), bf16),
-        in_specs=[smem()] + [vmem()] * (10 + len(pairs)),
+        in_specs=[smem()] + [vmem()] * 10,
         out_specs=vmem(),
         scratch_shapes=[
             pltpu.VMEM((tiles, tokens, LANES), f32),
@@ -363,28 +357,26 @@
         compiler_params=params(16),
         cost_estimate=pl.CostEstimate(flops=2 * 10**9, bytes_accessed=2 * MIB, transcendentals=0),
         name="scan_second",
-    )(core, step, sig, gate, into, outof, rate, skip, before, pre, sib, *pairs)
+    )(coords, step, sig, gate, into, outof, rate, skip, before, pre, ends)
 
 
 def run_project(coords, mixed, ids, proj, share, sides):
-    tokens = mixed.shape[0]
+    tokens, depth = mixed.shape
     nx, nz = sides
-    blocks = proj.shape[0] * proj.shape[2] // share
-    return pl.pallas_call(
-        functools.partial(project, sides=sides),
+    return pl.pallas_call(
+        functools.partial(project, sides=sides, halves=len(proj)),
         out_shape=[jax.ShapeDtypeStruct((nx, tokens // 2, share), bf16)] * nz
         + [jax.ShapeDtypeStruct((nz, tokens // 2, share), bf16)] * nx
-        + [jax.ShapeDtypeStruct(ids.shape, ids.dtype), jax.ShapeDtypeStruct((8, LANES), f32)],
-        in_specs=[smem(), vmem(), vmem(), anywhere()],
-        out_specs=[vmem()] * (nx + nz + 2),
+        + [jax.ShapeDtypeStruct(ids.shape, ids.dtype)],
+        in_specs=[smem(), vmem(), vmem()] + [anywhere()] * len(proj),
+        out_specs=[vmem()] * (nx + nz + 1),
         scratch_shapes=[
-            pltpu.VMEM((blocks, tokens, share), bf16),
-            pltpu.VMEM(proj.shape, bf16),
-            pltpu.SemaphoreType.DMA((proj.shape[0],)),
+            pltpu.VMEM((nx * nz, depth, share), bf16),
+            pltpu.SemaphoreType.DMA((nx * nz, len(proj))),
         ],
         compiler_params=params(16),
         name="project",
-    )(coords, mixed, ids, pltpu.with_memory_space_constraint(proj, pltpu.HBM))
+    )(coords, mixed, ids, *[pltpu.with_memory_space_constraint(p, pltpu.HBM) for p in proj])
 
 
 def run_fold(coords, parts, sides):
@@ -441,18 +433,19 @@
     )(after, *[pltpu.with_memory_space_constraint(w, pltpu.HBM) for w in weights])
 
 
-def run_ffn(groups, weights, turn, share):
+def run_ffn(groups, weights, turn, share, cut=1):
     pieces = [p for own, other in groups for p in (*own, *other)]
     rows = sum(p.shape[0] for p in groups[0][0])
     depth, hidden = weights[0].shape
     total = 2 * rows * len(groups)
     part = jax.ShapeDtypeStruct((depth // share, rows, share), bf16)
+    piece = jax.ShapeDtypeStruct((depth // share // cut, rows, share), bf16)
     weights = [pltpu.with_memory_space_constraint(w, pltpu.VMEM) for w in weights]
     return pl.pallas_call(
-        functools.partial(feed_forward, groups=tuple((len(own), len(other)) for own, other in groups)),
-        out_shape=(part,) * (2 * len(groups)) + (jax.ShapeDtypeStruct(turn.shape, turn.dtype),),
+        functools.partial(feed_forward, groups=tuple((len(own), len(other)) for own, other in groups), cut=cut),
+        out_shape=(part, *(piece,) * cut) * len(groups) + (jax.ShapeDtypeStruct(turn.shape, turn.dtype),),
         in_specs=[vmem()] * (len(pieces) + 4),
-        out_specs=(vmem(),) * (2 * len(groups) + 1),
+        out_specs=(vmem(),) * ((cut + 1) * len(groups) + 1),
         scratch_shapes=[pltpu.VMEM((total, depth), bf16), pltpu.VMEM((total, hidden), bf16)],
         compiler_params=params(12),
         cost_estimate=pl.CostEstimate(
@@ -462,15 +455,18 @@
     )(*pieces, *weights, turn)
 
 
-def run_add(*parts):
-    return pl.pallas_call(
-        add_up,
-        out_shape=jax.ShapeDtypeStruct(parts[0].shape, bf16),
-        in_specs=[vmem()] * len(parts),
+def run_add(*parts, dtype=bf16, bytes_accessed=MIB):
+    parts = [p if isinstance(p, list) else [p] for p in parts]
+    flat = [piece for p in parts for piece in p]
+    return pl.pallas_call(
+        functools.partial(add_up, pieces=tuple(len(p) for p in parts)),
+        out_shape=jax.ShapeDtypeStruct((sum(p.shape[0] for p in parts[0]), *flat[0].shape[1:]), dtype),
+        in_specs=[vmem()] * len(flat),
         out_specs=vmem(),
         compiler_params=params(8),
+        cost_estimate=pl.CostEstimate(flops=0, bytes_accessed=bytes_accessed, transcendentals=0),
         name="add_up",
-    )(*parts)
+    )(*flat)
 
 
 def run_combine(recv, ids, weights, res):
@@ -492,7 +488,7 @@
     tokens = slab_len * prompts
     share = hidden_in.shape[2]
     chips = lax.axis_size("y")
-    exp = ("x", "z")
+    ctx, exp = ("y", "core"), ("x", "z")
     experts = lax.axis_size(exp) * w_gate.shape[0]
     slots = 4 * tokens // experts
     turns = slab_len // SUBS
@@ -503,24 +499,19 @@
     def ring(value, d):
         return lax.ppermute(value, "y", [(i, (i + d) % chips) for i in range(chips)])
 
-    proj = lax.all_gather(out_proj, ("y", "core"))
+    proj = [lax.all_gather(p, ctx) for p in jnp.split(out_proj, 2, axis=0)]
     sig = mixer_input.reshape(tokens, channels)
     step = step_size.reshape(tokens, channels)
     into = scan_tables(state_in, turns)
     end, before, pre = run_first(step, sig, into, decay_rate, prompts)
-    core = lax.axis_index("core").astype(jnp.int32).reshape(1)
-    sib = swap(end)
-    pair = run_pair(core, end, sib, decay_rate)
-    pairs = [
-        lax.ppermute(pair, "y", [(i, i + d) for i in range(chips - d)]) for d in range(chips - 1, 0, -1)
-    ]
+    ends = lax.all_gather(end, ctx)
+    coords = jnp.stack([lax.axis_index(a).astype(jnp.int32) for a in (ctx, "x", "z")])
     gate = gate_in.reshape(tokens, channels)
     outof = scan_tables(state_out, turns)
     mixed = run_second(
-        core, step, sig, gate, into, outof, decay_rate, skip.reshape(1, channels), before, pre, sib, pairs
+        coords, step, sig, gate, into, outof, decay_rate, skip.reshape(1, channels), before, pre, ends
     )
     sides = (lax.axis_size("x"), lax.axis_size("z"))
-    coords = jnp.stack([lax.axis_index(a).astype(jnp.int32) for a in ("core", "x", "z")])
 
     def shift(value, axis, d):
         n = lax.axis_size(axis)
@@ -528,12 +519,9 @@
 
     nx, nz = sides
     ids = route_ids.reshape(tokens, -1)
-    *parts, by_choice, turn = run_project(coords, mixed, ids.T, proj, share, sides)
+    *parts, by_choice = run_project(coords, mixed, ids.T, proj, share, sides)
     hidden = hidden_in.reshape(tokens, share)
-    hidden, ids, turn = lax.optimization_barrier((hidden, ids, turn))
-    *weights, turn = run_load(turn, w_gate[0], w_up[0], w_down[0])
     parts = [shift(p, "z", d) for d, p in enumerate(parts[:nz])] + [shift(p, "x", d) for d, p in enumerate(parts[nz:])]
-    *parts, turn = lax.optimization_barrier((*parts, turn))
     parts = run_fold(coords, parts, sides)
     parts = [shift(p, "x", d) for d, p in enumerate(parts[:nx])] + [shift(p, "z", d) for d, p in enumerate(parts[nx:])]
     residual, slot_rows = run_dispatch(parts, hidden, by_choice, experts, slots, sides)
@@ -544,20 +532,26 @@
     own_sib = swap(own)
     low = ring(own, 1)
     high = ring(own, -1)
+    *weights, turn = run_load(own, w_gate[0], w_up[0], w_down[0])
+    own_sib, turn = lax.optimization_barrier((own_sib, turn))
     mine0, other0, turn = run_ffn([([own], [own_sib])], weights, turn, share)
     low, high, turn = lax.optimization_barrier((low, high, turn))
     from0 = swap(other0)
     far_low, far_high = ring(low[:half], 1), ring(high[half:], -1)
     low_sib, high_sib = swap(low), swap(high)
+    low_sib, from0 = lax.optimization_barrier((low_sib, from0))
     mine1, other1, mine3, other3, turn = run_ffn([([low], [low_sib]), ([high], [high_sib])], weights, turn, share)
     far_low, far_high, turn, other1, other3 = lax.optimization_barrier((far_low, far_high, turn, other1, other3))
-    mine2, other2, turn = run_ffn(
-        [([far_low, far_high], [swap(far_low), swap(far_high)])], weights, turn, share
+    far_low_sib, far_high_sib = swap(far_low), swap(far_high)
+    low_sum, high_sum = run_add(mine1, swap(other1)), run_add(mine3, swap(other3))
+    low_sum, high_sum, turn = lax.optimization_barrier((low_sum, high_sum, turn))
+    back1, back3 = ring(low_sum, -1), ring(high_sum, 1)
+    mine2, *other2, turn = run_ffn(
+        [([far_low, far_high], [far_low_sib, far_high_sib])], weights, turn, share, cut=CUT
     )
-    back1 = ring(run_add(mine1, swap(other1)), -1)
-    back3 = ring(run_add(mine3, swap(other3)), 1)
-    back2 = ring(run_add(mine2, swap(other2)), 2)
-    returned = run_add(mine0, from0, back1, back3, back2)
+    back2 = ring(run_add(mine2, [swap(p) for p in other2]), 2)
+    near = run_add(mine0, from0, back1, back3, dtype=f32, bytes_accessed=64 * MIB)
+    returned = run_add(near, back2)
 
     back = lax.all_to_all(returned, exp, 0, 0, tiled=True)
     out = run_combine(back, ids, route_weight.reshape(tokens, -1), residual)

time: 192 us -> 210 us (1.094)
  waiting for transfers between devices: 53.7 us -> 71.2 us
  starting transfers between devices: 52.1 us -> 37.6 us
  blocking collectives: 16.9 us -> 29.5 us
  Pallas kernels: 43.8 us -> 46 us
    all_gather x1 -> x2, waiting for transfers between devices: 0.05 us -> 19.4 us  [on_device(): proj = [lax.all_gather(p, ctx) for p in jnp.split(out_proj, 2, axis=0)]]
    all_gather x0 -> x1, blocking collectives: none -> 15.5 us  [on_device(): ends = lax.all_gather(end, ctx)]
    ppermute x12, waiting for transfers between devices: 2.02 us -> 12.4 us  [shift(): lax.ppermute(value, axis, [(i, (i + d) % n) for i in range(n)])]
    ppermute x3 -> x0, starting transfers between devices: 9.07 us -> none  [on_device(): lax.ppermute(pair, 'y', [(i, i + d) for i in range(chips - d)])]
    ppermute x7, waiting for transfers between devices: 33.2 us -> 25.6 us  [ring(): lax.ppermute(value, 'y', [(i, (i + d) % chips) for i in range(chips)])]
    ppermute x3 -> x0, waiting for transfers between devices: 6.11 us -> none  [on_device(): lax.ppermute(pair, 'y', [(i, i + d) for i in range(chips - d)])]
    ppermute x12, starting transfers between devices: 26.3 us -> 21.1 us  [shift(): lax.ppermute(value, axis, [(i, (i + d) % n) for i in range(n)])]
    all_to_all x1, blocking collectives: 16.9 us -> 14 us  [on_device(): whole = lax.all_to_all(slot_rows, exp, 0, 0, tiled=True)]
  transfers between devices with their start and end apart: 34 -> 31, of which waited for: 11 -> 14; matrix products, arithmetic and copies ran while one was open for 4% -> 3% of each run, Pallas kernels for 19% -> 15%
where the time goes in v3:
time: 210 us; the launch traced here: 209 us
  waiting for transfers between devices  71.2 us (34%)
  Pallas kernels  46 us (22%)
  starting transfers between devices  37.6 us (18%)
  blocking collectives  29.5 us (14%)
  between operations  13.6 us (6%)
  local copies, waits for them, and re-layouts  11.3 us (5%)
    ppermute x7, waiting for transfers between devices, ring(): lax.ppermute(value, 'y', [(i, (i + d) % chips) for i in range(chips)])  25.6 us
    ppermute x12, starting transfers between devices, shift(): lax.ppermute(value, axis, [(i, (i + d) % n) for i in range(n)])  21.1 us
    all_gather x2, waiting for transfers between devices, on_device(): proj = [lax.all_gather(p, ctx) for p in jnp.split(out_proj, 2, axis=0)]  19.4 us
    all_gather x1, blocking collectives, on_device(): ends = lax.all_gather(end, ctx)  15.5 us
    pallas_call x3, Pallas kernels, run_ffn(): pl.pallas_call(functools.partial(feed_forward, groups=tuple(((len(own), l...  15.2 us
    all_to_all x1, blocking collectives, on_device(): whole = lax.all_to_all(slot_rows, exp, 0, 0, tiled=True)  14 us
    ppermute x12, waiting for transfers between devices, shift(): lax.ppermute(value, axis, [(i, (i + d) % n) for i in range(n)])  12.4 us
    all_to_all x1, waiting for transfers between devices, on_device(): back = lax.all_to_all(returned, exp, 0, 0, tiled=True)  11 us
  transfers between devices with their start and end apart: 31, of which 14 were waited for; matrix products, arithmetic and copies ran while one was open for 3% of the time, Pallas kernels for 15%

profile of v3, /device:TPU:0, one launch (start us, length us, event | category | flops | bytes accessed | tf_op | source)
XLA Modules:
  0.0 209.4 jit_solution(12771983408924947741)
XLA Ops:
  16.3 6.1 %scan_first.1 = (f32[2,17,512]{2,1,0:T(8,128)S(1)}, f32[2,16,8,512]{3,2,1,0:T(8,128)S(1)}, f32[2,8,512]{2,1,0:T(8,128)S(1)}) custom-call(f32[256,512]{1,0:T(8,128)S(1)} %reshape.33.step_ref, bf16[256,512]{1,0:T(8,128)(2,1)S(1)} %reshape.34.sig_ref, f32[16,8,32]{2,1,0:T(8,128)S(1)} %bitcast.25, f32[16,512]{1,0:T(8,128)S(1)} %copy-done), custom_call_target="tpu_custom_call" | custom-call | tf_op jit(solution)/shard_map/scan_first/pallas_call | solution.py:320
  22.5 15.5 %all-gather = f32[16,17,512]{2,1,0:T(8,128)S(1)} all-gather(f32[2,17,512]{2,1,0:T(8,128)S(1)} %get-tuple-element.58), channel_id=2, replica_groups=mesh['y'=4,'core'=2,'x'=4,'z'=4] {'y','core'}, dimensions={0}, use_global_device_ids=true | all-gather | bytes 626688 | tf_op jit(solution)/shard_map/all_gather | solution.py:507
  39.4 7.2 %scan_second.1.mixed_ref = bf16[256,512]{1,0:T(8,128)(2,1)S(1)} custom-call(s32[3]{0:T(128)S(1)} %pad_add_fusion.coords_ref, f32[256,512]{1,0:T(8,128)S(1)} %reshape.33.step_ref, bf16[256,512]{1,0:T(8,128)(2,1)S(1)} %reshape.34.sig_ref, bf16[256,512]{1,0:T(8,128)(2,1)S(1)} %reshape.35.gate_ref, f32[16,8,32]{2,1,0:T(8,128)S(1)} %bitcast.26, ...), custom_call_target="tpu_custom_call" | custom-call | flops 2000000000 | bytes 2097152 | tf_op jit(solution)/shard_map/scan_second/pallas_call | solution.py:344
  46.6 19.4 %all-gather.8.cloned.1.call-done = bf16[2048,512]{1,0:T(8,128)(2,1)} async-done(((bf16[256,512]{1,0:T(8,128)(2,1)}), bf16[2048,512]{1,0:T(8,128)(2,1)}) %all-gather.8.cloned.1.call-update) | async-done | bytes 2097168 | tf_op jit(solution)/shard_map/all_gather | solution.py:502
  66.0 6.4 %project.1 = (bf16[4,128,256]{2,1,0:T(8,128)(2,1)S(1)}, bf16[4,128,256]{2,1,0:T(8,128)(2,1)S(1)}, bf16[4,128,256]{2,1,0:T(8,128)(2,1)S(1)}, bf16[4,128,256]{2,1,...) custom-call(s32[3]{0:T(128)S(1)} %pad_add_fusion.coords_ref, ...), custom_call_target="tpu_custom_call" | custom-call | tf_op jit(solution)/shard_map/project/pallas_call | solution.py:366
  74.0 2.9 %collective-permute-start.1 = (bf16[4,128,256]{2,1,0:T(8,128)(2,1)S(1)}, bf16[4,128,256]{2,1,0:T(8,128)(2,1)S(1)}, u32[]{:S(2)}, u32[]{:S(2)}) collective-permute-start(bf16[4,128,256]{2,1,0:T(8,128)(2,1)S(1)} %get-tuple-element.61), channel_id=1, source_target_pairs={{0,2},{1,3},{2,0},{3,1},{4,6},{5,7},{6,4},{7,5},{8,10},{9,11},{10,... | collective-permute-start | bytes 786440 | tf_op jit(solution)/shard_map/ppermute | solution.py:518
  79.7 2.7 %collective-permute-start.4 = (bf16[4,128,256]{2,1,0:T(8,128)(2,1)S(1)}, bf16[4,128,256]{2,1,0:T(8,128)(2,1)S(1)}, u32[]{:S(2)}, u32[]{:S(2)}) collective-permute-start(bf16[4,128,256]{2,1,0:T(8,128)(2,1)S(1)} %get-tuple-element.65), channel_id=1, source_target_pairs={{0,8},{4,12},{8,0},{12,4},{1,9},{5,13},{9,1},{13,5},{2,10},{6,14},... | collective-permute-start | bytes 786440 | tf_op jit(solution)/shard_map/ppermute | solution.py:518
  82.4 2.4 %collective-permute-start.5 = (bf16[4,128,256]{2,1,0:T(8,128)(2,1)S(1)}, bf16[4,128,256]{2,1,0:T(8,128)(2,1)S(1)}, u32[]{:S(2)}, u32[]{:S(2)}) collective-permute-start(bf16[4,128,256]{2,1,0:T(8,128)(2,1)S(1)} %get-tuple-element.66), channel_id=1, source_target_pairs={{0,12},{4,0},{8,4},{12,8},{1,13},{5,1},{9,5},{13,9},{2,14},{6,2},{... | collective-permute-start | bytes 786440 | tf_op jit(solution)/shard_map/ppermute | solution.py:518
  84.8 4.1 %collective-permute-done.1.rest_2_ = bf16[4,128,256]{2,1,0:T(8,128)(2,1)S(1)} collective-permute-done((bf16[4,128,256]{2,1,0:T(8,128)(2,1)S(1)}, bf16[4,128,256]{2,1,0:T(8,128)(2,1)S(1)}, u32[]{:S(2)}, u32[]{:S(2)}) %collective-permute-start.1) | collective-permute-done | bytes 262176 | tf_op jit(solution)/shard_map/ppermute | solution.py:518
  88.9 4.7 %collective-permute-done.4.rest_6_ = bf16[4,128,256]{2,1,0:T(8,128)(2,1)S(1)} collective-permute-done((bf16[4,128,256]{2,1,0:T(8,128)(2,1)S(1)}, bf16[4,128,256]{2,1,0:T(8,128)(2,1)S(1)}, u32[]{:S(2)}, u32[]{:S(2)}) %collective-permute-start.4) | collective-permute-done | bytes 262176 | tf_op jit(solution)/shard_map/ppermute | solution.py:518
  94.4 2.1 %collective-permute-start.6 = (bf16[128,256]{1,0:T(8,128)(2,1)S(1)}, bf16[128,256]{1,0:T(8,128)(2,1)S(1)}, u32[]{:S(2)}, u32[]{:S(2)}) collective-permute-start(bf16[128,256]{1,0:T(8,128)(2,1)S(1)} %get-tuple-element.68), channel_id=1, source_target_pairs={{0,4},{4,8},{8,12},{12,0},{1,5},{5,9},{9,13},{13,1},{2,6},{6,10},{... | collective-permute-start | bytes 196616 | tf_op jit(solution)/shard_map/ppermute | solution.py:518
  103.2 2.1 collective-permute-done.9.refs_5_
  107.3 14.0 %all_to_all.10.recv_ref = bf16[16,64,256]{2,1,0:T(8,128)(2,1)S(1)} all-to-all(bf16[16,64,256]{2,1,0:T(8,128)(2,1)S(1)} %get-tuple-element.76), channel_id=1, replica_groups=mesh['y'=4,'core'=2,'x'=4,'z'=4] {'x','z'}, dimensions={0} | all-to-all | bytes 1048576 | tf_op jit(solution)/shard_map/all_to_all | solution.py:528
  122.3 2.7 %collective-permute-start.14 = (bf16[64,4096]{1,0:T(8,128)(2,1)S(1)}, bf16[64,4096]{1,0:T(8,128)(2,1)S(1)}, u32[]{:S(2)}, u32[]{:S(2)}) collective-permute-start(bf16[64,4096]{1,0:T(8,128)(2,1)S(1)} %normalize.1.after_ref.refs_0_), channel_id=1, source_target_pairs={{0,96},{32,0},{64,32},{96,64},{1,97},{33,1},{65,33},{97,65},{2,98}... | collective-permute-start | bytes 1572872 | tf_op jit(solution)/shard_map/ppermute | solution.py:500
  125.0 7.3 %load_weights.1 = (bf16[4096,896]{1,0:T(8,128)(2,1)S(1)}, bf16[4096,896]{1,0:T(8,128)(2,1)S(1)}, bf16[896,4096]{1,0:T(8,128)(2,1)S(1)}, f32[8,128]{1,0:T(8,128)S(1)}) custom-call(bf16[64,4096]{1,0:T(8,128)(2,1)S(1)} %normalize.1.after_ref.refs_0_, bf16[4096,896]{1,0:T(8,128)(2,1)} %bitcast.30, bf16[4096,896]{1,0:T(8,128)(2,1)} %bitcast.31, ...), custom_call_target="tpu_custom_call" | custom-call | bytes 44040192 | tf_op jit(solution)/shard_map/load_weights/pallas_call | solution.py:424
  132.3 3.8 %feed_forward.3 = (bf16[16,64,256]{2,1,0:T(8,128)(2,1)S(1)}, bf16[16,64,256]{2,1,0:T(8,128)(2,1)S(1)}, f32[8,128]{1,0:T(8,128)S(1)}) custom-call(bf16[64,4096]{1,0:T(8,128)(2,1)S(1)} %normalize.1.after_ref.refs_0_, bf16[64,4096]{1,0:T(8,128)(2,1)S(1)} %collective-permute-done.12.refs_1_, bf16[4096,896]{1,0:T(8,128)(2,1)S(1)} %get-tuple-element.79.refs_2_.refs_4_, ...), custom_call_target="tpu_custom_call" | custom-call | flops 2818572288 | bytes 2097152 | tf_op jit(solution)/shard_map/feed_forward/pallas_call | solution.py:444
  138.3 2.8 %collective-permute-start.19 = (bf16[32,4096]{1,0:T(8,128)(2,1)S(1)}, bf16[32,4096]{1,0:T(8,128)(2,1)S(1)}, u32[]{:S(2)}, u32[]{:S(2)}) collective-permute-start(bf16[32,4096]{1,0:T(8,128)(2,1)S(1)} %slice.7), channel_id=1, source_target_pairs={{0,96},{32,0},{64,32},{96,64},{1,97},{33,1},{65,33},{97,65},{2,98}... | collective-permute-start | bytes 786440 | tf_op jit(solution)/shard_map/ppermute | solution.py:500
  141.1 7.2 %feed_forward.4 = (bf16[16,64,256]{2,1,0:T(8,128)(2,1)S(1)}, bf16[16,64,256]{2,1,0:T(8,128)(2,1)S(1)}, bf16[16,64,256]{2,1,0:T(8,128)(2,1)S(1)}, bf16[16,64,256]{2,1,0:T(8,128)(2,1)S(1)}, f32[8,128]{1,0:T(8,128)S(1)}) custom-call(bf16[64,4096]{1,0:T(8,128)(2,1)S(1)} %collective-permute-done.13.refs_0_, bf16[64,4096]{1,0:T(8,128)(2,1)S(1)} %collective-permute-done.15.refs_1_, ...), custom_call_target="tpu_custom_call" | custom-call | flops 5637144576 | bytes 4194304 | tf_op jit(solution)/shard_map/feed_forward/pallas_call | solution.py:444
  151.8 4.2 %feed_forward.5 = (bf16[16,64,256]{2,1,0:T(8,128)(2,1)S(1)}, bf16[16,64,256]{2,1,0:T(8,128)(2,1)S(1)}, f32[8,128]{1,0:T(8,128)}) custom-call(bf16[32,4096]{1,0:T(8,128)(2,1)S(1)} %collective-permute-done.18.refs_0_, bf16[32,4096]{1,0:T(8,128)(2,1)S(1)} %collective-permute-done.19.refs_1_, bf16[32,4096]{1,0:T(8,128)(2,1)S(1)} %collective-permute-done.24.refs_2_, ...), custom_call_target="tpu_custom_call" | custom-call | flops 2818572288 | bytes 2097152 | tf_op jit(solution)/shard_map/feed_forward/pallas_call | solution.py:444
  156.3 2.6 %collective-permute-start.22 = (bf16[16,64,256]{2,1,0:T(8,128)(2,1)S(1)}, bf16[16,64,256]{2,1,0:T(8,128)(2,1)S(1)}, u32[]{:S(2)}, u32[]{:S(2)}) collective-permute-start(bf16[16,64,256]{2,1,0:T(8,128)(2,1)S(1)} %add_up.5), channel_id=1, source_target_pairs={{0,96},{32,0},{64,32},{96,64},{1,97},{33,1},{65,33},{97,65},{2,98}... | collective-permute-start | bytes 1572872 | tf_op jit(solution)/shard_map/ppermute | solution.py:500
  160.8 21.1 %collective-permute-done.22.refs_2_ = bf16[16,64,256]{2,1,0:T(8,128)(2,1)S(1)} collective-permute-done((bf16[16,64,256]{2,1,0:T(8,128)(2,1)S(1)}, bf16[16,64,256]{2,1,0:T(8,128)(2,1)S(1)}, u32[]{:S(2)}, u32[]{:S(2)}) %collective-permute-start.22) | collective-permute-done | bytes 524320 | tf_op jit(solution)/shard_map/ppermute | solution.py:500
  181.8 3.4 %collective-permute-done.23.refs_3_ = bf16[16,64,256]{2,1,0:T(8,128)(2,1)S(1)} collective-permute-done((bf16[16,64,256]{2,1,0:T(8,128)(2,1)S(1)}, bf16[16,64,256]{2,1,0:T(8,128)(2,1)S(1)}, u32[]{:S(2)}, u32[]{:S(2)}) %collective-permute-start.23) | collective-permute-done | bytes 524320 | tf_op jit(solution)/shard_map/ppermute | solution.py:500
  186.4 3.6 %all-to-all-start.1 = ((bf16[16,64,256]{2,1,0:T(8,128)(2,1)}), bf16[16,64,256]{2,1,0:T(8,128)(2,1)S(1)}, u32[]{:S(2)}, u32[]{:S(2)}) async-start(bf16[16,64,256]{2,1,0:T(8,128)(2,1)} %add_up.9), calls=%async_computation.1 | async-start | bytes 1048576 | tf_op jit(solution)/shard_map/all_to_all | solution.py:556
  190.1 11.0 %all-to-all-done.1.recv_ref = bf16[16,64,256]{2,1,0:T(8,128)(2,1)S(1)} async-done(((bf16[16,64,256]{2,1,0:T(8,128)(2,1)}), bf16[16,64,256]{2,1,0:T(8,128)(2,1)S(1)}, u32[]{:S(2)}, u32[]{:S(2)}) %all-to-all-start.1) | async-done | bytes 524320 | tf_op jit(solution)/shard_map/all_to_all | solution.py:556
  (86 shorter events, 36.7 us)
Async XLA Ops:
  6.5 40.1 %all-gather.6.cloned.1.call-start = ((), (), s32[]{:S(2)}) async-start(), calls=%async_computation.2 | async-start | bytes 2359296 | tf_op jit(solution)/shard_map/all_gather | solution.py:502
  8.4 57.6 %all-gather.8.cloned.1.call-start = ((), (), s32[]{:S(2)}) async-start(), calls=%async_computation.3 | async-start | bytes 2359296 | tf_op jit(solution)/shard_map/all_gather | solution.py:502
  72.4 10.0 %collective-permute-start = (bf16[4,128,256]{2,1,0:T(8,128)(2,1)S(1)}, bf16[4,128,256]{2,1,0:T(8,128)(2,1)S(1)}, u32[]{:S(2)}, u32[]{:S(2)}) collective-permute-start(bf16[4,128,256]{2,1,0:T(8,128)(2,1)S(1)} %get-tuple-element.60), channel_id=1, source_target_pairs={{0,1},{1,2},{2,3},{3,0},{4,5},{5,6},{6,7},{7,4},{8,9},{9,10},{10,1... | collective-permute-start | bytes 786440 | tf_op jit(solution)/shard_map/ppermute | solution.py:518
  74.0 14.9 %collective-permute-start.1 = (bf16[4,128,256]{2,1,0:T(8,128)(2,1)S(1)}, bf16[4,128,256]{2,1,0:T(8,128)(2,1)S(1)}, u32[]{:S(2)}, u32[]{:S(2)}) collective-permute-start(bf16[4,128,256]{2,1,0:T(8,128)(2,1)S(1)} %get-tuple-element.61), channel_id=1, source_target_pairs={{0,2},{1,3},{2,0},{3,1},{4,6},{5,7},{6,4},{7,5},{8,10},{9,11},{10,... | collective-permute-start | bytes 786440 | tf_op jit(solution)/shard_map/ppermute | solution.py:518
  76.9 12.1 %collective-permute-start.2 = (bf16[4,128,256]{2,1,0:T(8,128)(2,1)S(1)}, bf16[4,128,256]{2,1,0:T(8,128)(2,1)S(1)}, u32[]{:S(2)}, u32[]{:S(2)}) collective-permute-start(bf16[4,128,256]{2,1,0:T(8,128)(2,1)S(1)} %get-tuple-element.62), channel_id=1, source_target_pairs={{0,3},{1,0},{2,1},{3,2},{4,7},{5,4},{6,5},{7,6},{8,11},{9,8},{10,9... | collective-permute-start | bytes 786440 | tf_op jit(solution)/shard_map/ppermute | solution.py:518
  78.2 10.7 %collective-permute-start.3 = (bf16[4,128,256]{2,1,0:T(8,128)(2,1)S(1)}, bf16[4,128,256]{2,1,0:T(8,128)(2,1)S(1)}, u32[]{:S(2)}, u32[]{:S(2)}) collective-permute-start(bf16[4,128,256]{2,1,0:T(8,128)(2,1)S(1)} %get-tuple-element.64), channel_id=1, source_target_pairs={{0,4},{4,8},{8,12},{12,0},{1,5},{5,9},{9,13},{13,1},{2,6},{6,10},{... | collective-permute-start | bytes 786440 | tf_op jit(solution)/shard_map/ppermute | solution.py:518
  79.7 13.9 %collective-permute-start.4 = (bf16[4,128,256]{2,1,0:T(8,128)(2,1)S(1)}, bf16[4,128,256]{2,1,0:T(8,128)(2,1)S(1)}, u32[]{:S(2)}, u32[]{:S(2)}) collective-permute-start(bf16[4,128,256]{2,1,0:T(8,128)(2,1)S(1)} %get-tuple-element.65), channel_id=1, source_target_pairs={{0,8},{4,12},{8,0},{12,4},{1,9},{5,13},{9,1},{13,5},{2,10},{6,14},... | collective-permute-start | bytes 786440 | tf_op jit(solution)/shard_map/ppermute | solution.py:518
  82.4 11.2 %collective-permute-start.5 = (bf16[4,128,256]{2,1,0:T(8,128)(2,1)S(1)}, bf16[4,128,256]{2,1,0:T(8,128)(2,1)S(1)}, u32[]{:S(2)}, u32[]{:S(2)}) collective-permute-start(bf16[4,128,256]{2,1,0:T(8,128)(2,1)S(1)} %get-tuple-element.66), channel_id=1, source_target_pairs={{0,12},{4,0},{8,4},{12,8},{1,13},{5,1},{9,5},{13,9},{2,14},{6,2},{... | collective-permute-start | bytes 786440 | tf_op jit(solution)/shard_map/ppermute | solution.py:518
  94.4 7.1 %collective-permute-start.6 = (bf16[128,256]{1,0:T(8,128)(2,1)S(1)}, bf16[128,256]{1,0:T(8,128)(2,1)S(1)}, u32[]{:S(2)}, u32[]{:S(2)}) collective-permute-start(bf16[128,256]{1,0:T(8,128)(2,1)S(1)} %get-tuple-element.68), channel_id=1, source_target_pairs={{0,4},{4,8},{8,12},{12,0},{1,5},{5,9},{9,13},{13,1},{2,6},{6,10},{... | collective-permute-start | bytes 196616 | tf_op jit(solution)/shard_map/ppermute | solution.py:518
  96.5 6.7 %collective-permute-start.7 = (bf16[128,256]{1,0:T(8,128)(2,1)S(1)}, bf16[128,256]{1,0:T(8,128)(2,1)S(1)}, u32[]{:S(2)}, u32[]{:S(2)}) collective-permute-start(bf16[128,256]{1,0:T(8,128)(2,1)S(1)} %get-tuple-element.69), channel_id=1, source_target_pairs={{0,8},{4,12},{8,0},{12,4},{1,9},{5,13},{9,1},{13,5},{2,10},{6,14},... | collective-permute-start | bytes 196616 | tf_op jit(solution)/shard_map/ppermute | solution.py:518
  98.3 4.9 %collective-permute-start.8 = (bf16[128,256]{1,0:T(8,128)(2,1)S(1)}, bf16[128,256]{1,0:T(8,128)(2,1)S(1)}, u32[]{:S(2)}, u32[]{:S(2)}) collective-permute-start(bf16[128,256]{1,0:T(8,128)(2,1)S(1)} %get-tuple-element.70), channel_id=1, source_target_pairs={{0,12},{4,0},{8,4},{12,8},{1,13},{5,1},{9,5},{13,9},{2,14},{6,2},{... | collective-permute-start | bytes 196616 | tf_op jit(solution)/shard_map/ppermute | solution.py:518
  99.8 5.5 %collective-permute-start.9 = (bf16[128,256]{1,0:T(8,128)(2,1)S(1)}, bf16[128,256]{1,0:T(8,128)(2,1)S(1)}, u32[]{:S(2)}, u32[]{:S(2)}) collective-permute-start(bf16[128,256]{1,0:T(8,128)(2,1)S(1)} %get-tuple-element.72), channel_id=1, source_target_pairs={{0,1},{1,2},{2,3},{3,0},{4,5},{5,6},{6,7},{7,4},{8,9},{9,10},{10,1... | collective-permute-start | bytes 196616 | tf_op jit(solution)/shard_map/ppermute | solution.py:518
  100.5 5.8 %collective-permute-start.10 = (bf16[128,256]{1,0:T(8,128)(2,1)S(1)}, bf16[128,256]{1,0:T(8,128)(2,1)S(1)}, u32[]{:S(2)}, u32[]{:S(2)}) collective-permute-start(bf16[128,256]{1,0:T(8,128)(2,1)S(1)} %get-tuple-element.73), channel_id=1, source_target_pairs={{0,2},{1,3},{2,0},{3,1},{4,6},{5,7},{6,4},{7,5},{8,10},{9,11},{10,... | collective-permute-start | bytes 196616 | tf_op jit(solution)/shard_map/ppermute | solution.py:518
  101.5 5.3 %collective-permute-start.11 = (bf16[128,256]{1,0:T(8,128)(2,1)S(1)}, bf16[128,256]{1,0:T(8,128)(2,1)S(1)}, u32[]{:S(2)}, u32[]{:S(2)}) collective-permute-start(bf16[128,256]{1,0:T(8,128)(2,1)S(1)} %get-tuple-element.74), channel_id=1, source_target_pairs={{0,3},{1,0},{2,1},{3,2},{4,7},{5,4},{6,5},{7,6},{8,11},{9,8},{10,9... | collective-permute-start | bytes 196616 | tf_op jit(solution)/shard_map/ppermute | solution.py:518
  121.6 10.7 %collective-permute-start.12 = (bf16[64,4096]{1,0:T(8,128)(2,1)S(1)}, bf16[64,4096]{1,0:T(8,128)(2,1)S(1)}, u32[]{:S(2)}, u32[]{:S(2)}) collective-permute-start(bf16[64,4096]{1,0:T(8,128)(2,1)S(1)} %normalize.1.after_ref.refs_0_), channel_id=1, source_target_pairs={{0,16},{16,0},{1,17},{17,1},{2,18},{18,2},{3,19},{19,3},{4,20},{20... | collective-permute-start | bytes 1572872 | tf_op jit(solution)/shard_map/ppermute | solution.py:497
  121.7 15.6 %collective-permute-start.13 = (bf16[64,4096]{1,0:T(8,128)(2,1)S(1)}, bf16[64,4096]{1,0:T(8,128)(2,1)S(1)}, u32[]{:S(2)}, u32[]{:S(2)}) collective-permute-start(bf16[64,4096]{1,0:T(8,128)(2,1)S(1)} %normalize.1.after_ref.refs_0_), channel_id=1, source_target_pairs={{0,32},{32,64},{64,96},{96,0},{1,33},{33,65},{65,97},{97,1},{2,34}... | collective-permute-start | bytes 1572872 | tf_op jit(solution)/shard_map/ppermute | solution.py:500
  122.3 14.9 %collective-permute-start.14 = (bf16[64,4096]{1,0:T(8,128)(2,1)S(1)}, bf16[64,4096]{1,0:T(8,128)(2,1)S(1)}, u32[]{:S(2)}, u32[]{:S(2)}) collective-permute-start(bf16[64,4096]{1,0:T(8,128)(2,1)S(1)} %normalize.1.after_ref.refs_0_), channel_id=1, source_target_pairs={{0,96},{32,0},{64,32},{96,64},{1,97},{33,1},{65,33},{97,65},{2,98}... | collective-permute-start | bytes 1572872 | tf_op jit(solution)/shard_map/ppermute | solution.py:500
  137.2 3.9 %collective-permute-start.15 = (bf16[64,4096]{1,0:T(8,128)(2,1)S(1)}, bf16[64,4096]{1,0:T(8,128)(2,1)S(1)}, u32[]{:S(2)}, u32[]{:S(2)}) collective-permute-start(bf16[64,4096]{1,0:T(8,128)(2,1)S(1)} %collective-permute-done.13.refs_0_), channel_id=1, source_target_pairs={{0,16},{16,0},{1,17},{17,1},{2,18},{18,2},{3,19},{19,3},{4,20},{20... | collective-permute-start | bytes 1572872 | tf_op jit(solution)/shard_map/ppermute | solution.py:497
  137.8 10.5 %collective-permute-start.18 = (bf16[32,4096]{1,0:T(8,128)(2,1)S(1)}, bf16[32,4096]{1,0:T(8,128)(2,1)S(1)}, u32[]{:S(2)}, u32[]{:S(2)}) collective-permute-start(bf16[32,4096]{1,0:T(8,128)(2,1)S(1)} %slice.6), channel_id=1, source_target_pairs={{0,32},{32,64},{64,96},{96,0},{1,33},{33,65},{65,97},{97,1},{2,34}... | collective-permute-start | bytes 786440 | tf_op jit(solution)/shard_map/ppermute | solution.py:500
  138.3 10.0 %collective-permute-start.19 = (bf16[32,4096]{1,0:T(8,128)(2,1)S(1)}, bf16[32,4096]{1,0:T(8,128)(2,1)S(1)}, u32[]{:S(2)}, u32[]{:S(2)}) collective-permute-start(bf16[32,4096]{1,0:T(8,128)(2,1)S(1)} %slice.7), channel_id=1, source_target_pairs={{0,96},{32,0},{64,32},{96,64},{1,97},{33,1},{65,33},{97,65},{2,98}... | collective-permute-start | bytes 786440 | tf_op jit(solution)/shard_map/ppermute | solution.py:500
  156.3 25.5 %collective-permute-start.22 = (bf16[16,64,256]{2,1,0:T(8,128)(2,1)S(1)}, bf16[16,64,256]{2,1,0:T(8,128)(2,1)S(1)}, u32[]{:S(2)}, u32[]{:S(2)}) collective-permute-start(bf16[16,64,256]{2,1,0:T(8,128)(2,1)S(1)} %add_up.5), channel_id=1, source_target_pairs={{0,96},{32,0},{64,32},{96,64},{1,97},{33,1},{65,33},{97,65},{2,98}... | collective-permute-start | bytes 1572872 | tf_op jit(solution)/shard_map/ppermute | solution.py:500
  158.9 26.4 %collective-permute-start.23 = (bf16[16,64,256]{2,1,0:T(8,128)(2,1)S(1)}, bf16[16,64,256]{2,1,0:T(8,128)(2,1)S(1)}, u32[]{:S(2)}, u32[]{:S(2)}) collective-permute-start(bf16[16,64,256]{2,1,0:T(8,128)(2,1)S(1)} %add_up.6), channel_id=1, source_target_pairs={{0,32},{32,64},{64,96},{96,0},{1,33},{33,65},{65,97},{97,1},{2,34}... | collective-permute-start | bytes 1572872 | tf_op jit(solution)/shard_map/ppermute | solution.py:500
  159.0 26.5 %collective-permute-start.27 = (bf16[16,64,256]{2,1,0:T(8,128)(2,1)S(1)}, bf16[16,64,256]{2,1,0:T(8,128)(2,1)S(1)}, u32[]{:S(2)}, u32[]{:S(2)}) collective-permute-start(bf16[16,64,256]{2,1,0:T(8,128)(2,1)S(1)} %add_up.8), channel_id=1, source_target_pairs={{0,64},{32,96},{64,0},{96,32},{1,65},{33,97},{65,1},{97,33},{2,66}... | collective-permute-start | bytes 1572872 | tf_op jit(solution)/shard_map/ppermute | solution.py:500
  186.4 14.7 %all-to-all-start.1 = ((bf16[16,64,256]{2,1,0:T(8,128)(2,1)}), bf16[16,64,256]{2,1,0:T(8,128)(2,1)S(1)}, u32[]{:S(2)}, u32[]{:S(2)}) async-start(bf16[16,64,256]{2,1,0:T(8,128)(2,1)} %add_up.9), calls=%async_computation.1 | async-start | bytes 1048576 | tf_op jit(solution)/shard_map/all_to_all | solution.py:556
  (13 other events, 218.4 us)
Sparse Core Ops, SparseCore 0:
  9.1 28.8 all-gather.5
  39.7 26.2 all-gather.7

commit v4 on v3

--- a/solution.py
+++ b/solution.py
@@ -144,39 +144,27 @@
         mixed_ref[:, lanes] = (y * (gate / (1.0 + jnp.exp(-gate)))).astype(bf16)
 
 
-def project(coords_ref, mixed_ref, ids_ref, *refs, sides, halves):
+def project(coords_ref, mixed_ref, ids_ref, proj_hbm, *rest, sides):
     nx, nz = sides
-    sources, rest = refs[:halves], refs[halves:]
     z_refs, x_refs = rest[:nz], rest[nz : nz + nx]
-    ids_out, proj, sem = rest[nz + nx :]
+    ids_out, whole, proj, sem = rest[nz + nx :]
     _, half, width = z_refs[0].shape
-    _, depth, _ = proj.shape
-    per = sources[0].shape[2] // width
-    piece = depth // halves
+    blocks, _, columns = proj.shape
+    for c in range(blocks):
+        pltpu.make_async_copy(proj_hbm.at[c], proj.at[c], sem.at[c]).start()
+    for c in range(blocks):
+        pltpu.make_async_copy(proj_hbm.at[c], proj.at[c], sem.at[c]).wait()
+        part = jnp.dot(mixed_ref[...], proj[c], preferred_element_type=f32).astype(bf16)
+        for i in range(columns // width):
+            whole[c * (columns // width) + i] = part[:, i * width : (i + 1) * width]
     x, z = coords_ref[1], coords_ref[2]
-    hops = [(dx, dz) for dx in range(nx) for dz in range(nz)]
-    copies = []
-    for r, (dx, dz) in enumerate(hops):
-        to_x, to_z = lax.rem(x + dx, nx), lax.rem(z + dz, nz)
-        block = to_x * nz + to_z
-        columns = pl.ds(pl.multiple_of(lax.rem(block, per) * width, width), width)
-        copies.append(
-            [
-                pltpu.make_async_copy(
-                    source.at[block // per, :, columns], proj.at[r, i * piece : (i + 1) * piece], sem.at[r, i]
-                )
-                for i, source in enumerate(sources)
-            ]
-        )
-        for c in copies[-1]:
-            c.start()
+    for d, out in enumerate(z_refs):
+        for i in range(nx):
+            out[i] = whole[i * nz + lax.rem(z + d, nz), :half]
+    for d, out in enumerate(x_refs):
+        for i in range(nz):
+            out[i] = whole[lax.rem(x + d, nx) * nz + i, half:]
     ids_out[...] = ids_ref[...]
-    for r, (dx, dz) in enumerate(hops):
-        for c in copies[r]:
-            c.wait()
-        part = jnp.dot(mixed_ref[...], proj[r], preferred_element_type=f32).astype(bf16)
-        z_refs[dz][lax.rem(x + dx, nx)] = part[:half]
-        x_refs[dx][lax.rem(z + dz, nz)] = part[half:]
 
 
 def fold(coords_ref, *rest, sides):
@@ -361,22 +349,24 @@
 
 
 def run_project(coords, mixed, ids, proj, share, sides):
-    tokens, depth = mixed.shape
+    tokens = mixed.shape[0]
     nx, nz = sides
-    return pl.pallas_call(
-        functools.partial(project, sides=sides, halves=len(proj)),
+    blocks = proj.shape[0] * proj.shape[2] // share
+    return pl.pallas_call(
+        functools.partial(project, sides=sides),
         out_shape=[jax.ShapeDtypeStruct((nx, tokens // 2, share), bf16)] * nz
         + [jax.ShapeDtypeStruct((nz, tokens // 2, share), bf16)] * nx
         + [jax.ShapeDtypeStruct(ids.shape, ids.dtype)],
-        in_specs=[smem(), vmem(), vmem()] + [anywhere()] * len(proj),
+        in_specs=[smem(), vmem(), vmem(), anywhere()],
         out_specs=[vmem()] * (nx + nz + 1),
         scratch_shapes=[
-            pltpu.VMEM((nx * nz, depth, share), bf16),
-            pltpu.SemaphoreType.DMA((nx * nz, len(proj))),
+            pltpu.VMEM((blocks, tokens, share), bf16),
+            pltpu.VMEM(proj.shape, bf16),
+            pltpu.SemaphoreType.DMA((proj.shape[0],)),
         ],
         compiler_params=params(16),
         name="project",
-    )(coords, mixed, ids, *[pltpu.with_memory_space_constraint(p, pltpu.HBM) for p in proj])
+    )(coords, mixed, ids, pltpu.with_memory_space_constraint(proj, pltpu.HBM))
 
 
 def run_fold(coords, parts, sides):
@@ -499,7 +489,7 @@
     def ring(value, d):
         return lax.ppermute(value, "y", [(i, (i + d) % chips) for i in range(chips)])
 
-    proj = [lax.all_gather(p, ctx) for p in jnp.split(out_proj, 2, axis=0)]
+    proj = lax.all_gather(out_proj, ctx)
     sig = mixer_input.reshape(tokens, channels)
     step = step_size.reshape(tokens, channels)
     into = scan_tables(state_in, turns)

time: 210 us -> 190 us (0.905)
  waiting for transfers between devices: 71.2 us -> 54.2 us
  Pallas kernels: 46 us -> 43.7 us
    all_gather x2 -> x1, waiting for transfers between devices: 19.4 us -> 2.11 us  [on_device(): proj = lax.all_gather(out_proj, ctx)]
    pallas_call x1, Pallas kernels: 6.4 us -> 4.18 us  [run_project(): pl.pallas_call(functools.partial(project, sides=sides), out_shape=[jax.Sh...]
  transfers between devices with their start and end apart: 31 -> 30, of which waited for: 14 -> 15; matrix products, arithmetic and copies ran while one was open for 3% -> 3% of each run, Pallas kernels for 15% -> 17%
where the time goes in v4:
time: 190 us; the launch traced here: 189 us
  waiting for transfers between devices  54.2 us (29%)
  Pallas kernels  43.7 us (23%)
  starting transfers between devices  38.4 us (20%)
  blocking collectives  29.6 us (16%)
  between operations  13.6 us (7%)
  local copies, waits for them, and re-layouts  9.45 us (5%)
    ppermute x7, waiting for transfers between devices, ring(): lax.ppermute(value, 'y', [(i, (i + d) % chips) for i in range(chips)])  25.9 us
    ppermute x12, starting transfers between devices, shift(): lax.ppermute(value, axis, [(i, (i + d) % n) for i in range(n)])  21.1 us
    all_gather x1, blocking collectives, on_device(): ends = lax.all_gather(end, ctx)  15.6 us
    pallas_call x3, Pallas kernels, run_ffn(): pl.pallas_call(functools.partial(feed_forward, groups=tuple(((len(own), l...  15.2 us
    all_to_all x1, blocking collectives, on_device(): whole = lax.all_to_all(slot_rows, exp, 0, 0, tiled=True)  14.1 us
    ppermute x12, waiting for transfers between devices, shift(): lax.ppermute(value, axis, [(i, (i + d) % n) for i in range(n)])  12.4 us
    ppermute x7, starting transfers between devices, ring(): lax.ppermute(value, 'y', [(i, (i + d) % chips) for i in range(chips)])  11.8 us
    all_to_all x1, waiting for transfers between devices, on_device(): back = lax.all_to_all(returned, exp, 0, 0, tiled=True)  11 us
  transfers between devices with their start and end apart: 30, of which 15 were waited for; matrix products, arithmetic and copies ran while one was open for 3% of the time, Pallas kernels for 17%

profile of v4, /device:TPU:0, one launch (start us, length us, event | category | flops | bytes accessed | tf_op | source)
XLA Modules:
  0.0 189.1 jit_solution(5647382481149719736)
XLA Ops:
  14.3 6.1 %scan_first.1 = (f32[2,17,512]{2,1,0:T(8,128)S(1)}, f32[2,16,8,512]{3,2,1,0:T(8,128)S(1)}, f32[2,8,512]{2,1,0:T(8,128)S(1)}) custom-call(f32[256,512]{1,0:T(8,128)S(1)} %reshape.33.step_ref, bf16[256,512]{1,0:T(8,128)(2,1)S(1)} %reshape.34.sig_ref, f32[16,8,32]{2,1,0:T(8,128)S(1)} %bitcast.24, f32[16,512]{1,0:T(8,128)S(1)} %copy-done), custom_call_target="tpu_custom_call" | custom-call | tf_op jit(solution)/shard_map/scan_first/pallas_call | solution.py:308
  20.6 15.6 %all-gather = f32[16,17,512]{2,1,0:T(8,128)S(1)} all-gather(f32[2,17,512]{2,1,0:T(8,128)S(1)} %get-tuple-element.58), channel_id=2, replica_groups=mesh['y'=4,'core'=2,'x'=4,'z'=4] {'y','core'}, dimensions={0}, use_global_device_ids=true | all-gather | bytes 626688 | tf_op jit(solution)/shard_map/all_gather | solution.py:497
  37.6 7.2 %scan_second.1.mixed_ref = bf16[256,512]{1,0:T(8,128)(2,1)S(1)} custom-call(s32[3]{0:T(128)S(1)} %pad_add_fusion.coords_ref, f32[256,512]{1,0:T(8,128)S(1)} %reshape.33.step_ref, bf16[256,512]{1,0:T(8,128)(2,1)S(1)} %reshape.34.sig_ref, bf16[256,512]{1,0:T(8,128)(2,1)S(1)} %reshape.35.gate_ref, f32[16,8,32]{2,1,0:T(8,128)S(1)} %bitcast.25, ...), custom_call_target="tpu_custom_call" | custom-call | flops 2000000000 | bytes 2097152 | tf_op jit(solution)/shard_map/scan_second/pallas_call | solution.py:332
  44.8 2.1 %all-gather.4.cloned.1.call-done = bf16[4096,512]{1,0:T(8,128)(2,1)} async-done(((bf16[512,512]{1,0:T(8,128)(2,1)}), bf16[4096,512]{1,0:T(8,128)(2,1)}) %all-gather.4.cloned.1.call-update) | async-done | bytes 4194320 | tf_op jit(solution)/shard_map/all_gather | solution.py:492
  46.9 4.2 %project.1 = (bf16[4,128,256]{2,1,0:T(8,128)(2,1)S(1)}, bf16[4,128,256]{2,1,0:T(8,128)(2,1)S(1)}, bf16[4,128,256]{2,1,0:T(8,128)(2,1)S(1)}, bf16[4,128,256]{2,1,...) custom-call(s32[3]{0:T(128)S(1)} %pad_add_fusion.coords_ref, ...), custom_call_target="tpu_custom_call" | custom-call | tf_op jit(solution)/shard_map/project/pallas_call | solution.py:355
  52.7 2.8 %collective-permute-start.1 = (bf16[4,128,256]{2,1,0:T(8,128)(2,1)S(1)}, bf16[4,128,256]{2,1,0:T(8,128)(2,1)S(1)}, u32[]{:S(2)}, u32[]{:S(2)}) collective-permute-start(bf16[4,128,256]{2,1,0:T(8,128)(2,1)S(1)} %get-tuple-element.61), channel_id=1, source_target_pairs={{0,2},{1,3},{2,0},{3,1},{4,6},{5,7},{6,4},{7,5},{8,10},{9,11},{10,... | collective-permute-start | bytes 786440 | tf_op jit(solution)/shard_map/ppermute | solution.py:508
  58.4 2.7 %collective-permute-start.4 = (bf16[4,128,256]{2,1,0:T(8,128)(2,1)S(1)}, bf16[4,128,256]{2,1,0:T(8,128)(2,1)S(1)}, u32[]{:S(2)}, u32[]{:S(2)}) collective-permute-start(bf16[4,128,256]{2,1,0:T(8,128)(2,1)S(1)} %get-tuple-element.65), channel_id=1, source_target_pairs={{0,8},{4,12},{8,0},{12,4},{1,9},{5,13},{9,1},{13,5},{2,10},{6,14},... | collective-permute-start | bytes 786440 | tf_op jit(solution)/shard_map/ppermute | solution.py:508
  61.1 2.4 %collective-permute-start.5 = (bf16[4,128,256]{2,1,0:T(8,128)(2,1)S(1)}, bf16[4,128,256]{2,1,0:T(8,128)(2,1)S(1)}, u32[]{:S(2)}, u32[]{:S(2)}) collective-permute-start(bf16[4,128,256]{2,1,0:T(8,128)(2,1)S(1)} %get-tuple-element.66), channel_id=1, source_target_pairs={{0,12},{4,0},{8,4},{12,8},{1,13},{5,1},{9,5},{13,9},{2,14},{6,2},{... | collective-permute-start | bytes 786440 | tf_op jit(solution)/shard_map/ppermute | solution.py:508
  63.5 4.1 %collective-permute-done.1.rest_2_ = bf16[4,128,256]{2,1,0:T(8,128)(2,1)S(1)} collective-permute-done((bf16[4,128,256]{2,1,0:T(8,128)(2,1)S(1)}, bf16[4,128,256]{2,1,0:T(8,128)(2,1)S(1)}, u32[]{:S(2)}, u32[]{:S(2)}) %collective-permute-start.1) | collective-permute-done | bytes 262176 | tf_op jit(solution)/shard_map/ppermute | solution.py:508
  67.6 4.7 %collective-permute-done.4.rest_6_ = bf16[4,128,256]{2,1,0:T(8,128)(2,1)S(1)} collective-permute-done((bf16[4,128,256]{2,1,0:T(8,128)(2,1)S(1)}, bf16[4,128,256]{2,1,0:T(8,128)(2,1)S(1)}, u32[]{:S(2)}, u32[]{:S(2)}) %collective-permute-start.4) | collective-permute-done | bytes 262176 | tf_op jit(solution)/shard_map/ppermute | solution.py:508
  73.1 2.1 %collective-permute-start.6 = (bf16[128,256]{1,0:T(8,128)(2,1)S(1)}, bf16[128,256]{1,0:T(8,128)(2,1)S(1)}, u32[]{:S(2)}, u32[]{:S(2)}) collective-permute-start(bf16[128,256]{1,0:T(8,128)(2,1)S(1)} %get-tuple-element.68), channel_id=1, source_target_pairs={{0,4},{4,8},{8,12},{12,0},{1,5},{5,9},{9,13},{13,1},{2,6},{6,10},{... | collective-permute-start | bytes 196616 | tf_op jit(solution)/shard_map/ppermute | solution.py:508
  81.9 2.1 %collective-permute-done.9.refs_5_ = bf16[128,256]{1,0:T(8,128)(2,1)S(1)} collective-permute-done((bf16[128,256]{1,0:T(8,128)(2,1)S(1)}, bf16[128,256]{1,0:T(8,128)(2,1)S(1)}, u32[]{:S(2)}, u32[]{:S(2)}) %collective-permute-start.9) | collective-permute-done | bytes 65568 | tf_op jit(solution)/shard_map/ppermute | solution.py:508
  85.9 14.1 %all_to_all.10.recv_ref = bf16[16,64,256]{2,1,0:T(8,128)(2,1)S(1)} all-to-all(bf16[16,64,256]{2,1,0:T(8,128)(2,1)S(1)} %get-tuple-element.76), channel_id=1, replica_groups=mesh['y'=4,'core'=2,'x'=4,'z'=4] {'x','z'}, dimensions={0} | all-to-all | bytes 1048576 | tf_op jit(solution)/shard_map/all_to_all | solution.py:518
  100.3 2.9 %collective-permute-start.13 = (bf16[64,4096]{1,0:T(8,128)(2,1)S(1)}, bf16[64,4096]{1,0:T(8,128)(2,1)S(1)}, u32[]{:S(2)}, u32[]{:S(2)}) collective-permute-start(bf16[64,4096]{1,0:T(8,128)(2,1)S(1)} %normalize.1.after_ref.refs_0_), channel_id=1, source_target_pairs={{0,32},{32,64},{64,96},{96,0},{1,33},{33,65},{65,97},{97,1},{2,34}... | collective-permute-start | bytes 1572872 | tf_op jit(solution)/shard_map/ppermute | solution.py:490
  104.5 7.3 %load_weights.1 = (bf16[4096,896]{1,0:T(8,128)(2,1)S(1)}, bf16[4096,896]{1,0:T(8,128)(2,1)S(1)}, bf16[896,4096]{1,0:T(8,128)(2,1)S(1)}, f32[8,128]{1,0:T(8,128)S(1)}) custom-call(bf16[64,4096]{1,0:T(8,128)(2,1)S(1)} %normalize.1.after_ref.refs_0_, bf16[4096,896]{1,0:T(8,128)(2,1)} %bitcast.29, bf16[4096,896]{1,0:T(8,128)(2,1)} %bitcast.30, ...), custom_call_target="tpu_custom_call" | custom-call | bytes 44040192 | tf_op jit(solution)/shard_map/load_weights/pallas_call | solution.py:414
  111.9 3.8 %feed_forward.3 = (bf16[16,64,256]{2,1,0:T(8,128)(2,1)S(1)}, bf16[16,64,256]{2,1,0:T(8,128)(2,1)S(1)}, f32[8,128]{1,0:T(8,128)S(1)}) custom-call(bf16[64,4096]{1,0:T(8,128)(2,1)S(1)} %normalize.1.after_ref.refs_0_, bf16[64,4096]{1,0:T(8,128)(2,1)S(1)} %collective-permute-done.12.refs_1_, bf16[4096,896]{1,0:T(8,128)(2,1)S(1)} %get-tuple-element.79.refs_2_.refs_4_, ...), custom_call_target="tpu_custom_call" | custom-call | flops 2818572288 | bytes 2097152 | tf_op jit(solution)/shard_map/feed_forward/pallas_call | solution.py:434
  118.8 2.3 %collective-permute-start.19 = (bf16[32,4096]{1,0:T(8,128)(2,1)S(1)}, bf16[32,4096]{1,0:T(8,128)(2,1)S(1)}, u32[]{:S(2)}, u32[]{:S(2)}) collective-permute-start(bf16[32,4096]{1,0:T(8,128)(2,1)S(1)} %slice.7), channel_id=1, source_target_pairs={{0,96},{32,0},{64,32},{96,64},{1,97},{33,1},{65,33},{97,65},{2,98}... | collective-permute-start | bytes 786440 | tf_op jit(solution)/shard_map/ppermute | solution.py:490
  121.1 7.2 %feed_forward.4 = (bf16[16,64,256]{2,1,0:T(8,128)(2,1)S(1)}, bf16[16,64,256]{2,1,0:T(8,128)(2,1)S(1)}, bf16[16,64,256]{2,1,0:T(8,128)(2,1)S(1)}, bf16[16,64,256]{2,1,0:T(8,128)(2,1)S(1)}, f32[8,128]{1,0:T(8,128)S(1)}) custom-call(bf16[64,4096]{1,0:T(8,128)(2,1)S(1)} %collective-permute-done.13.refs_0_, bf16[64,4096]{1,0:T(8,128)(2,1)S(1)} %collective-permute-done.15.refs_1_, ...), custom_call_target="tpu_custom_call" | custom-call | flops 5637144576 | bytes 4194304 | tf_op jit(solution)/shard_map/feed_forward/pallas_call | solution.py:434
  131.8 4.2 %feed_forward.5 = (bf16[16,64,256]{2,1,0:T(8,128)(2,1)S(1)}, bf16[16,64,256]{2,1,0:T(8,128)(2,1)S(1)}, f32[8,128]{1,0:T(8,128)}) custom-call(bf16[32,4096]{1,0:T(8,128)(2,1)S(1)} %collective-permute-done.18.refs_0_, bf16[32,4096]{1,0:T(8,128)(2,1)S(1)} %collective-permute-done.19.refs_1_, bf16[32,4096]{1,0:T(8,128)(2,1)S(1)} %collective-permute-done.24.refs_2_, ...), custom_call_target="tpu_custom_call" | custom-call | flops 2818572288 | bytes 2097152 | tf_op jit(solution)/shard_map/feed_forward/pallas_call | solution.py:434
  136.2 2.4 %collective-permute-start.22 = (bf16[16,64,256]{2,1,0:T(8,128)(2,1)S(1)}, bf16[16,64,256]{2,1,0:T(8,128)(2,1)S(1)}, u32[]{:S(2)}, u32[]{:S(2)}) collective-permute-start(bf16[16,64,256]{2,1,0:T(8,128)(2,1)S(1)} %add_up.5), channel_id=1, source_target_pairs={{0,96},{32,0},{64,32},{96,64},{1,97},{33,1},{65,33},{97,65},{2,98}... | collective-permute-start | bytes 1572872 | tf_op jit(solution)/shard_map/ppermute | solution.py:490
  140.7 20.9 %collective-permute-done.22.refs_2_ = bf16[16,64,256]{2,1,0:T(8,128)(2,1)S(1)} collective-permute-done((bf16[16,64,256]{2,1,0:T(8,128)(2,1)S(1)}, bf16[16,64,256]{2,1,0:T(8,128)(2,1)S(1)}, u32[]{:S(2)}, u32[]{:S(2)}) %collective-permute-start.22) | collective-permute-done | bytes 524320 | tf_op jit(solution)/shard_map/ppermute | solution.py:490
  161.5 3.4 %collective-permute-done.23.refs_3_ = bf16[16,64,256]{2,1,0:T(8,128)(2,1)S(1)} collective-permute-done((bf16[16,64,256]{2,1,0:T(8,128)(2,1)S(1)}, bf16[16,64,256]{2,1,0:T(8,128)(2,1)S(1)}, u32[]{:S(2)}, u32[]{:S(2)}) %collective-permute-start.23) | collective-permute-done | bytes 524320 | tf_op jit(solution)/shard_map/ppermute | solution.py:490
  166.1 3.6 %all-to-all-start.1 = ((bf16[16,64,256]{2,1,0:T(8,128)(2,1)}), bf16[16,64,256]{2,1,0:T(8,128)(2,1)S(1)}, u32[]{:S(2)}, u32[]{:S(2)}) async-start(bf16[16,64,256]{2,1,0:T(8,128)(2,1)} %add_up.9), calls=%async_computation.1 | async-start | bytes 1048576 | tf_op jit(solution)/shard_map/all_to_all | solution.py:546
  169.8 11.0 %all-to-all-done.1.recv_ref = bf16[16,64,256]{2,1,0:T(8,128)(2,1)S(1)} async-done(((bf16[16,64,256]{2,1,0:T(8,128)(2,1)}), bf16[16,64,256]{2,1,0:T(8,128)(2,1)S(1)}, u32[]{:S(2)}, u32[]{:S(2)}) %all-to-all-start.1) | async-done | bytes 524320 | tf_op jit(solution)/shard_map/all_to_all | solution.py:546
  (82 shorter events, 36.5 us)
Async XLA Ops:
  6.5 40.3 %all-gather.4.cloned.1.call-start = ((), (), s32[]{:S(2)}) async-start(), calls=%async_computation.2 | async-start | bytes 4718592 | tf_op jit(solution)/shard_map/all_gather | solution.py:492
  51.0 10.0 %collective-permute-start = (bf16[4,128,256]{2,1,0:T(8,128)(2,1)S(1)}, bf16[4,128,256]{2,1,0:T(8,128)(2,1)S(1)}, u32[]{:S(2)}, u32[]{:S(2)}) collective-permute-start(bf16[4,128,256]{2,1,0:T(8,128)(2,1)S(1)} %get-tuple-element.60), channel_id=1, source_target_pairs={{0,1},{1,2},{2,3},{3,0},{4,5},{5,6},{6,7},{7,4},{8,9},{9,10},{10,1... | collective-permute-start | bytes 786440 | tf_op jit(solution)/shard_map/ppermute | solution.py:508
  52.7 14.9 %collective-permute-start.1 = (bf16[4,128,256]{2,1,0:T(8,128)(2,1)S(1)}, bf16[4,128,256]{2,1,0:T(8,128)(2,1)S(1)}, u32[]{:S(2)}, u32[]{:S(2)}) collective-permute-start(bf16[4,128,256]{2,1,0:T(8,128)(2,1)S(1)} %get-tuple-element.61), channel_id=1, source_target_pairs={{0,2},{1,3},{2,0},{3,1},{4,6},{5,7},{6,4},{7,5},{8,10},{9,11},{10,... | collective-permute-start | bytes 786440 | tf_op jit(solution)/shard_map/ppermute | solution.py:508
  55.5 12.1 %collective-permute-start.2 = (bf16[4,128,256]{2,1,0:T(8,128)(2,1)S(1)}, bf16[4,128,256]{2,1,0:T(8,128)(2,1)S(1)}, u32[]{:S(2)}, u32[]{:S(2)}) collective-permute-start(bf16[4,128,256]{2,1,0:T(8,128)(2,1)S(1)} %get-tuple-element.62), channel_id=1, source_target_pairs={{0,3},{1,0},{2,1},{3,2},{4,7},{5,4},{6,5},{7,6},{8,11},{9,8},{10,9... | collective-permute-start | bytes 786440 | tf_op jit(solution)/shard_map/ppermute | solution.py:508
  56.9 10.7 %collective-permute-start.3 = (bf16[4,128,256]{2,1,0:T(8,128)(2,1)S(1)}, bf16[4,128,256]{2,1,0:T(8,128)(2,1)S(1)}, u32[]{:S(2)}, u32[]{:S(2)}) collective-permute-start(bf16[4,128,256]{2,1,0:T(8,128)(2,1)S(1)} %get-tuple-element.64), channel_id=1, source_target_pairs={{0,4},{4,8},{8,12},{12,0},{1,5},{5,9},{9,13},{13,1},{2,6},{6,10},{... | collective-permute-start | bytes 786440 | tf_op jit(solution)/shard_map/ppermute | solution.py:508
  58.4 13.9 %collective-permute-start.4 = (bf16[4,128,256]{2,1,0:T(8,128)(2,1)S(1)}, bf16[4,128,256]{2,1,0:T(8,128)(2,1)S(1)}, u32[]{:S(2)}, u32[]{:S(2)}) collective-permute-start(bf16[4,128,256]{2,1,0:T(8,128)(2,1)S(1)} %get-tuple-element.65), channel_id=1, source_target_pairs={{0,8},{4,12},{8,0},{12,4},{1,9},{5,13},{9,1},{13,5},{2,10},{6,14},... | collective-permute-start | bytes 786440 | tf_op jit(solution)/shard_map/ppermute | solution.py:508
  61.1 11.2 %collective-permute-start.5 = (bf16[4,128,256]{2,1,0:T(8,128)(2,1)S(1)}, bf16[4,128,256]{2,1,0:T(8,128)(2,1)S(1)}, u32[]{:S(2)}, u32[]{:S(2)}) collective-permute-start(bf16[4,128,256]{2,1,0:T(8,128)(2,1)S(1)} %get-tuple-element.66), channel_id=1, source_target_pairs={{0,12},{4,0},{8,4},{12,8},{1,13},{5,1},{9,5},{13,9},{2,14},{6,2},{... | collective-permute-start | bytes 786440 | tf_op jit(solution)/shard_map/ppermute | solution.py:508
  73.1 7.1 %collective-permute-start.6 = (bf16[128,256]{1,0:T(8,128)(2,1)S(1)}, bf16[128,256]{1,0:T(8,128)(2,1)S(1)}, u32[]{:S(2)}, u32[]{:S(2)}) collective-permute-start(bf16[128,256]{1,0:T(8,128)(2,1)S(1)} %get-tuple-element.68), channel_id=1, source_target_pairs={{0,4},{4,8},{8,12},{12,0},{1,5},{5,9},{9,13},{13,1},{2,6},{6,10},{... | collective-permute-start | bytes 196616 | tf_op jit(solution)/shard_map/ppermute | solution.py:508
  75.2 6.7 %collective-permute-start.7 = (bf16[128,256]{1,0:T(8,128)(2,1)S(1)}, bf16[128,256]{1,0:T(8,128)(2,1)S(1)}, u32[]{:S(2)}, u32[]{:S(2)}) collective-permute-start(bf16[128,256]{1,0:T(8,128)(2,1)S(1)} %get-tuple-element.69), channel_id=1, source_target_pairs={{0,8},{4,12},{8,0},{12,4},{1,9},{5,13},{9,1},{13,5},{2,10},{6,14},... | collective-permute-start | bytes 196616 | tf_op jit(solution)/shard_map/ppermute | solution.py:508
  76.9 4.9 %collective-permute-start.8 = (bf16[128,256]{1,0:T(8,128)(2,1)S(1)}, bf16[128,256]{1,0:T(8,128)(2,1)S(1)}, u32[]{:S(2)}, u32[]{:S(2)}) collective-permute-start(bf16[128,256]{1,0:T(8,128)(2,1)S(1)} %get-tuple-element.70), channel_id=1, source_target_pairs={{0,12},{4,0},{8,4},{12,8},{1,13},{5,1},{9,5},{13,9},{2,14},{6,2},{... | collective-permute-start | bytes 196616 | tf_op jit(solution)/shard_map/ppermute | solution.py:508
  78.5 5.5 %collective-permute-start.9 = (bf16[128,256]{1,0:T(8,128)(2,1)S(1)}, bf16[128,256]{1,0:T(8,128)(2,1)S(1)}, u32[]{:S(2)}, u32[]{:S(2)}) collective-permute-start(bf16[128,256]{1,0:T(8,128)(2,1)S(1)} %get-tuple-element.72), channel_id=1, source_target_pairs={{0,1},{1,2},{2,3},{3,0},{4,5},{5,6},{6,7},{7,4},{8,9},{9,10},{10,1... | collective-permute-start | bytes 196616 | tf_op jit(solution)/shard_map/ppermute | solution.py:508
  79.1 5.8 %collective-permute-start.10 = (bf16[128,256]{1,0:T(8,128)(2,1)S(1)}, bf16[128,256]{1,0:T(8,128)(2,1)S(1)}, u32[]{:S(2)}, u32[]{:S(2)}) collective-permute-start(bf16[128,256]{1,0:T(8,128)(2,1)S(1)} %get-tuple-element.73), channel_id=1, source_target_pairs={{0,2},{1,3},{2,0},{3,1},{4,6},{5,7},{6,4},{7,5},{8,10},{9,11},{10,... | collective-permute-start | bytes 196616 | tf_op jit(solution)/shard_map/ppermute | solution.py:508
  80.2 5.3 %collective-permute-start.11 = (bf16[128,256]{1,0:T(8,128)(2,1)S(1)}, bf16[128,256]{1,0:T(8,128)(2,1)S(1)}, u32[]{:S(2)}, u32[]{:S(2)}) collective-permute-start(bf16[128,256]{1,0:T(8,128)(2,1)S(1)} %get-tuple-element.74), channel_id=1, source_target_pairs={{0,3},{1,0},{2,1},{3,2},{4,7},{5,4},{6,5},{7,6},{8,11},{9,8},{10,9... | collective-permute-start | bytes 196616 | tf_op jit(solution)/shard_map/ppermute | solution.py:508
  100.2 11.6 %collective-permute-start.12 = (bf16[64,4096]{1,0:T(8,128)(2,1)S(1)}, bf16[64,4096]{1,0:T(8,128)(2,1)S(1)}, u32[]{:S(2)}, u32[]{:S(2)}) collective-permute-start(bf16[64,4096]{1,0:T(8,128)(2,1)S(1)} %normalize.1.after_ref.refs_0_), channel_id=1, source_target_pairs={{0,16},{16,0},{1,17},{17,1},{2,18},{18,2},{3,19},{19,3},{4,20},{20... | collective-permute-start | bytes 1572872 | tf_op jit(solution)/shard_map/ppermute | solution.py:487
  100.3 16.6 %collective-permute-start.13 = (bf16[64,4096]{1,0:T(8,128)(2,1)S(1)}, bf16[64,4096]{1,0:T(8,128)(2,1)S(1)}, u32[]{:S(2)}, u32[]{:S(2)}) collective-permute-start(bf16[64,4096]{1,0:T(8,128)(2,1)S(1)} %normalize.1.after_ref.refs_0_), channel_id=1, source_target_pairs={{0,32},{32,64},{64,96},{96,0},{1,33},{33,65},{65,97},{97,1},{2,34}... | collective-permute-start | bytes 1572872 | tf_op jit(solution)/shard_map/ppermute | solution.py:490
  103.3 14.0 %collective-permute-start.14 = (bf16[64,4096]{1,0:T(8,128)(2,1)S(1)}, bf16[64,4096]{1,0:T(8,128)(2,1)S(1)}, u32[]{:S(2)}, u32[]{:S(2)}) collective-permute-start(bf16[64,4096]{1,0:T(8,128)(2,1)S(1)} %normalize.1.after_ref.refs_0_), channel_id=1, source_target_pairs={{0,96},{32,0},{64,32},{96,64},{1,97},{33,1},{65,33},{97,65},{2,98}... | collective-permute-start | bytes 1572872 | tf_op jit(solution)/shard_map/ppermute | solution.py:490
  117.2 3.9 %collective-permute-start.15 = (bf16[64,4096]{1,0:T(8,128)(2,1)S(1)}, bf16[64,4096]{1,0:T(8,128)(2,1)S(1)}, u32[]{:S(2)}, u32[]{:S(2)}) collective-permute-start(bf16[64,4096]{1,0:T(8,128)(2,1)S(1)} %collective-permute-done.13.refs_0_), channel_id=1, source_target_pairs={{0,16},{16,0},{1,17},{17,1},{2,18},{18,2},{3,19},{19,3},{4,20},{20... | collective-permute-start | bytes 1572872 | tf_op jit(solution)/shard_map/ppermute | solution.py:487
  117.3 3.9 %collective-permute-start.16 = (bf16[16,64,256]{2,1,0:T(8,128)(2,1)S(1)}, bf16[16,64,256]{2,1,0:T(8,128)(2,1)S(1)}, u32[]{:S(2)}, u32[]{:S(2)}) collective-permute-start(bf16[16,64,256]{2,1,0:T(8,128)(2,1)S(1)} %get-tuple-element.86), channel_id=1, source_target_pairs={{0,16},{16,0},{1,17},{17,1},{2,18},{18,2},{3,19},{19,3},{4,20},{20... | collective-permute-start | bytes 1572872 | tf_op jit(solution)/shard_map/ppermute | solution.py:487
  117.8 10.5 %collective-permute-start.18 = (bf16[32,4096]{1,0:T(8,128)(2,1)S(1)}, bf16[32,4096]{1,0:T(8,128)(2,1)S(1)}, u32[]{:S(2)}, u32[]{:S(2)}) collective-permute-start(bf16[32,4096]{1,0:T(8,128)(2,1)S(1)} %slice.6), channel_id=1, source_target_pairs={{0,32},{32,64},{64,96},{96,0},{1,33},{33,65},{65,97},{97,1},{2,34}... | collective-permute-start | bytes 786440 | tf_op jit(solution)/shard_map/ppermute | solution.py:490
  118.8 9.6 %collective-permute-start.19 = (bf16[32,4096]{1,0:T(8,128)(2,1)S(1)}, bf16[32,4096]{1,0:T(8,128)(2,1)S(1)}, u32[]{:S(2)}, u32[]{:S(2)}) collective-permute-start(bf16[32,4096]{1,0:T(8,128)(2,1)S(1)} %slice.7), channel_id=1, source_target_pairs={{0,96},{32,0},{64,32},{96,64},{1,97},{33,1},{65,33},{97,65},{2,98}... | collective-permute-start | bytes 786440 | tf_op jit(solution)/shard_map/ppermute | solution.py:490
  136.2 25.3 %collective-permute-start.22 = (bf16[16,64,256]{2,1,0:T(8,128)(2,1)S(1)}, bf16[16,64,256]{2,1,0:T(8,128)(2,1)S(1)}, u32[]{:S(2)}, u32[]{:S(2)}) collective-permute-start(bf16[16,64,256]{2,1,0:T(8,128)(2,1)S(1)} %add_up.5), channel_id=1, source_target_pairs={{0,96},{32,0},{64,32},{96,64},{1,97},{33,1},{65,33},{97,65},{2,98}... | collective-permute-start | bytes 1572872 | tf_op jit(solution)/shard_map/ppermute | solution.py:490
  138.6 26.4 %collective-permute-start.23 = (bf16[16,64,256]{2,1,0:T(8,128)(2,1)S(1)}, bf16[16,64,256]{2,1,0:T(8,128)(2,1)S(1)}, u32[]{:S(2)}, u32[]{:S(2)}) collective-permute-start(bf16[16,64,256]{2,1,0:T(8,128)(2,1)S(1)} %add_up.6), channel_id=1, source_target_pairs={{0,32},{32,64},{64,96},{96,0},{1,33},{33,65},{65,97},{97,1},{2,34}... | collective-permute-start | bytes 1572872 | tf_op jit(solution)/shard_map/ppermute | solution.py:490
  138.7 26.5 %collective-permute-start.27 = (bf16[16,64,256]{2,1,0:T(8,128)(2,1)S(1)}, bf16[16,64,256]{2,1,0:T(8,128)(2,1)S(1)}, u32[]{:S(2)}, u32[]{:S(2)}) collective-permute-start(bf16[16,64,256]{2,1,0:T(8,128)(2,1)S(1)} %add_up.8), channel_id=1, source_target_pairs={{0,64},{32,96},{64,0},{96,32},{1,65},{33,97},{65,1},{97,33},{2,66}... | collective-permute-start | bytes 1572872 | tf_op jit(solution)/shard_map/ppermute | solution.py:490
  166.1 14.7 %all-to-all-start.1 = ((bf16[16,64,256]{2,1,0:T(8,128)(2,1)}), bf16[16,64,256]{2,1,0:T(8,128)(2,1)S(1)}, u32[]{:S(2)}, u32[]{:S(2)}) async-start(bf16[16,64,256]{2,1,0:T(8,128)(2,1)} %add_up.9), calls=%async_computation.1 | async-start | bytes 1048576 | tf_op jit(solution)/shard_map/all_to_all | solution.py:546
  (12 other events, 175.3 us)
Sparse Core Ops, SparseCore 0:
  9.1 37.7 all-gather.3

commit v5 on v4

--- a/solution.py
+++ b/solution.py
@@ -167,12 +167,12 @@
     ids_out[...] = ids_ref[...]
 
 
-def fold(coords_ref, *rest, sides):
+def fold(coords_ref, *rest, sides, ways):
     nx, nz = sides
-    z_refs, x_refs = rest[:nz], rest[nz : nz + nx]
-    first_refs, last_refs = rest[nz + nx : nz + 2 * nx], rest[nz + 2 * nx :]
+    parts, outs = rest[: len(ways)], rest[len(ways) :]
+    groups = [[p for p, (i, _) in zip(parts, ways) if i == group] for group in (0, 1)]
     x, z = coords_ref[1], coords_ref[2]
-    for parts, outs, at, count in ((z_refs, first_refs, x, nx), (x_refs, last_refs, z, nz)):
+    for parts, outs, at, count in ((groups[0], outs[:nx], x, nx), (groups[1], outs[nx:], z, nz)):
         for d, out in enumerate(outs):
             block = lax.rem(at + d, count)
             total = parts[0][block].astype(f32)
@@ -181,12 +181,13 @@
             out[...] = total.astype(bf16)
 
 
-def dispatch(*refs, sides):
+def dispatch(*refs, ways):
     *recvs, hidden_ref, ids_ref, res_ref, slots_ref, pick = refs
     experts, slots, width = slots_ref.shape
     tokens = hidden_ref.shape[0]
     half = tokens // 2
-    for rows, parts in ((slice(0, half), recvs[: sides[0]]), (slice(half, tokens), recvs[sides[0] :])):
+    groups = [[p for p, (i, _) in zip(recvs, ways) if i == group] for group in (0, 1)]
+    for rows, parts in ((slice(0, half), groups[0]), (slice(half, tokens), groups[1])):
         part = hidden_ref[rows].astype(f32)
         for p in parts:
             part = part + p[...].astype(f32)
@@ -369,11 +370,11 @@
     )(coords, mixed, ids, pltpu.with_memory_space_constraint(proj, pltpu.HBM))
 
 
-def run_fold(coords, parts, sides):
+def run_fold(coords, parts, sides, ways):
     nx, nz = sides
     _, half, share = parts[0].shape
     return pl.pallas_call(
-        functools.partial(fold, sides=sides),
+        functools.partial(fold, sides=sides, ways=ways),
         out_shape=[jax.ShapeDtypeStruct((half, share), bf16)] * (nx + nz),
         in_specs=[smem()] + [vmem()] * (nx + nz),
         out_specs=[vmem()] * (nx + nz),
@@ -382,10 +383,10 @@
     )(coords, *parts)
 
 
-def run_dispatch(recvs, hidden, ids, experts, slots, sides):
+def run_dispatch(recvs, hidden, ids, experts, slots, ways):
     tokens, share = hidden.shape
     return pl.pallas_call(
-        functools.partial(dispatch, sides=sides),
+        functools.partial(dispatch, ways=ways),
         out_shape=(
             jax.ShapeDtypeStruct((tokens, share), f32),
             jax.ShapeDtypeStruct((experts, slots, share), bf16),
@@ -507,14 +508,22 @@
         n = lax.axis_size(axis)
         return lax.ppermute(value, axis, [(i, (i + d) % n) for i in range(n)]) if d else value
 
+    def spread_out(one, one_axis, two, two_axis):
+        sides = ((one, one_axis), (two, two_axis))
+        ways = [(i, d) for i, (parts, _) in enumerate(sides) for d in range(len(parts))]
+        hops = {(i, d): min(d, len(sides[i][0]) - d) for i, d in ways}
+        lead = (0, 1)
+        ways = sorted(ways, key=lambda w: (w != lead, -hops[w], w[1], w[0]))
+        return [shift(sides[i][0][d], sides[i][1], d) for i, d in ways], tuple(ways)
+
     nx, nz = sides
     ids = route_ids.reshape(tokens, -1)
     *parts, by_choice = run_project(coords, mixed, ids.T, proj, share, sides)
     hidden = hidden_in.reshape(tokens, share)
-    parts = [shift(p, "z", d) for d, p in enumerate(parts[:nz])] + [shift(p, "x", d) for d, p in enumerate(parts[nz:])]
-    parts = run_fold(coords, parts, sides)
-    parts = [shift(p, "x", d) for d, p in enumerate(parts[:nx])] + [shift(p, "z", d) for d, p in enumerate(parts[nx:])]
-    residual, slot_rows = run_dispatch(parts, hidden, by_choice, experts, slots, sides)
+    parts, ways = spread_out(parts[:nz], "z", parts[nz:], "x")
+    parts = run_fold(coords, parts, sides, ways)
+    parts, ways = spread_out(parts[:nx], "x", parts[nx:], "z")
+    residual, slot_rows = run_dispatch(parts, hidden, by_choice, experts, slots, ways)
     whole = lax.all_to_all(slot_rows, exp, 0, 0, tiled=True)
     own = run_normalize(whole, norm_gain.reshape(1, -1))
 

time: 190 us -> 191 us (level)
  waiting for transfers between devices: 54.2 us -> 51.6 us
    ppermute x12, waiting for transfers between devices: 12.4 us -> 9.83 us  [shift(): lax.ppermute(value, axis, [(i, (i + d) % n) for i in range(n)])]
    ppermute x7, starting transfers between devices: 11.8 us -> 14 us  [ring(): lax.ppermute(value, 'y', [(i, (i + d) % chips) for i in range(chips)])]
  transfers between devices with their start and end apart: 30 -> 30, of which waited for: 15 -> 17; matrix products, arithmetic and copies ran while one was open for 3% -> 3% of each run, Pallas kernels for 17% -> 17%
where the time goes in v5:
time: 191 us; the launch traced here: 190 us
  waiting for transfers between devices  51.6 us (27%)
  Pallas kernels  43.7 us (23%)
  starting transfers between devices  40.3 us (21%)
  blocking collectives  31.2 us (16%)
  between operations  13.6 us (7%)
  local copies, waits for them, and re-layouts  9.45 us (5%)
    ppermute x7, waiting for transfers between devices, ring(): lax.ppermute(value, 'y', [(i, (i + d) % chips) for i in range(chips)])  25.9 us
    ppermute x12, starting transfers between devices, shift(): lax.ppermute(value, axis, [(i, (i + d) % n) for i in range(n)])  20.9 us
    all_to_all x1, blocking collectives, on_device(): whole = lax.all_to_all(slot_rows, exp, 0, 0, tiled=True)  15.6 us
    all_gather x1, blocking collectives, on_device(): ends = lax.all_gather(end, ctx)  15.6 us
    pallas_call x3, Pallas kernels, run_ffn(): pl.pallas_call(functools.partial(feed_forward, groups=tuple(((len(own), l...  15.2 us
    ppermute x7, starting transfers between devices, ring(): lax.ppermute(value, 'y', [(i, (i + d) % chips) for i in range(chips)])  14 us
    all_to_all x1, waiting for transfers between devices, on_device(): back = lax.all_to_all(returned, exp, 0, 0, tiled=True)  11 us
    ppermute x12, waiting for transfers between devices, shift(): lax.ppermute(value, axis, [(i, (i + d) % n) for i in range(n)])  9.83 us
  transfers between devices with their start and end apart: 30, of which 17 were waited for; matrix products, arithmetic and copies ran while one was open for 3% of the time, Pallas kernels for 17%

profile of v5, /device:TPU:0, one launch (start us, length us, event | category | flops | bytes accessed | tf_op | source)
XLA Modules:
  0.0 190.1 jit_solution(8108622985301803922)
XLA Ops:
  14.3 6.1 %scan_first.1 = (f32[2,17,512]{2,1,0:T(8,128)S(1)}, f32[2,16,8,512]{3,2,1,0:T(8,128)S(1)}, f32[2,8,512]{2,1,0:T(8,128)S(1)}) custom-call(f32[256,512]{1,0:T(8,128)S(1)} %reshape.33.step_ref, bf16[256,512]{1,0:T(8,128)(2,1)S(1)} %reshape.34.sig_ref, f32[16,8,32]{2,1,0:T(8,128)S(1)} %bitcast.24, f32[16,512]{1,0:T(8,128)S(1)} %copy-done), custom_call_target="tpu_custom_call" | custom-call | tf_op jit(solution)/shard_map/scan_first/pallas_call | solution.py:309
  20.6 15.6 %all-gather = f32[16,17,512]{2,1,0:T(8,128)S(1)} all-gather(f32[2,17,512]{2,1,0:T(8,128)S(1)} %get-tuple-element.58), channel_id=2, replica_groups=mesh['y'=4,'core'=2,'x'=4,'z'=4] {'y','core'}, dimensions={0}, use_global_device_ids=true | all-gather | bytes 626688 | tf_op jit(solution)/shard_map/all_gather | solution.py:498
  37.6 7.2 %scan_second.1.mixed_ref = bf16[256,512]{1,0:T(8,128)(2,1)S(1)} custom-call(s32[3]{0:T(128)S(1)} %pad_add_fusion.coords_ref, f32[256,512]{1,0:T(8,128)S(1)} %reshape.33.step_ref, bf16[256,512]{1,0:T(8,128)(2,1)S(1)} %reshape.34.sig_ref, bf16[256,512]{1,0:T(8,128)(2,1)S(1)} %reshape.35.gate_ref, f32[16,8,32]{2,1,0:T(8,128)S(1)} %bitcast.25, ...), custom_call_target="tpu_custom_call" | custom-call | flops 2000000000 | bytes 2097152 | tf_op jit(solution)/shard_map/scan_second/pallas_call | solution.py:333
  44.8 2.1 %all-gather.4.cloned.1.call-done = bf16[4096,512]{1,0:T(8,128)(2,1)} async-done(((bf16[512,512]{1,0:T(8,128)(2,1)}), bf16[4096,512]{1,0:T(8,128)(2,1)}) %all-gather.4.cloned.1.call-update) | async-done | bytes 4194320 | tf_op jit(solution)/shard_map/all_gather | solution.py:493
  46.9 4.2 %project.1 = (bf16[4,128,256]{2,1,0:T(8,128)(2,1)S(1)}, bf16[4,128,256]{2,1,0:T(8,128)(2,1)S(1)}, bf16[4,128,256]{2,1,0:T(8,128)(2,1)S(1)}, bf16[4,128,256]{2,1,...) custom-call(s32[3]{0:T(128)S(1)} %pad_add_fusion.coords_ref, ...), custom_call_target="tpu_custom_call" | custom-call | tf_op jit(solution)/shard_map/project/pallas_call | solution.py:356
  52.7 2.8 %collective-permute-start.1 = (bf16[4,128,256]{2,1,0:T(8,128)(2,1)S(1)}, bf16[4,128,256]{2,1,0:T(8,128)(2,1)S(1)}, u32[]{:S(2)}, u32[]{:S(2)}) collective-permute-start(bf16[4,128,256]{2,1,0:T(8,128)(2,1)S(1)} %get-tuple-element.60), channel_id=1, source_target_pairs={{0,2},{1,3},{2,0},{3,1},{4,6},{5,7},{6,4},{7,5},{8,10},{9,11},{10,... | collective-permute-start | bytes 786440 | tf_op jit(solution)/shard_map/ppermute | solution.py:509
  55.5 3.0 %collective-permute-start.2 = (bf16[4,128,256]{2,1,0:T(8,128)(2,1)S(1)}, bf16[4,128,256]{2,1,0:T(8,128)(2,1)S(1)}, u32[]{:S(2)}, u32[]{:S(2)}) collective-permute-start(bf16[4,128,256]{2,1,0:T(8,128)(2,1)S(1)} %get-tuple-element.61), channel_id=1, source_target_pairs={{0,8},{4,12},{8,0},{12,4},{1,9},{5,13},{9,1},{13,5},{2,10},{6,14},... | collective-permute-start | bytes 786440 | tf_op jit(solution)/shard_map/ppermute | solution.py:509
  60.8 2.7 %collective-permute-start.5 = (bf16[4,128,256]{2,1,0:T(8,128)(2,1)S(1)}, bf16[4,128,256]{2,1,0:T(8,128)(2,1)S(1)}, u32[]{:S(2)}, u32[]{:S(2)}) collective-permute-start(bf16[4,128,256]{2,1,0:T(8,128)(2,1)S(1)} %get-tuple-element.64), channel_id=1, source_target_pairs={{0,12},{4,0},{8,4},{12,8},{1,13},{5,1},{9,5},{13,9},{2,14},{6,2},{... | collective-permute-start | bytes 786440 | tf_op jit(solution)/shard_map/ppermute | solution.py:509
  63.5 4.1 %collective-permute-done.1.rest_1_ = bf16[4,128,256]{2,1,0:T(8,128)(2,1)S(1)} collective-permute-done((bf16[4,128,256]{2,1,0:T(8,128)(2,1)S(1)}, bf16[4,128,256]{2,1,0:T(8,128)(2,1)S(1)}, u32[]{:S(2)}, u32[]{:S(2)}) %collective-permute-start.1) | collective-permute-done | bytes 262176 | tf_op jit(solution)/shard_map/ppermute | solution.py:509
  67.6 3.0 %collective-permute-done.3.rest_3_ = bf16[4,128,256]{2,1,0:T(8,128)(2,1)S(1)} collective-permute-done((bf16[4,128,256]{2,1,0:T(8,128)(2,1)S(1)}, bf16[4,128,256]{2,1,0:T(8,128)(2,1)S(1)}, u32[]{:S(2)}, u32[]{:S(2)}) %collective-permute-start.3) | collective-permute-done | bytes 262176 | tf_op jit(solution)/shard_map/ppermute | solution.py:509
  73.0 2.8 %collective-permute-start.7 = (bf16[128,256]{1,0:T(8,128)(2,1)S(1)}, bf16[128,256]{1,0:T(8,128)(2,1)S(1)}, u32[]{:S(2)}, u32[]{:S(2)}) collective-permute-start(bf16[128,256]{1,0:T(8,128)(2,1)S(1)} %get-tuple-element.68), channel_id=1, source_target_pairs={{0,8},{4,12},{8,0},{12,4},{1,9},{5,13},{9,1},{13,5},{2,10},{6,14},... | collective-permute-start | bytes 196616 | tf_op jit(solution)/shard_map/ppermute | solution.py:509
  83.1 15.6 %all_to_all.10.recv_ref = bf16[16,64,256]{2,1,0:T(8,128)(2,1)S(1)} all-to-all(bf16[16,64,256]{2,1,0:T(8,128)(2,1)S(1)} %get-tuple-element.76), channel_id=1, replica_groups=mesh['y'=4,'core'=2,'x'=4,'z'=4] {'x','z'}, dimensions={0} | all-to-all | bytes 1048576 | tf_op jit(solution)/shard_map/all_to_all | solution.py:527
  99.1 5.1 %collective-permute-start.13 = (bf16[64,4096]{1,0:T(8,128)(2,1)S(1)}, bf16[64,4096]{1,0:T(8,128)(2,1)S(1)}, u32[]{:S(2)}, u32[]{:S(2)}) collective-permute-start(bf16[64,4096]{1,0:T(8,128)(2,1)S(1)} %normalize.1.after_ref.refs_0_), channel_id=1, source_target_pairs={{0,32},{32,64},{64,96},{96,0},{1,33},{33,65},{65,97},{97,1},{2,34}... | collective-permute-start | bytes 1572872 | tf_op jit(solution)/shard_map/ppermute | solution.py:491
  105.5 7.3 %load_weights.1 = (bf16[4096,896]{1,0:T(8,128)(2,1)S(1)}, bf16[4096,896]{1,0:T(8,128)(2,1)S(1)}, bf16[896,4096]{1,0:T(8,128)(2,1)S(1)}, f32[8,128]{1,0:T(8,128)S(1)}) custom-call(bf16[64,4096]{1,0:T(8,128)(2,1)S(1)} %normalize.1.after_ref.refs_0_, bf16[4096,896]{1,0:T(8,128)(2,1)} %bitcast.29, bf16[4096,896]{1,0:T(8,128)(2,1)} %bitcast.30, ...), custom_call_target="tpu_custom_call" | custom-call | bytes 44040192 | tf_op jit(solution)/shard_map/load_weights/pallas_call | solution.py:415
  112.8 3.8 %feed_forward.3 = (bf16[16,64,256]{2,1,0:T(8,128)(2,1)S(1)}, bf16[16,64,256]{2,1,0:T(8,128)(2,1)S(1)}, f32[8,128]{1,0:T(8,128)S(1)}) custom-call(bf16[64,4096]{1,0:T(8,128)(2,1)S(1)} %normalize.1.after_ref.refs_0_, bf16[64,4096]{1,0:T(8,128)(2,1)S(1)} %collective-permute-done.12.refs_1_, bf16[4096,896]{1,0:T(8,128)(2,1)S(1)} %get-tuple-element.79.refs_2_.refs_4_, ...), custom_call_target="tpu_custom_call" | custom-call | flops 2818572288 | bytes 2097152 | tf_op jit(solution)/shard_map/feed_forward/pallas_call | solution.py:435
  119.7 2.3 %collective-permute-start.19 = (bf16[32,4096]{1,0:T(8,128)(2,1)S(1)}, bf16[32,4096]{1,0:T(8,128)(2,1)S(1)}, u32[]{:S(2)}, u32[]{:S(2)}) collective-permute-start(bf16[32,4096]{1,0:T(8,128)(2,1)S(1)} %slice.7), channel_id=1, source_target_pairs={{0,96},{32,0},{64,32},{96,64},{1,97},{33,1},{65,33},{97,65},{2,98}... | collective-permute-start | bytes 786440 | tf_op jit(solution)/shard_map/ppermute | solution.py:491
  122.1 7.2 %feed_forward.4 = (bf16[16,64,256]{2,1,0:T(8,128)(2,1)S(1)}, bf16[16,64,256]{2,1,0:T(8,128)(2,1)S(1)}, bf16[16,64,256]{2,1,0:T(8,128)(2,1)S(1)}, bf16[16,64,256]{2,1,0:T(8,128)(2,1)S(1)}, f32[8,128]{1,0:T(8,128)S(1)}) custom-call(bf16[64,4096]{1,0:T(8,128)(2,1)S(1)} %collective-permute-done.13.refs_0_, bf16[64,4096]{1,0:T(8,128)(2,1)S(1)} %collective-permute-done.15.refs_1_, ...), custom_call_target="tpu_custom_call" | custom-call | flops 5637144576 | bytes 4194304 | tf_op jit(solution)/shard_map/feed_forward/pallas_call | solution.py:435
  132.8 4.2 %feed_forward.5 = (bf16[16,64,256]{2,1,0:T(8,128)(2,1)S(1)}, bf16[16,64,256]{2,1,0:T(8,128)(2,1)S(1)}, f32[8,128]{1,0:T(8,128)}) custom-call(bf16[32,4096]{1,0:T(8,128)(2,1)S(1)} %collective-permute-done.18.refs_0_, bf16[32,4096]{1,0:T(8,128)(2,1)S(1)} %collective-permute-done.19.refs_1_, bf16[32,4096]{1,0:T(8,128)(2,1)S(1)} %collective-permute-done.24.refs_2_, ...), custom_call_target="tpu_custom_call" | custom-call | flops 2818572288 | bytes 2097152 | tf_op jit(solution)/shard_map/feed_forward/pallas_call | solution.py:435
  137.2 2.4 %collective-permute-start.22 = (bf16[16,64,256]{2,1,0:T(8,128)(2,1)S(1)}, bf16[16,64,256]{2,1,0:T(8,128)(2,1)S(1)}, u32[]{:S(2)}, u32[]{:S(2)}) collective-permute-start(bf16[16,64,256]{2,1,0:T(8,128)(2,1)S(1)} %add_up.5), channel_id=1, source_target_pairs={{0,96},{32,0},{64,32},{96,64},{1,97},{33,1},{65,33},{97,65},{2,98}... | collective-permute-start | bytes 1572872 | tf_op jit(solution)/shard_map/ppermute | solution.py:491
  139.7 2.0 %collective-permute-start.27 = (bf16[16,64,256]{2,1,0:T(8,128)(2,1)S(1)}, bf16[16,64,256]{2,1,0:T(8,128)(2,1)S(1)}, u32[]{:S(2)}, u32[]{:S(2)}) collective-permute-start(bf16[16,64,256]{2,1,0:T(8,128)(2,1)S(1)} %add_up.8), channel_id=1, source_target_pairs={{0,64},{32,96},{64,0},{96,32},{1,65},{33,97},{65,1},{97,33},{2,66}... | collective-permute-start | bytes 1572872 | tf_op jit(solution)/shard_map/ppermute | solution.py:491
  141.6 20.9 %collective-permute-done.22.refs_2_ = bf16[16,64,256]{2,1,0:T(8,128)(2,1)S(1)} collective-permute-done((bf16[16,64,256]{2,1,0:T(8,128)(2,1)S(1)}, bf16[16,64,256]{2,1,0:T(8,128)(2,1)S(1)}, u32[]{:S(2)}, u32[]{:S(2)}) %collective-permute-start.22) | collective-permute-done | bytes 524320 | tf_op jit(solution)/shard_map/ppermute | solution.py:491
  162.5 3.4 %collective-permute-done.23.refs_3_ = bf16[16,64,256]{2,1,0:T(8,128)(2,1)S(1)} collective-permute-done((bf16[16,64,256]{2,1,0:T(8,128)(2,1)S(1)}, bf16[16,64,256]{2,1,0:T(8,128)(2,1)S(1)}, u32[]{:S(2)}, u32[]{:S(2)}) %collective-permute-start.23) | collective-permute-done | bytes 524320 | tf_op jit(solution)/shard_map/ppermute | solution.py:491
  167.0 3.6 %all-to-all-start.1 = ((bf16[16,64,256]{2,1,0:T(8,128)(2,1)}), bf16[16,64,256]{2,1,0:T(8,128)(2,1)S(1)}, u32[]{:S(2)}, u32[]{:S(2)}) async-start(bf16[16,64,256]{2,1,0:T(8,128)(2,1)} %add_up.9), calls=%async_computation.1 | async-start | bytes 1048576 | tf_op jit(solution)/shard_map/all_to_all | solution.py:555
  170.8 11.0 %all-to-all-done.1.recv_ref = bf16[16,64,256]{2,1,0:T(8,128)(2,1)S(1)} async-done(((bf16[16,64,256]{2,1,0:T(8,128)(2,1)}), bf16[16,64,256]{2,1,0:T(8,128)(2,1)S(1)}, u32[]{:S(2)}, u32[]{:S(2)}) %all-to-all-start.1) | async-done | bytes 524320 | tf_op jit(solution)/shard_map/all_to_all | solution.py:555
  (82 shorter events, 34.2 us)
Async XLA Ops:
  6.5 40.3 %all-gather.4.cloned.1.call-start = ((), (), s32[]{:S(2)}) async-start(), calls=%async_computation.2 | async-start | bytes 4718592 | tf_op jit(solution)/shard_map/all_gather | solution.py:493
  51.0 9.7 %collective-permute-start = (bf16[4,128,256]{2,1,0:T(8,128)(2,1)S(1)}, bf16[4,128,256]{2,1,0:T(8,128)(2,1)S(1)}, u32[]{:S(2)}, u32[]{:S(2)}) collective-permute-start(bf16[4,128,256]{2,1,0:T(8,128)(2,1)S(1)} %get-tuple-element.59), channel_id=1, source_target_pairs={{0,1},{1,2},{2,3},{3,0},{4,5},{5,6},{6,7},{7,4},{8,9},{9,10},{10,1... | collective-permute-start | bytes 786440 | tf_op jit(solution)/shard_map/ppermute | solution.py:509
  52.7 14.9 %collective-permute-start.1 = (bf16[4,128,256]{2,1,0:T(8,128)(2,1)S(1)}, bf16[4,128,256]{2,1,0:T(8,128)(2,1)S(1)}, u32[]{:S(2)}, u32[]{:S(2)}) collective-permute-start(bf16[4,128,256]{2,1,0:T(8,128)(2,1)S(1)} %get-tuple-element.60), channel_id=1, source_target_pairs={{0,2},{1,3},{2,0},{3,1},{4,6},{5,7},{6,4},{7,5},{8,10},{9,11},{10,... | collective-permute-start | bytes 786440 | tf_op jit(solution)/shard_map/ppermute | solution.py:509
  55.5 12.1 %collective-permute-start.2 = (bf16[4,128,256]{2,1,0:T(8,128)(2,1)S(1)}, bf16[4,128,256]{2,1,0:T(8,128)(2,1)S(1)}, u32[]{:S(2)}, u32[]{:S(2)}) collective-permute-start(bf16[4,128,256]{2,1,0:T(8,128)(2,1)S(1)} %get-tuple-element.61), channel_id=1, source_target_pairs={{0,8},{4,12},{8,0},{12,4},{1,9},{5,13},{9,1},{13,5},{2,10},{6,14},... | collective-permute-start | bytes 786440 | tf_op jit(solution)/shard_map/ppermute | solution.py:509
  58.5 12.0 %collective-permute-start.3 = (bf16[4,128,256]{2,1,0:T(8,128)(2,1)S(1)}, bf16[4,128,256]{2,1,0:T(8,128)(2,1)S(1)}, u32[]{:S(2)}, u32[]{:S(2)}) collective-permute-start(bf16[4,128,256]{2,1,0:T(8,128)(2,1)S(1)} %get-tuple-element.62), channel_id=1, source_target_pairs={{0,4},{4,8},{8,12},{12,0},{1,5},{5,9},{9,13},{13,1},{2,6},{6,10},{... | collective-permute-start | bytes 786440 | tf_op jit(solution)/shard_map/ppermute | solution.py:509
  59.1 11.5 %collective-permute-start.4 = (bf16[4,128,256]{2,1,0:T(8,128)(2,1)S(1)}, bf16[4,128,256]{2,1,0:T(8,128)(2,1)S(1)}, u32[]{:S(2)}, u32[]{:S(2)}) collective-permute-start(bf16[4,128,256]{2,1,0:T(8,128)(2,1)S(1)} %get-tuple-element.63), channel_id=1, source_target_pairs={{0,3},{1,0},{2,1},{3,2},{4,7},{5,4},{6,5},{7,6},{8,11},{9,8},{10,9... | collective-permute-start | bytes 786440 | tf_op jit(solution)/shard_map/ppermute | solution.py:509
  60.8 9.8 %collective-permute-start.5 = (bf16[4,128,256]{2,1,0:T(8,128)(2,1)S(1)}, bf16[4,128,256]{2,1,0:T(8,128)(2,1)S(1)}, u32[]{:S(2)}, u32[]{:S(2)}) collective-permute-start(bf16[4,128,256]{2,1,0:T(8,128)(2,1)S(1)} %get-tuple-element.64), channel_id=1, source_target_pairs={{0,12},{4,0},{8,4},{12,8},{1,13},{5,1},{9,5},{13,9},{2,14},{6,2},{... | collective-permute-start | bytes 786440 | tf_op jit(solution)/shard_map/ppermute | solution.py:509
  71.4 7.0 %collective-permute-start.6 = (bf16[128,256]{1,0:T(8,128)(2,1)S(1)}, bf16[128,256]{1,0:T(8,128)(2,1)S(1)}, u32[]{:S(2)}, u32[]{:S(2)}) collective-permute-start(bf16[128,256]{1,0:T(8,128)(2,1)S(1)} %get-tuple-element.67), channel_id=1, source_target_pairs={{0,4},{4,8},{8,12},{12,0},{1,5},{5,9},{9,13},{13,1},{2,6},{6,10},{... | collective-permute-start | bytes 196616 | tf_op jit(solution)/shard_map/ppermute | solution.py:509
  73.0 7.3 %collective-permute-start.7 = (bf16[128,256]{1,0:T(8,128)(2,1)S(1)}, bf16[128,256]{1,0:T(8,128)(2,1)S(1)}, u32[]{:S(2)}, u32[]{:S(2)}) collective-permute-start(bf16[128,256]{1,0:T(8,128)(2,1)S(1)} %get-tuple-element.68), channel_id=1, source_target_pairs={{0,8},{4,12},{8,0},{12,4},{1,9},{5,13},{9,1},{13,5},{2,10},{6,14},... | collective-permute-start | bytes 196616 | tf_op jit(solution)/shard_map/ppermute | solution.py:509
  75.8 5.8 %collective-permute-start.8 = (bf16[128,256]{1,0:T(8,128)(2,1)S(1)}, bf16[128,256]{1,0:T(8,128)(2,1)S(1)}, u32[]{:S(2)}, u32[]{:S(2)}) collective-permute-start(bf16[128,256]{1,0:T(8,128)(2,1)S(1)} %get-tuple-element.69), channel_id=1, source_target_pairs={{0,2},{1,3},{2,0},{3,1},{4,6},{5,7},{6,4},{7,5},{8,10},{9,11},{10,... | collective-permute-start | bytes 196616 | tf_op jit(solution)/shard_map/ppermute | solution.py:509
  76.9 5.5 %collective-permute-start.9 = (bf16[128,256]{1,0:T(8,128)(2,1)S(1)}, bf16[128,256]{1,0:T(8,128)(2,1)S(1)}, u32[]{:S(2)}, u32[]{:S(2)}) collective-permute-start(bf16[128,256]{1,0:T(8,128)(2,1)S(1)} %get-tuple-element.70), channel_id=1, source_target_pairs={{0,1},{1,2},{2,3},{3,0},{4,5},{5,6},{6,7},{7,4},{8,9},{9,10},{10,1... | collective-permute-start | bytes 196616 | tf_op jit(solution)/shard_map/ppermute | solution.py:509
  78.2 4.3 %collective-permute-start.10 = (bf16[128,256]{1,0:T(8,128)(2,1)S(1)}, bf16[128,256]{1,0:T(8,128)(2,1)S(1)}, u32[]{:S(2)}, u32[]{:S(2)}) collective-permute-start(bf16[128,256]{1,0:T(8,128)(2,1)S(1)} %get-tuple-element.71), channel_id=1, source_target_pairs={{0,12},{4,0},{8,4},{12,8},{1,13},{5,1},{9,5},{13,9},{2,14},{6,2},{... | collective-permute-start | bytes 196616 | tf_op jit(solution)/shard_map/ppermute | solution.py:509
  78.4 4.3 %collective-permute-start.11 = (bf16[128,256]{1,0:T(8,128)(2,1)S(1)}, bf16[128,256]{1,0:T(8,128)(2,1)S(1)}, u32[]{:S(2)}, u32[]{:S(2)}) collective-permute-start(bf16[128,256]{1,0:T(8,128)(2,1)S(1)} %get-tuple-element.72), channel_id=1, source_target_pairs={{0,3},{1,0},{2,1},{3,2},{4,7},{5,4},{6,5},{7,6},{8,11},{9,8},{10,9... | collective-permute-start | bytes 196616 | tf_op jit(solution)/shard_map/ppermute | solution.py:509
  99.0 13.8 %collective-permute-start.12 = (bf16[64,4096]{1,0:T(8,128)(2,1)S(1)}, bf16[64,4096]{1,0:T(8,128)(2,1)S(1)}, u32[]{:S(2)}, u32[]{:S(2)}) collective-permute-start(bf16[64,4096]{1,0:T(8,128)(2,1)S(1)} %normalize.1.after_ref.refs_0_), channel_id=1, source_target_pairs={{0,16},{16,0},{1,17},{17,1},{2,18},{18,2},{3,19},{19,3},{4,20},{20... | collective-permute-start | bytes 1572872 | tf_op jit(solution)/shard_map/ppermute | solution.py:488
  99.1 18.8 %collective-permute-start.13 = (bf16[64,4096]{1,0:T(8,128)(2,1)S(1)}, bf16[64,4096]{1,0:T(8,128)(2,1)S(1)}, u32[]{:S(2)}, u32[]{:S(2)}) collective-permute-start(bf16[64,4096]{1,0:T(8,128)(2,1)S(1)} %normalize.1.after_ref.refs_0_), channel_id=1, source_target_pairs={{0,32},{32,64},{64,96},{96,0},{1,33},{33,65},{65,97},{97,1},{2,34}... | collective-permute-start | bytes 1572872 | tf_op jit(solution)/shard_map/ppermute | solution.py:491
  104.2 14.0 %collective-permute-start.14 = (bf16[64,4096]{1,0:T(8,128)(2,1)S(1)}, bf16[64,4096]{1,0:T(8,128)(2,1)S(1)}, u32[]{:S(2)}, u32[]{:S(2)}) collective-permute-start(bf16[64,4096]{1,0:T(8,128)(2,1)S(1)} %normalize.1.after_ref.refs_0_), channel_id=1, source_target_pairs={{0,96},{32,0},{64,32},{96,64},{1,97},{33,1},{65,33},{97,65},{2,98}... | collective-permute-start | bytes 1572872 | tf_op jit(solution)/shard_map/ppermute | solution.py:491
  118.2 3.9 %collective-permute-start.15 = (bf16[64,4096]{1,0:T(8,128)(2,1)S(1)}, bf16[64,4096]{1,0:T(8,128)(2,1)S(1)}, u32[]{:S(2)}, u32[]{:S(2)}) collective-permute-start(bf16[64,4096]{1,0:T(8,128)(2,1)S(1)} %collective-permute-done.13.refs_0_), channel_id=1, source_target_pairs={{0,16},{16,0},{1,17},{17,1},{2,18},{18,2},{3,19},{19,3},{4,20},{20... | collective-permute-start | bytes 1572872 | tf_op jit(solution)/shard_map/ppermute | solution.py:488
  118.2 3.9 %collective-permute-start.16 = (bf16[16,64,256]{2,1,0:T(8,128)(2,1)S(1)}, bf16[16,64,256]{2,1,0:T(8,128)(2,1)S(1)}, u32[]{:S(2)}, u32[]{:S(2)}) collective-permute-start(bf16[16,64,256]{2,1,0:T(8,128)(2,1)S(1)} %get-tuple-element.86), channel_id=1, source_target_pairs={{0,16},{16,0},{1,17},{17,1},{2,18},{18,2},{3,19},{19,3},{4,20},{20... | collective-permute-start | bytes 1572872 | tf_op jit(solution)/shard_map/ppermute | solution.py:488
  118.8 10.5 %collective-permute-start.18 = (bf16[32,4096]{1,0:T(8,128)(2,1)S(1)}, bf16[32,4096]{1,0:T(8,128)(2,1)S(1)}, u32[]{:S(2)}, u32[]{:S(2)}) collective-permute-start(bf16[32,4096]{1,0:T(8,128)(2,1)S(1)} %slice.6), channel_id=1, source_target_pairs={{0,32},{32,64},{64,96},{96,0},{1,33},{33,65},{65,97},{97,1},{2,34}... | collective-permute-start | bytes 786440 | tf_op jit(solution)/shard_map/ppermute | solution.py:491
  119.7 9.6 %collective-permute-start.19 = (bf16[32,4096]{1,0:T(8,128)(2,1)S(1)}, bf16[32,4096]{1,0:T(8,128)(2,1)S(1)}, u32[]{:S(2)}, u32[]{:S(2)}) collective-permute-start(bf16[32,4096]{1,0:T(8,128)(2,1)S(1)} %slice.7), channel_id=1, source_target_pairs={{0,96},{32,0},{64,32},{96,64},{1,97},{33,1},{65,33},{97,65},{2,98}... | collective-permute-start | bytes 786440 | tf_op jit(solution)/shard_map/ppermute | solution.py:491
  137.2 25.3 %collective-permute-start.22 = (bf16[16,64,256]{2,1,0:T(8,128)(2,1)S(1)}, bf16[16,64,256]{2,1,0:T(8,128)(2,1)S(1)}, u32[]{:S(2)}, u32[]{:S(2)}) collective-permute-start(bf16[16,64,256]{2,1,0:T(8,128)(2,1)S(1)} %add_up.5), channel_id=1, source_target_pairs={{0,96},{32,0},{64,32},{96,64},{1,97},{33,1},{65,33},{97,65},{2,98}... | collective-permute-start | bytes 1572872 | tf_op jit(solution)/shard_map/ppermute | solution.py:491
  139.5 26.4 %collective-permute-start.23 = (bf16[16,64,256]{2,1,0:T(8,128)(2,1)S(1)}, bf16[16,64,256]{2,1,0:T(8,128)(2,1)S(1)}, u32[]{:S(2)}, u32[]{:S(2)}) collective-permute-start(bf16[16,64,256]{2,1,0:T(8,128)(2,1)S(1)} %add_up.6), channel_id=1, source_target_pairs={{0,32},{32,64},{64,96},{96,0},{1,33},{33,65},{65,97},{97,1},{2,34}... | collective-permute-start | bytes 1572872 | tf_op jit(solution)/shard_map/ppermute | solution.py:491
  139.7 26.5 %collective-permute-start.27 = (bf16[16,64,256]{2,1,0:T(8,128)(2,1)S(1)}, bf16[16,64,256]{2,1,0:T(8,128)(2,1)S(1)}, u32[]{:S(2)}, u32[]{:S(2)}) collective-permute-start(bf16[16,64,256]{2,1,0:T(8,128)(2,1)S(1)} %add_up.8), channel_id=1, source_target_pairs={{0,64},{32,96},{64,0},{96,32},{1,65},{33,97},{65,1},{97,33},{2,66}... | collective-permute-start | bytes 1572872 | tf_op jit(solution)/shard_map/ppermute | solution.py:491
  167.0 14.7 %all-to-all-start.1 = ((bf16[16,64,256]{2,1,0:T(8,128)(2,1)}), bf16[16,64,256]{2,1,0:T(8,128)(2,1)S(1)}, u32[]{:S(2)}, u32[]{:S(2)}) async-start(bf16[16,64,256]{2,1,0:T(8,128)(2,1)} %add_up.9), calls=%async_computation.1 | async-start | bytes 1048576 | tf_op jit(solution)/shard_map/all_to_all | solution.py:555
  (12 other events, 172.5 us)
Sparse Core Ops, SparseCore 0:
  9.1 37.7 all-gather.3

commit v6 on v5

--- a/solution.py
+++ b/solution.py
@@ -94,10 +94,24 @@
             pre_ref[b, :, lanes] = jnp.where(sub >= 1, pltpu.roll(width, 1, 0), 0.0)
 
 
+def pair_up(core_ref, own_ref, sib_ref, rate_ref, out_ref):
+    states = rate_ref.shape[0]
+    low = core_ref[0] == 0
+    rate = rate_ref[...] * -LOG2E
+    for b in range(own_ref.shape[0]):
+        first = jnp.where(low, own_ref[b], sib_ref[b])
+        second = jnp.where(low, sib_ref[b], own_ref[b])
+        decay = jnp.exp2(rate * second[states:])
+        out_ref[b, :states] = decay * first[:states] + second[:states]
+        out_ref[b, states:] = first[states:] + second[states:]
+
+
 def second_pass(
-    coords_ref, step_ref, sig_ref, gate_ref, into_ref, outof_ref, rate_ref, skip_ref, before_ref, pre_ref,
-    ends_ref, mixed_ref, st4, v4, y4, into_b, outof_b, enter,
+    core_ref, step_ref, sig_ref, gate_ref, into_ref, outof_ref, rate_ref, skip_ref, before_ref, pre_ref,
+    *rest, earlier,
 ):
+    sib_ref, *pair_refs = rest[: earlier + 1]
+    mixed_ref, st4, v4, y4, into_b, outof_b, enter = rest[earlier + 1 :]
     states, channels = rate_ref.shape
     prompts = pre_ref.shape[0]
     turns = into_ref.shape[0]
@@ -105,18 +119,17 @@
     spread(into_ref, into_b)
     spread(outof_ref, outof_b)
     split_lanes(step_ref, sig_ref, st4, v4)
-    mine = coords_ref[0]
+    live = jnp.where(core_ref[0] > 0, 1.0, 0.0).astype(f32)
     for q in range(channels // LANES):
         lanes = slice(q * LANES, (q + 1) * LANES)
         rate_q = rate_ref[:, lanes] * -LOG2E
         rates = [jnp.broadcast_to(rate_q[n : n + 1], (SUBS, LANES)) for n in range(states)]
         for b in range(prompts):
             h0 = jnp.zeros((states, LANES), f32)
-            for c in range(ends_ref.shape[0] - 1):
-                live = jnp.where(c < mine, 1.0, 0.0).astype(f32)
-                decay = jnp.exp2(rate_q * (ends_ref[c, b, states : states + 1, lanes] * live))
-                h0 = decay * h0 + ends_ref[c, b, :states, lanes] * live
-            enter[...] = h0
+            for pair in pair_refs:
+                h0 = jnp.exp2(rate_q * pair[b, states : states + 1, lanes]) * h0 + pair[b, :states, lanes]
+            decay = jnp.exp2(rate_q * (sib_ref[b, states : states + 1, lanes] * live))
+            enter[...] = decay * h0 + sib_ref[b, :states, lanes] * live
             pre = pre_ref[b, :, lanes]
             hs = tuple(
                 before_ref[b, n, :, lanes]
@@ -325,15 +338,26 @@
     )(step, sig, into, rate)
 
 
-def run_second(coords, step, sig, gate, into, outof, rate, skip, before, pre, ends):
+def run_pair(core, own, sib, rate):
+    return pl.pallas_call(
+        pair_up,
+        out_shape=jax.ShapeDtypeStruct(own.shape, f32),
+        in_specs=[smem()] + [vmem()] * 3,
+        out_specs=vmem(),
+        compiler_params=params(8),
+        name="pair_up",
+    )(core, own, sib, rate)
+
+
+def run_second(core, step, sig, gate, into, outof, rate, skip, before, pre, sib, pairs):
     tokens, channels = step.shape
     prompts, states = before.shape[:2]
     turns = into.shape[0]
     tiles = channels // LANES
     return pl.pallas_call(
-        second_pass,
+        functools.partial(second_pass, earlier=len(pairs)),
         out_shape=jax.ShapeDtypeStruct((tokens, channels), bf16),
-        in_specs=[smem()] + [vmem()] * 10,
+        in_specs=[smem()] + [vmem()] * (10 + len(pairs)),
         out_specs=vmem(),
         scratch_shapes=[
             pltpu.VMEM((tiles, tokens, LANES), f32),
@@ -346,7 +370,7 @@
         compiler_params=params(16),
         cost_estimate=pl.CostEstimate(flops=2 * 10**9, bytes_accessed=2 * MIB, transcendentals=0),
         name="scan_second",
-    )(coords, step, sig, gate, into, outof, rate, skip, before, pre, ends)
+    )(core, step, sig, gate, into, outof, rate, skip, before, pre, sib, *pairs)
 
 
 def run_project(coords, mixed, ids, proj, share, sides):
@@ -495,12 +519,17 @@
     step = step_size.reshape(tokens, channels)
     into = scan_tables(state_in, turns)
     end, before, pre = run_first(step, sig, into, decay_rate, prompts)
-    ends = lax.all_gather(end, ctx)
-    coords = jnp.stack([lax.axis_index(a).astype(jnp.int32) for a in (ctx, "x", "z")])
+    coords = jnp.stack([lax.axis_index(a).astype(jnp.int32) for a in ("core", "x", "z")])
+    sib = swap(end)
+    pair = run_pair(coords, end, sib, decay_rate)
+    gate_in, state_out, pair = lax.optimization_barrier((gate_in, state_out, pair))
+    pairs = [
+        lax.ppermute(pair, "y", [(i, i + d) for i in range(chips - d)]) for d in range(chips - 1, 0, -1)
+    ]
     gate = gate_in.reshape(tokens, channels)
     outof = scan_tables(state_out, turns)
     mixed = run_second(
-        coords, step, sig, gate, into, outof, decay_rate, skip.reshape(1, channels), before, pre, ends
+        coords, step, sig, gate, into, outof, decay_rate, skip.reshape(1, channels), before, pre, sib, pairs
     )
     sides = (lax.axis_size("x"), lax.axis_size("z"))
 

time: 191 us -> 186 us (0.974)
  blocking collectives: 31.2 us -> 15.6 us
  starting transfers between devices: 40.3 us -> 47.1 us
  waiting for transfers between devices: 51.6 us -> 55.1 us
    all_gather x1 -> x0, blocking collectives: 15.6 us -> none  [on_device(): ends = lax.all_gather(end, ctx)]
    ppermute x0 -> x3, starting transfers between devices: none -> 9.07 us  [on_device(): lax.ppermute(pair, 'y', [(i, i + d) for i in range(chips - d)])]
    ppermute x0 -> x3, waiting for transfers between devices: none -> 3.43 us  [on_device(): lax.ppermute(pair, 'y', [(i, i + d) for i in range(chips - d)])]
    ppermute x7, starting transfers between devices: 14 us -> 11.8 us  [ring(): lax.ppermute(value, 'y', [(i, (i + d) % chips) for i in range(chips)])]
    pallas_call x1 -> x2, Pallas kernels: 7.17 us -> 7.72 us  [the longest x1 7.15 us: run_second(): pl.pallas_call(functools.partial(second_pass, earlier=len(pairs)), out_sh...]
  transfers between devices with their start and end apart: 30 -> 34, of which waited for: 17 -> 19; matrix products, arithmetic and copies ran while one was open for 3% -> 4% of each run, Pallas kernels for 17% -> 18%
where the time goes in v6:
time: 186 us; the launch traced here: 185 us
  waiting for transfers between devices  55.1 us (30%)
  starting transfers between devices  47.1 us (25%)
  Pallas kernels  44.3 us (24%)
  blocking collectives  15.6 us (8%)
  between operations  13.7 us (7%)
  local copies, waits for them, and re-layouts  9.47 us (5%)
    ppermute x7, waiting for transfers between devices, ring(): lax.ppermute(value, 'y', [(i, (i + d) % chips) for i in range(chips)])  25.5 us
    ppermute x12, starting transfers between devices, shift(): lax.ppermute(value, axis, [(i, (i + d) % n) for i in range(n)])  20.8 us
    all_to_all x1, blocking collectives, on_device(): whole = lax.all_to_all(slot_rows, exp, 0, 0, tiled=True)  15.6 us
    pallas_call x3, Pallas kernels, run_ffn(): pl.pallas_call(functools.partial(feed_forward, groups=tuple(((len(own), l...  15.2 us
    ppermute x7, starting transfers between devices, ring(): lax.ppermute(value, 'y', [(i, (i + d) % chips) for i in range(chips)])  11.8 us
    all_to_all x1, waiting for transfers between devices, on_device(): back = lax.all_to_all(returned, exp, 0, 0, tiled=True)  11 us
    ppermute x12, waiting for transfers between devices, shift(): lax.ppermute(value, axis, [(i, (i + d) % n) for i in range(n)])  9.95 us
    ppermute x3, starting transfers between devices, on_device(): lax.ppermute(pair, 'y', [(i, i + d) for i in range(chips - d)])  9.07 us
  transfers between devices with their start and end apart: 34, of which 19 were waited for; matrix products, arithmetic and copies ran while one was open for 4% of the time, Pallas kernels for 18%

profile of v6, /device:TPU:0, one launch (start us, length us, event | category | flops | bytes accessed | tf_op | source)
XLA Modules:
  0.0 185.4 jit_solution(18055832044335418222)
XLA Ops:
  11.4 6.1 %scan_first.1 = (f32[2,17,512]{2,1,0:T(8,128)S(1)}, f32[2,16,8,512]{3,2,1,0:T(8,128)S(1)}, f32[2,8,512]{2,1,0:T(8,128)S(1)}) custom-call(f32[256,512]{1,0:T(8,128)S(1)} %reshape.33.step_ref, bf16[256,512]{1,0:T(8,128)(2,1)S(1)} %reshape.34.sig_ref, f32[16,8,32]{2,1,0:T(8,128)S(1)} %bitcast.22, f32[16,512]{1,0:T(8,128)S(1)} %copy-done), custom_call_target="tpu_custom_call" | custom-call | tf_op jit(solution)/shard_map/scan_first/pallas_call | solution.py:322
  19.5 5.0 %collective-permute-start.1 = (f32[2,17,512]{2,1,0:T(8,128)S(1)}, f32[2,17,512]{2,1,0:T(8,128)S(1)}, u32[]{:S(2)}, u32[]{:S(2)}) collective-permute-start(f32[2,17,512]{2,1,0:T(8,128)S(1)} %pair_up.1), channel_id=1, source_target_pairs={{0,96},{1,97},{2,98},{3,99},{4,100},{5,101},{6,102},{7,103},{8,104... | collective-permute-start | bytes 208904 | tf_op jit(solution)/shard_map/ppermute | solution.py:527
  25.8 2.8 %collective-permute-start.3 = (f32[2,17,512]{2,1,0:T(8,128)S(1)}, f32[2,17,512]{2,1,0:T(8,128)S(1)}, u32[]{:S(2)}, u32[]{:S(2)}) collective-permute-start(f32[2,17,512]{2,1,0:T(8,128)S(1)} %pair_up.1), channel_id=1, source_target_pairs={{0,32},{32,64},{64,96},{1,33},{33,65},{65,97},{2,34},{34,66},{66,9... | collective-permute-start | bytes 208904 | tf_op jit(solution)/shard_map/ppermute | solution.py:527
  31.6 3.4 %collective-permute-done.3.rest_3_ = f32[2,17,512]{2,1,0:T(8,128)S(1)} collective-permute-done((f32[2,17,512]{2,1,0:T(8,128)S(1)}, f32[2,17,512]{2,1,0:T(8,128)S(1)}, u32[]{:S(2)}, u32[]{:S(2)}) %collective-permute-start.3) | collective-permute-done | bytes 69664 | tf_op jit(solution)/shard_map/ppermute | solution.py:527
  36.4 7.2 %scan_second.1.mixed_ref = bf16[256,512]{1,0:T(8,128)(2,1)S(1)} custom-call(s32[3]{0:T(128)S(1)} %pad_add_fusion.core_ref.coords_ref, f32[256,512]{1,0:T(8,128)S(1)} %reshape.33.step_ref, bf16[256,512]{1,0:T(8,128)(2,1)S(1)} %reshape.34.sig_ref, bf16[256,512]{1,0:T(8,128)(2,1)S(1)} %reshape.36.gate_ref, f32[16,8,32]{2,1,0:T(8,128)S(1)} %bitcast.23, ...), custom_call_target="tpu_custom_call" | custom-call | flops 2000000000 | bytes 2097152 | tf_op jit(solution)/shard_map/scan_second/pallas_call | solution.py:357
  44.8 4.2 %project.1 = (bf16[4,128,256]{2,1,0:T(8,128)(2,1)S(1)}, bf16[4,128,256]{2,1,0:T(8,128)(2,1)S(1)}, bf16[4,128,256]{2,1,0:T(8,128)(2,1)S(1)}, bf16[4,128,256]{2,1,...) custom-call(s32[3]{0:T(128)S(1)} %pad_add_fusion.core_ref.coords_ref, ...), custom_call_target="tpu_custom_call" | custom-call | tf_op jit(solution)/shard_map/project/pallas_call | solution.py:380
  50.6 2.9 %collective-permute-start.5 = (bf16[4,128,256]{2,1,0:T(8,128)(2,1)S(1)}, bf16[4,128,256]{2,1,0:T(8,128)(2,1)S(1)}, u32[]{:S(2)}, u32[]{:S(2)}) collective-permute-start(bf16[4,128,256]{2,1,0:T(8,128)(2,1)S(1)} %get-tuple-element.66), channel_id=1, source_target_pairs={{0,2},{1,3},{2,0},{3,1},{4,6},{5,7},{6,4},{7,5},{8,10},{9,11},{10,... | collective-permute-start | bytes 786440 | tf_op jit(solution)/shard_map/ppermute | solution.py:538
  53.5 2.9 %collective-permute-start.6 = (bf16[4,128,256]{2,1,0:T(8,128)(2,1)S(1)}, bf16[4,128,256]{2,1,0:T(8,128)(2,1)S(1)}, u32[]{:S(2)}, u32[]{:S(2)}) collective-permute-start(bf16[4,128,256]{2,1,0:T(8,128)(2,1)S(1)} %get-tuple-element.67), channel_id=1, source_target_pairs={{0,8},{4,12},{8,0},{12,4},{1,9},{5,13},{9,1},{13,5},{2,10},{6,14},... | collective-permute-start | bytes 786440 | tf_op jit(solution)/shard_map/ppermute | solution.py:538
  58.7 2.6 %collective-permute-start.9 = (bf16[4,128,256]{2,1,0:T(8,128)(2,1)S(1)}, bf16[4,128,256]{2,1,0:T(8,128)(2,1)S(1)}, u32[]{:S(2)}, u32[]{:S(2)}) collective-permute-start(bf16[4,128,256]{2,1,0:T(8,128)(2,1)S(1)} %get-tuple-element.70), channel_id=1, source_target_pairs={{0,12},{4,0},{8,4},{12,8},{1,13},{5,1},{9,5},{13,9},{2,14},{6,2},{... | collective-permute-start | bytes 786440 | tf_op jit(solution)/shard_map/ppermute | solution.py:538
  61.4 4.2 %collective-permute-done.5.rest_1_ = bf16[4,128,256]{2,1,0:T(8,128)(2,1)S(1)} collective-permute-done((bf16[4,128,256]{2,1,0:T(8,128)(2,1)S(1)}, bf16[4,128,256]{2,1,0:T(8,128)(2,1)S(1)}, u32[]{:S(2)}, u32[]{:S(2)}) %collective-permute-start.5) | collective-permute-done | bytes 262176 | tf_op jit(solution)/shard_map/ppermute | solution.py:538
  65.5 3.0 %collective-permute-done.7.rest_3_ = bf16[4,128,256]{2,1,0:T(8,128)(2,1)S(1)} collective-permute-done((bf16[4,128,256]{2,1,0:T(8,128)(2,1)S(1)}, bf16[4,128,256]{2,1,0:T(8,128)(2,1)S(1)}, u32[]{:S(2)}, u32[]{:S(2)}) %collective-permute-start.7) | collective-permute-done | bytes 262176 | tf_op jit(solution)/shard_map/ppermute | solution.py:538
  70.9 2.9 %collective-permute-start.11 = (bf16[128,256]{1,0:T(8,128)(2,1)S(1)}, bf16[128,256]{1,0:T(8,128)(2,1)S(1)}, u32[]{:S(2)}, u32[]{:S(2)}) collective-permute-start(bf16[128,256]{1,0:T(8,128)(2,1)S(1)} %get-tuple-element.74), channel_id=1, source_target_pairs={{0,8},{4,12},{8,0},{12,4},{1,9},{5,13},{9,1},{13,5},{2,10},{6,14},... | collective-permute-start | bytes 196616 | tf_op jit(solution)/shard_map/ppermute | solution.py:538
  81.0 15.6 %all_to_all.10.recv_ref = bf16[16,64,256]{2,1,0:T(8,128)(2,1)S(1)} all-to-all(bf16[16,64,256]{2,1,0:T(8,128)(2,1)S(1)} %get-tuple-element.82), channel_id=1, replica_groups=mesh['y'=4,'core'=2,'x'=4,'z'=4] {'x','z'}, dimensions={0} | all-to-all | bytes 1048576 | tf_op jit(solution)/shard_map/all_to_all | solution.py:556
  97.0 2.5 %collective-permute-start.17 = (bf16[64,4096]{1,0:T(8,128)(2,1)S(1)}, bf16[64,4096]{1,0:T(8,128)(2,1)S(1)}, u32[]{:S(2)}, u32[]{:S(2)}) collective-permute-start(bf16[64,4096]{1,0:T(8,128)(2,1)S(1)} %normalize.1.after_ref.refs_0_), channel_id=1, source_target_pairs={{0,32},{32,64},{64,96},{96,0},{1,33},{33,65},{65,97},{97,1},{2,34}... | collective-permute-start | bytes 1572872 | tf_op jit(solution)/shard_map/ppermute | solution.py:515
  101.0 7.3 %load_weights.1 = (bf16[4096,896]{1,0:T(8,128)(2,1)S(1)}, bf16[4096,896]{1,0:T(8,128)(2,1)S(1)}, bf16[896,4096]{1,0:T(8,128)(2,1)S(1)}, f32[8,128]{1,0:T(8,128)S(1)}) custom-call(bf16[64,4096]{1,0:T(8,128)(2,1)S(1)} %normalize.1.after_ref.refs_0_, bf16[4096,896]{1,0:T(8,128)(2,1)} %bitcast.27, bf16[4096,896]{1,0:T(8,128)(2,1)} %bitcast.28, ...), custom_call_target="tpu_custom_call" | custom-call | bytes 44040192 | tf_op jit(solution)/shard_map/load_weights/pallas_call | solution.py:439
  108.3 3.8 %feed_forward.3 = (bf16[16,64,256]{2,1,0:T(8,128)(2,1)S(1)}, bf16[16,64,256]{2,1,0:T(8,128)(2,1)S(1)}, f32[8,128]{1,0:T(8,128)S(1)}) custom-call(bf16[64,4096]{1,0:T(8,128)(2,1)S(1)} %normalize.1.after_ref.refs_0_, bf16[64,4096]{1,0:T(8,128)(2,1)S(1)} %collective-permute-done.16.refs_1_, bf16[4096,896]{1,0:T(8,128)(2,1)S(1)} %get-tuple-element.85.refs_2_.refs_4_, ...), custom_call_target="tpu_custom_call" | custom-call | flops 2818572288 | bytes 2097152 | tf_op jit(solution)/shard_map/feed_forward/pallas_call | solution.py:459
  117.4 7.2 %feed_forward.4 = (bf16[16,64,256]{2,1,0:T(8,128)(2,1)S(1)}, bf16[16,64,256]{2,1,0:T(8,128)(2,1)S(1)}, bf16[16,64,256]{2,1,0:T(8,128)(2,1)S(1)}, bf16[16,64,256]{2,1,0:T(8,128)(2,1)S(1)}, f32[8,128]{1,0:T(8,128)S(1)}) custom-call(bf16[64,4096]{1,0:T(8,128)(2,1)S(1)} %collective-permute-done.17.refs_0_, bf16[64,4096]{1,0:T(8,128)(2,1)S(1)} %collective-permute-done.19.refs_1_, ...), custom_call_target="tpu_custom_call" | custom-call | flops 5637144576 | bytes 4194304 | tf_op jit(solution)/shard_map/feed_forward/pallas_call | solution.py:459
  128.1 4.2 %feed_forward.5 = (bf16[16,64,256]{2,1,0:T(8,128)(2,1)S(1)}, bf16[16,64,256]{2,1,0:T(8,128)(2,1)S(1)}, f32[8,128]{1,0:T(8,128)}) custom-call(bf16[32,4096]{1,0:T(8,128)(2,1)S(1)} %collective-permute-done.22.refs_0_, bf16[32,4096]{1,0:T(8,128)(2,1)S(1)} %collective-permute-done.23.refs_1_, bf16[32,4096]{1,0:T(8,128)(2,1)S(1)} %collective-permute-done.28.refs_2_, ...), custom_call_target="tpu_custom_call" | custom-call | flops 2818572288 | bytes 2097152 | tf_op jit(solution)/shard_map/feed_forward/pallas_call | solution.py:459
  132.5 2.4 %collective-permute-start.26 = (bf16[16,64,256]{2,1,0:T(8,128)(2,1)S(1)}, bf16[16,64,256]{2,1,0:T(8,128)(2,1)S(1)}, u32[]{:S(2)}, u32[]{:S(2)}) collective-permute-start(bf16[16,64,256]{2,1,0:T(8,128)(2,1)S(1)} %add_up.5), channel_id=1, source_target_pairs={{0,96},{32,0},{64,32},{96,64},{1,97},{33,1},{65,33},{97,65},{2,98}... | collective-permute-start | bytes 1572872 | tf_op jit(solution)/shard_map/ppermute | solution.py:515
  135.0 2.1 %collective-permute-start.31 = (bf16[16,64,256]{2,1,0:T(8,128)(2,1)S(1)}, bf16[16,64,256]{2,1,0:T(8,128)(2,1)S(1)}, u32[]{:S(2)}, u32[]{:S(2)}) collective-permute-start(bf16[16,64,256]{2,1,0:T(8,128)(2,1)S(1)} %add_up.8), channel_id=1, source_target_pairs={{0,64},{32,96},{64,0},{96,32},{1,65},{33,97},{65,1},{97,33},{2,66}... | collective-permute-start | bytes 1572872 | tf_op jit(solution)/shard_map/ppermute | solution.py:515
  137.1 20.8 %collective-permute-done.26.refs_2_ = bf16[16,64,256]{2,1,0:T(8,128)(2,1)S(1)} collective-permute-done((bf16[16,64,256]{2,1,0:T(8,128)(2,1)S(1)}, bf16[16,64,256]{2,1,0:T(8,128)(2,1)S(1)}, u32[]{:S(2)}, u32[]{:S(2)}) %collective-permute-start.26) | collective-permute-done | bytes 524320 | tf_op jit(solution)/shard_map/ppermute | solution.py:515
  157.9 3.4 %collective-permute-done.27.refs_3_ = bf16[16,64,256]{2,1,0:T(8,128)(2,1)S(1)} collective-permute-done((bf16[16,64,256]{2,1,0:T(8,128)(2,1)S(1)}, bf16[16,64,256]{2,1,0:T(8,128)(2,1)S(1)}, u32[]{:S(2)}, u32[]{:S(2)}) %collective-permute-start.27) | collective-permute-done | bytes 524320 | tf_op jit(solution)/shard_map/ppermute | solution.py:515
  162.4 3.6 %all-to-all-start.1 = ((bf16[16,64,256]{2,1,0:T(8,128)(2,1)}), bf16[16,64,256]{2,1,0:T(8,128)(2,1)S(1)}, u32[]{:S(2)}, u32[]{:S(2)}) async-start(bf16[16,64,256]{2,1,0:T(8,128)(2,1)} %add_up.9), calls=%async_computation.1 | async-start | bytes 1048576 | tf_op jit(solution)/shard_map/all_to_all | solution.py:584
  166.1 11.0 %all-to-all-done.1.recv_ref = bf16[16,64,256]{2,1,0:T(8,128)(2,1)S(1)} async-done(((bf16[16,64,256]{2,1,0:T(8,128)(2,1)}), bf16[16,64,256]{2,1,0:T(8,128)(2,1)S(1)}, u32[]{:S(2)}, u32[]{:S(2)}) %all-to-all-start.1) | async-done | bytes 524320 | tf_op jit(solution)/shard_map/all_to_all | solution.py:584
  (90 shorter events, 40.8 us)
Async XLA Ops:
  6.5 38.2 %all-gather.3.cloned.1.call-start = ((), (), s32[]{:S(2)}) async-start(), calls=%async_computation.2 | async-start | bytes 4718592 | tf_op jit(solution)/shard_map/all_gather | solution.py:517
  19.5 12.0 %collective-permute-start.1 = (f32[2,17,512]{2,1,0:T(8,128)S(1)}, f32[2,17,512]{2,1,0:T(8,128)S(1)}, u32[]{:S(2)}, u32[]{:S(2)}) collective-permute-start(f32[2,17,512]{2,1,0:T(8,128)S(1)} %pair_up.1), channel_id=1, source_target_pairs={{0,96},{1,97},{2,98},{3,99},{4,100},{5,101},{6,102},{7,103},{8,104... | collective-permute-start | bytes 208904 | tf_op jit(solution)/shard_map/ppermute | solution.py:527
  24.5 7.0 %collective-permute-start.2 = (f32[2,17,512]{2,1,0:T(8,128)S(1)}, f32[2,17,512]{2,1,0:T(8,128)S(1)}, u32[]{:S(2)}, u32[]{:S(2)}) collective-permute-start(f32[2,17,512]{2,1,0:T(8,128)S(1)} %pair_up.1), channel_id=1, source_target_pairs={{0,64},{32,96},{1,65},{33,97},{2,66},{34,98},{3,67},{35,99},{4,68}... | collective-permute-start | bytes 208904 | tf_op jit(solution)/shard_map/ppermute | solution.py:527
  25.8 9.2 %collective-permute-start.3 = (f32[2,17,512]{2,1,0:T(8,128)S(1)}, f32[2,17,512]{2,1,0:T(8,128)S(1)}, u32[]{:S(2)}, u32[]{:S(2)}) collective-permute-start(f32[2,17,512]{2,1,0:T(8,128)S(1)} %pair_up.1), channel_id=1, source_target_pairs={{0,32},{32,64},{64,96},{1,33},{33,65},{65,97},{2,34},{34,66},{66,9... | collective-permute-start | bytes 208904 | tf_op jit(solution)/shard_map/ppermute | solution.py:527
  49.0 9.8 %collective-permute-start.4 = (bf16[4,128,256]{2,1,0:T(8,128)(2,1)S(1)}, bf16[4,128,256]{2,1,0:T(8,128)(2,1)S(1)}, u32[]{:S(2)}, u32[]{:S(2)}) collective-permute-start(bf16[4,128,256]{2,1,0:T(8,128)(2,1)S(1)} %get-tuple-element.65), channel_id=1, source_target_pairs={{0,1},{1,2},{2,3},{3,0},{4,5},{5,6},{6,7},{7,4},{8,9},{9,10},{10,1... | collective-permute-start | bytes 786440 | tf_op jit(solution)/shard_map/ppermute | solution.py:538
  50.6 15.0 %collective-permute-start.5 = (bf16[4,128,256]{2,1,0:T(8,128)(2,1)S(1)}, bf16[4,128,256]{2,1,0:T(8,128)(2,1)S(1)}, u32[]{:S(2)}, u32[]{:S(2)}) collective-permute-start(bf16[4,128,256]{2,1,0:T(8,128)(2,1)S(1)} %get-tuple-element.66), channel_id=1, source_target_pairs={{0,2},{1,3},{2,0},{3,1},{4,6},{5,7},{6,4},{7,5},{8,10},{9,11},{10,... | collective-permute-start | bytes 786440 | tf_op jit(solution)/shard_map/ppermute | solution.py:538
  53.5 12.0 %collective-permute-start.6 = (bf16[4,128,256]{2,1,0:T(8,128)(2,1)S(1)}, bf16[4,128,256]{2,1,0:T(8,128)(2,1)S(1)}, u32[]{:S(2)}, u32[]{:S(2)}) collective-permute-start(bf16[4,128,256]{2,1,0:T(8,128)(2,1)S(1)} %get-tuple-element.67), channel_id=1, source_target_pairs={{0,8},{4,12},{8,0},{12,4},{1,9},{5,13},{9,1},{13,5},{2,10},{6,14},... | collective-permute-start | bytes 786440 | tf_op jit(solution)/shard_map/ppermute | solution.py:538
  56.4 12.1 %collective-permute-start.7 = (bf16[4,128,256]{2,1,0:T(8,128)(2,1)S(1)}, bf16[4,128,256]{2,1,0:T(8,128)(2,1)S(1)}, u32[]{:S(2)}, u32[]{:S(2)}) collective-permute-start(bf16[4,128,256]{2,1,0:T(8,128)(2,1)S(1)} %get-tuple-element.68), channel_id=1, source_target_pairs={{0,4},{4,8},{8,12},{12,0},{1,5},{5,9},{9,13},{13,1},{2,6},{6,10},{... | collective-permute-start | bytes 786440 | tf_op jit(solution)/shard_map/ppermute | solution.py:538
  57.0 11.5 %collective-permute-start.8 = (bf16[4,128,256]{2,1,0:T(8,128)(2,1)S(1)}, bf16[4,128,256]{2,1,0:T(8,128)(2,1)S(1)}, u32[]{:S(2)}, u32[]{:S(2)}) collective-permute-start(bf16[4,128,256]{2,1,0:T(8,128)(2,1)S(1)} %get-tuple-element.69), channel_id=1, source_target_pairs={{0,3},{1,0},{2,1},{3,2},{4,7},{5,4},{6,5},{7,6},{8,11},{9,8},{10,9... | collective-permute-start | bytes 786440 | tf_op jit(solution)/shard_map/ppermute | solution.py:538
  58.7 9.8 %collective-permute-start.9 = (bf16[4,128,256]{2,1,0:T(8,128)(2,1)S(1)}, bf16[4,128,256]{2,1,0:T(8,128)(2,1)S(1)}, u32[]{:S(2)}, u32[]{:S(2)}) collective-permute-start(bf16[4,128,256]{2,1,0:T(8,128)(2,1)S(1)} %get-tuple-element.70), channel_id=1, source_target_pairs={{0,12},{4,0},{8,4},{12,8},{1,13},{5,1},{9,5},{13,9},{2,14},{6,2},{... | collective-permute-start | bytes 786440 | tf_op jit(solution)/shard_map/ppermute | solution.py:538
  69.3 7.0 %collective-permute-start.10 = (bf16[128,256]{1,0:T(8,128)(2,1)S(1)}, bf16[128,256]{1,0:T(8,128)(2,1)S(1)}, u32[]{:S(2)}, u32[]{:S(2)}) collective-permute-start(bf16[128,256]{1,0:T(8,128)(2,1)S(1)} %get-tuple-element.73), channel_id=1, source_target_pairs={{0,4},{4,8},{8,12},{12,0},{1,5},{5,9},{9,13},{13,1},{2,6},{6,10},{... | collective-permute-start | bytes 196616 | tf_op jit(solution)/shard_map/ppermute | solution.py:538
  70.9 7.3 %collective-permute-start.11 = (bf16[128,256]{1,0:T(8,128)(2,1)S(1)}, bf16[128,256]{1,0:T(8,128)(2,1)S(1)}, u32[]{:S(2)}, u32[]{:S(2)}) collective-permute-start(bf16[128,256]{1,0:T(8,128)(2,1)S(1)} %get-tuple-element.74), channel_id=1, source_target_pairs={{0,8},{4,12},{8,0},{12,4},{1,9},{5,13},{9,1},{13,5},{2,10},{6,14},... | collective-permute-start | bytes 196616 | tf_op jit(solution)/shard_map/ppermute | solution.py:538
  73.7 5.8 %collective-permute-start.12 = (bf16[128,256]{1,0:T(8,128)(2,1)S(1)}, bf16[128,256]{1,0:T(8,128)(2,1)S(1)}, u32[]{:S(2)}, u32[]{:S(2)}) collective-permute-start(bf16[128,256]{1,0:T(8,128)(2,1)S(1)} %get-tuple-element.75), channel_id=1, source_target_pairs={{0,2},{1,3},{2,0},{3,1},{4,6},{5,7},{6,4},{7,5},{8,10},{9,11},{10,... | collective-permute-start | bytes 196616 | tf_op jit(solution)/shard_map/ppermute | solution.py:538
  74.8 5.5 %collective-permute-start.13 = (bf16[128,256]{1,0:T(8,128)(2,1)S(1)}, bf16[128,256]{1,0:T(8,128)(2,1)S(1)}, u32[]{:S(2)}, u32[]{:S(2)}) collective-permute-start(bf16[128,256]{1,0:T(8,128)(2,1)S(1)} %get-tuple-element.76), channel_id=1, source_target_pairs={{0,1},{1,2},{2,3},{3,0},{4,5},{5,6},{6,7},{7,4},{8,9},{9,10},{10,1... | collective-permute-start | bytes 196616 | tf_op jit(solution)/shard_map/ppermute | solution.py:538
  76.3 4.3 %collective-permute-start.15 = (bf16[128,256]{1,0:T(8,128)(2,1)S(1)}, bf16[128,256]{1,0:T(8,128)(2,1)S(1)}, u32[]{:S(2)}, u32[]{:S(2)}) collective-permute-start(bf16[128,256]{1,0:T(8,128)(2,1)S(1)} %get-tuple-element.78), channel_id=1, source_target_pairs={{0,3},{1,0},{2,1},{3,2},{4,7},{5,4},{6,5},{7,6},{8,11},{9,8},{10,9... | collective-permute-start | bytes 196616 | tf_op jit(solution)/shard_map/ppermute | solution.py:538
  96.9 11.4 %collective-permute-start.16 = (bf16[64,4096]{1,0:T(8,128)(2,1)S(1)}, bf16[64,4096]{1,0:T(8,128)(2,1)S(1)}, u32[]{:S(2)}, u32[]{:S(2)}) collective-permute-start(bf16[64,4096]{1,0:T(8,128)(2,1)S(1)} %normalize.1.after_ref.refs_0_), channel_id=1, source_target_pairs={{0,16},{16,0},{1,17},{17,1},{2,18},{18,2},{3,19},{19,3},{4,20},{20... | collective-permute-start | bytes 1572872 | tf_op jit(solution)/shard_map/ppermute | solution.py:512
  97.0 16.4 %collective-permute-start.17 = (bf16[64,4096]{1,0:T(8,128)(2,1)S(1)}, bf16[64,4096]{1,0:T(8,128)(2,1)S(1)}, u32[]{:S(2)}, u32[]{:S(2)}) collective-permute-start(bf16[64,4096]{1,0:T(8,128)(2,1)S(1)} %normalize.1.after_ref.refs_0_), channel_id=1, source_target_pairs={{0,32},{32,64},{64,96},{96,0},{1,33},{33,65},{65,97},{97,1},{2,34}... | collective-permute-start | bytes 1572872 | tf_op jit(solution)/shard_map/ppermute | solution.py:515
  99.5 14.0 %collective-permute-start.18 = (bf16[64,4096]{1,0:T(8,128)(2,1)S(1)}, bf16[64,4096]{1,0:T(8,128)(2,1)S(1)}, u32[]{:S(2)}, u32[]{:S(2)}) collective-permute-start(bf16[64,4096]{1,0:T(8,128)(2,1)S(1)} %normalize.1.after_ref.refs_0_), channel_id=1, source_target_pairs={{0,96},{32,0},{64,32},{96,64},{1,97},{33,1},{65,33},{97,65},{2,98}... | collective-permute-start | bytes 1572872 | tf_op jit(solution)/shard_map/ppermute | solution.py:515
  114.1 10.5 %collective-permute-start.22 = (bf16[32,4096]{1,0:T(8,128)(2,1)S(1)}, bf16[32,4096]{1,0:T(8,128)(2,1)S(1)}, u32[]{:S(2)}, u32[]{:S(2)}) collective-permute-start(bf16[32,4096]{1,0:T(8,128)(2,1)S(1)} %slice.6), channel_id=1, source_target_pairs={{0,32},{32,64},{64,96},{96,0},{1,33},{33,65},{65,97},{97,1},{2,34}... | collective-permute-start | bytes 786440 | tf_op jit(solution)/shard_map/ppermute | solution.py:515
  115.6 9.0 %collective-permute-start.23 = (bf16[32,4096]{1,0:T(8,128)(2,1)S(1)}, bf16[32,4096]{1,0:T(8,128)(2,1)S(1)}, u32[]{:S(2)}, u32[]{:S(2)}) collective-permute-start(bf16[32,4096]{1,0:T(8,128)(2,1)S(1)} %slice.7), channel_id=1, source_target_pairs={{0,96},{32,0},{64,32},{96,64},{1,97},{33,1},{65,33},{97,65},{2,98}... | collective-permute-start | bytes 786440 | tf_op jit(solution)/shard_map/ppermute | solution.py:515
  132.5 25.4 %collective-permute-start.26 = (bf16[16,64,256]{2,1,0:T(8,128)(2,1)S(1)}, bf16[16,64,256]{2,1,0:T(8,128)(2,1)S(1)}, u32[]{:S(2)}, u32[]{:S(2)}) collective-permute-start(bf16[16,64,256]{2,1,0:T(8,128)(2,1)S(1)} %add_up.5), channel_id=1, source_target_pairs={{0,96},{32,0},{64,32},{96,64},{1,97},{33,1},{65,33},{97,65},{2,98}... | collective-permute-start | bytes 1572872 | tf_op jit(solution)/shard_map/ppermute | solution.py:515
  134.9 26.4 %collective-permute-start.27 = (bf16[16,64,256]{2,1,0:T(8,128)(2,1)S(1)}, bf16[16,64,256]{2,1,0:T(8,128)(2,1)S(1)}, u32[]{:S(2)}, u32[]{:S(2)}) collective-permute-start(bf16[16,64,256]{2,1,0:T(8,128)(2,1)S(1)} %add_up.6), channel_id=1, source_target_pairs={{0,32},{32,64},{64,96},{96,0},{1,33},{33,65},{65,97},{97,1},{2,34}... | collective-permute-start | bytes 1572872 | tf_op jit(solution)/shard_map/ppermute | solution.py:515
  135.0 26.5 %collective-permute-start.31 = (bf16[16,64,256]{2,1,0:T(8,128)(2,1)S(1)}, bf16[16,64,256]{2,1,0:T(8,128)(2,1)S(1)}, u32[]{:S(2)}, u32[]{:S(2)}) collective-permute-start(bf16[16,64,256]{2,1,0:T(8,128)(2,1)S(1)} %add_up.8), channel_id=1, source_target_pairs={{0,64},{32,96},{64,0},{96,32},{1,65},{33,97},{65,1},{97,33},{2,66}... | collective-permute-start | bytes 1572872 | tf_op jit(solution)/shard_map/ppermute | solution.py:515
  162.4 14.7 %all-to-all-start.1 = ((bf16[16,64,256]{2,1,0:T(8,128)(2,1)}), bf16[16,64,256]{2,1,0:T(8,128)(2,1)S(1)}, u32[]{:S(2)}, u32[]{:S(2)}) async-start(bf16[16,64,256]{2,1,0:T(8,128)(2,1)} %add_up.9), calls=%async_computation.1 | async-start | bytes 1048576 | tf_op jit(solution)/shard_map/all_to_all | solution.py:584
  (16 other events, 173.9 us)
Sparse Core Ops, SparseCore 0:
  9.1 35.6 all-gather.2

commit v7 on v6

--- a/solution.py
+++ b/solution.py
@@ -12,7 +12,6 @@
 LOG2E = 1.4426950408889634
 SUBS = 8
 LANES = 128
-CUT = 1
 UNROLL = 16
 MIB = 1 << 20
 f32, bf16 = jnp.float32, jnp.bfloat16
@@ -574,11 +573,11 @@
     low_sum, high_sum = run_add(mine1, swap(other1)), run_add(mine3, swap(other3))
     low_sum, high_sum, turn = lax.optimization_barrier((low_sum, high_sum, turn))
     back1, back3 = ring(low_sum, -1), ring(high_sum, 1)
-    mine2, *other2, turn = run_ffn(
-        [([far_low, far_high], [far_low_sib, far_high_sib])], weights, turn, share, cut=CUT
-    )
-    back2 = ring(run_add(mine2, [swap(p) for p in other2]), 2)
-    near = run_add(mine0, from0, back1, back3, dtype=f32, bytes_accessed=64 * MIB)
+    mine2, other2, turn = run_ffn([([far_low, far_high], [far_low_sib, far_high_sib])], weights, turn, share)
+    far_swap = swap(other2)
+    back1, back3, far_swap = lax.optimization_barrier((back1, back3, far_swap))
+    near = run_add(mine0, from0, back1, back3, dtype=f32)
+    back2 = ring(run_add(mine2, far_swap), 2)
     returned = run_add(near, back2)
 
     back = lax.all_to_all(returned, exp, 0, 0, tiled=True)

time: 186 us -> 183 us (0.984)
  starting transfers between devices: 47.1 us -> 45.1 us
    ppermute x7, starting transfers between devices: 11.8 us -> 9.88 us  [ring(): lax.ppermute(value, 'y', [(i, (i + d) % chips) for i in range(chips)])]
  transfers between devices with their start and end apart: 34 -> 34, of which waited for: 19 -> 18; matrix products, arithmetic and copies ran while one was open for 4% -> 4% of each run, Pallas kernels for 18% -> 20%
where the time goes in v7:
time: 183 us; the launch traced here: 182 us
  waiting for transfers between devices  54 us (30%)
  starting transfers between devices  45.1 us (25%)
  Pallas kernels  44.3 us (24%)
  blocking collectives  15.6 us (9%)
  between operations  13.7 us (7%)
  local copies, waits for them, and re-layouts  9.47 us (5%)
    ppermute x7, waiting for transfers between devices, ring(): lax.ppermute(value, 'y', [(i, (i + d) % chips) for i in range(chips)])  26.1 us
    ppermute x12, starting transfers between devices, shift(): lax.ppermute(value, axis, [(i, (i + d) % n) for i in range(n)])  20.8 us
    all_to_all x1, blocking collectives, on_device(): whole = lax.all_to_all(slot_rows, exp, 0, 0, tiled=True)  15.6 us
    pallas_call x3, Pallas kernels, run_ffn(): pl.pallas_call(functools.partial(feed_forward, groups=tuple(((len(own), l...  15.2 us
    ppermute x12, waiting for transfers between devices, shift(): lax.ppermute(value, axis, [(i, (i + d) % n) for i in range(n)])  9.95 us
    all_to_all x1, waiting for transfers between devices, on_device(): back = lax.all_to_all(returned, exp, 0, 0, tiled=True)  9.89 us
    ppermute x7, starting transfers between devices, ring(): lax.ppermute(value, 'y', [(i, (i + d) % chips) for i in range(chips)])  9.88 us
    ppermute x3, starting transfers between devices, on_device(): lax.ppermute(pair, 'y', [(i, i + d) for i in range(chips - d)])  9.07 us
  transfers between devices with their start and end apart: 34, of which 18 were waited for; matrix products, arithmetic and copies ran while one was open for 4% of the time, Pallas kernels for 20%

profile of v7, /device:TPU:0, one launch (start us, length us, event | category | flops | bytes accessed | tf_op | source)
XLA Modules:
  0.0 182.2 jit_solution(1605937444074129283)
XLA Ops:
  11.4 6.1 %scan_first.1 = (f32[2,17,512]{2,1,0:T(8,128)S(1)}, f32[2,16,8,512]{3,2,1,0:T(8,128)S(1)}, f32[2,8,512]{2,1,0:T(8,128)S(1)}) custom-call(f32[256,512]{1,0:T(8,128)S(1)} %reshape.33.step_ref, bf16[256,512]{1,0:T(8,128)(2,1)S(1)} %reshape.34.sig_ref, f32[16,8,32]{2,1,0:T(8,128)S(1)} %bitcast.22, f32[16,512]{1,0:T(8,128)S(1)} %copy-done), custom_call_target="tpu_custom_call" | custom-call | tf_op jit(solution)/shard_map/scan_first/pallas_call | solution.py:321
  19.5 5.0 %collective-permute-start.1 = (f32[2,17,512]{2,1,0:T(8,128)S(1)}, f32[2,17,512]{2,1,0:T(8,128)S(1)}, u32[]{:S(2)}, u32[]{:S(2)}) collective-permute-start(f32[2,17,512]{2,1,0:T(8,128)S(1)} %pair_up.1), channel_id=1, source_target_pairs={{0,96},{1,97},{2,98},{3,99},{4,100},{5,101},{6,102},{7,103},{8,104... | collective-permute-start | bytes 208904 | tf_op jit(solution)/shard_map/ppermute | solution.py:526
  25.8 2.8 %collective-permute-start.3 = (f32[2,17,512]{2,1,0:T(8,128)S(1)}, f32[2,17,512]{2,1,0:T(8,128)S(1)}, u32[]{:S(2)}, u32[]{:S(2)}) collective-permute-start(f32[2,17,512]{2,1,0:T(8,128)S(1)} %pair_up.1), channel_id=1, source_target_pairs={{0,32},{32,64},{64,96},{1,33},{33,65},{65,97},{2,34},{34,66},{66,9... | collective-permute-start | bytes 208904 | tf_op jit(solution)/shard_map/ppermute | solution.py:526
  31.6 3.4 %collective-permute-done.3.rest_3_ = f32[2,17,512]{2,1,0:T(8,128)S(1)} collective-permute-done((f32[2,17,512]{2,1,0:T(8,128)S(1)}, f32[2,17,512]{2,1,0:T(8,128)S(1)}, u32[]{:S(2)}, u32[]{:S(2)}) %collective-permute-start.3) | collective-permute-done | bytes 69664 | tf_op jit(solution)/shard_map/ppermute | solution.py:526
  36.4 7.2 %scan_second.1.mixed_ref = bf16[256,512]{1,0:T(8,128)(2,1)S(1)} custom-call(s32[3]{0:T(128)S(1)} %pad_add_fusion.core_ref.coords_ref, f32[256,512]{1,0:T(8,128)S(1)} %reshape.33.step_ref, bf16[256,512]{1,0:T(8,128)(2,1)S(1)} %reshape.34.sig_ref, bf16[256,512]{1,0:T(8,128)(2,1)S(1)} %reshape.36.gate_ref, f32[16,8,32]{2,1,0:T(8,128)S(1)} %bitcast.23, ...), custom_call_target="tpu_custom_call" | custom-call | flops 2000000000 | bytes 2097152 | tf_op jit(solution)/shard_map/scan_second/pallas_call | solution.py:356
  44.8 4.2 %project.1 = (bf16[4,128,256]{2,1,0:T(8,128)(2,1)S(1)}, bf16[4,128,256]{2,1,0:T(8,128)(2,1)S(1)}, bf16[4,128,256]{2,1,0:T(8,128)(2,1)S(1)}, bf16[4,128,256]{2,1,...) custom-call(s32[3]{0:T(128)S(1)} %pad_add_fusion.core_ref.coords_ref, ...), custom_call_target="tpu_custom_call" | custom-call | tf_op jit(solution)/shard_map/project/pallas_call | solution.py:379
  50.6 2.9 %collective-permute-start.5 = (bf16[4,128,256]{2,1,0:T(8,128)(2,1)S(1)}, bf16[4,128,256]{2,1,0:T(8,128)(2,1)S(1)}, u32[]{:S(2)}, u32[]{:S(2)}) collective-permute-start(bf16[4,128,256]{2,1,0:T(8,128)(2,1)S(1)} %get-tuple-element.69), channel_id=1, source_target_pairs={{0,2},{1,3},{2,0},{3,1},{4,6},{5,7},{6,4},{7,5},{8,10},{9,11},{10,... | collective-permute-start | bytes 786440 | tf_op jit(solution)/shard_map/ppermute | solution.py:537
  53.5 2.9 %collective-permute-start.6 = (bf16[4,128,256]{2,1,0:T(8,128)(2,1)S(1)}, bf16[4,128,256]{2,1,0:T(8,128)(2,1)S(1)}, u32[]{:S(2)}, u32[]{:S(2)}) collective-permute-start(bf16[4,128,256]{2,1,0:T(8,128)(2,1)S(1)} %get-tuple-element.70), channel_id=1, source_target_pairs={{0,8},{4,12},{8,0},{12,4},{1,9},{5,13},{9,1},{13,5},{2,10},{6,14},... | collective-permute-start | bytes 786440 | tf_op jit(solution)/shard_map/ppermute | solution.py:537
  58.7 2.6 %collective-permute-start.9 = (bf16[4,128,256]{2,1,0:T(8,128)(2,1)S(1)}, bf16[4,128,256]{2,1,0:T(8,128)(2,1)S(1)}, u32[]{:S(2)}, u32[]{:S(2)}) collective-permute-start(bf16[4,128,256]{2,1,0:T(8,128)(2,1)S(1)} %get-tuple-element.73), channel_id=1, source_target_pairs={{0,12},{4,0},{8,4},{12,8},{1,13},{5,1},{9,5},{13,9},{2,14},{6,2},{... | collective-permute-start | bytes 786440 | tf_op jit(solution)/shard_map/ppermute | solution.py:537
  61.4 4.2 %collective-permute-done.5.rest_1_ = bf16[4,128,256]{2,1,0:T(8,128)(2,1)S(1)} collective-permute-done((bf16[4,128,256]{2,1,0:T(8,128)(2,1)S(1)}, bf16[4,128,256]{2,1,0:T(8,128)(2,1)S(1)}, u32[]{:S(2)}, u32[]{:S(2)}) %collective-permute-start.5) | collective-permute-done | bytes 262176 | tf_op jit(solution)/shard_map/ppermute | solution.py:537
  65.5 3.0 %collective-permute-done.7.rest_3_ = bf16[4,128,256]{2,1,0:T(8,128)(2,1)S(1)} collective-permute-done((bf16[4,128,256]{2,1,0:T(8,128)(2,1)S(1)}, bf16[4,128,256]{2,1,0:T(8,128)(2,1)S(1)}, u32[]{:S(2)}, u32[]{:S(2)}) %collective-permute-start.7) | collective-permute-done | bytes 262176 | tf_op jit(solution)/shard_map/ppermute | solution.py:537
  70.9 2.9 %collective-permute-start.11 = (bf16[128,256]{1,0:T(8,128)(2,1)S(1)}, bf16[128,256]{1,0:T(8,128)(2,1)S(1)}, u32[]{:S(2)}, u32[]{:S(2)}) collective-permute-start(bf16[128,256]{1,0:T(8,128)(2,1)S(1)} %get-tuple-element.77), channel_id=1, source_target_pairs={{0,8},{4,12},{8,0},{12,4},{1,9},{5,13},{9,1},{13,5},{2,10},{6,14},... | collective-permute-start | bytes 196616 | tf_op jit(solution)/shard_map/ppermute | solution.py:537
  81.0 15.6 %all_to_all.10.recv_ref = bf16[16,64,256]{2,1,0:T(8,128)(2,1)S(1)} all-to-all(bf16[16,64,256]{2,1,0:T(8,128)(2,1)S(1)} %get-tuple-element.85), channel_id=1, replica_groups=mesh['y'=4,'core'=2,'x'=4,'z'=4] {'x','z'}, dimensions={0} | all-to-all | bytes 1048576 | tf_op jit(solution)/shard_map/all_to_all | solution.py:555
  97.0 2.5 %collective-permute-start.17 = (bf16[64,4096]{1,0:T(8,128)(2,1)S(1)}, bf16[64,4096]{1,0:T(8,128)(2,1)S(1)}, u32[]{:S(2)}, u32[]{:S(2)}) collective-permute-start(bf16[64,4096]{1,0:T(8,128)(2,1)S(1)} %normalize.1.after_ref.refs_0_), channel_id=1, source_target_pairs={{0,32},{32,64},{64,96},{96,0},{1,33},{33,65},{65,97},{97,1},{2,34}... | collective-permute-start | bytes 1572872 | tf_op jit(solution)/shard_map/ppermute | solution.py:514
  101.0 7.3 %load_weights.1 = (bf16[4096,896]{1,0:T(8,128)(2,1)S(1)}, bf16[4096,896]{1,0:T(8,128)(2,1)S(1)}, bf16[896,4096]{1,0:T(8,128)(2,1)S(1)}, f32[8,128]{1,0:T(8,128)S(1)}) custom-call(bf16[64,4096]{1,0:T(8,128)(2,1)S(1)} %normalize.1.after_ref.refs_0_, bf16[4096,896]{1,0:T(8,128)(2,1)} %bitcast.27, bf16[4096,896]{1,0:T(8,128)(2,1)} %bitcast.28, ...), custom_call_target="tpu_custom_call" | custom-call | bytes 44040192 | tf_op jit(solution)/shard_map/load_weights/pallas_call | solution.py:438
  108.3 3.8 %feed_forward.3 = (bf16[16,64,256]{2,1,0:T(8,128)(2,1)S(1)}, bf16[16,64,256]{2,1,0:T(8,128)(2,1)S(1)}, f32[8,128]{1,0:T(8,128)S(1)}) custom-call(bf16[64,4096]{1,0:T(8,128)(2,1)S(1)} %normalize.1.after_ref.refs_0_, bf16[64,4096]{1,0:T(8,128)(2,1)S(1)} %collective-permute-done.16.refs_1_, bf16[4096,896]{1,0:T(8,128)(2,1)S(1)} %get-tuple-element.88.refs_2_.refs_4_, ...), custom_call_target="tpu_custom_call" | custom-call | flops 2818572288 | bytes 2097152 | tf_op jit(solution)/shard_map/feed_forward/pallas_call | solution.py:458
  117.4 7.2 %feed_forward.4 = (bf16[16,64,256]{2,1,0:T(8,128)(2,1)S(1)}, bf16[16,64,256]{2,1,0:T(8,128)(2,1)S(1)}, bf16[16,64,256]{2,1,0:T(8,128)(2,1)S(1)}, bf16[16,64,256]{2,1,0:T(8,128)(2,1)S(1)}, f32[8,128]{1,0:T(8,128)S(1)}) custom-call(bf16[64,4096]{1,0:T(8,128)(2,1)S(1)} %collective-permute-done.17.refs_0_, bf16[64,4096]{1,0:T(8,128)(2,1)S(1)} %collective-permute-done.19.refs_1_, ...), custom_call_target="tpu_custom_call" | custom-call | flops 5637144576 | bytes 4194304 | tf_op jit(solution)/shard_map/feed_forward/pallas_call | solution.py:458
  127.4 2.5 %collective-permute-start.26 = (bf16[16,64,256]{2,1,0:T(8,128)(2,1)S(1)}, bf16[16,64,256]{2,1,0:T(8,128)(2,1)S(1)}, u32[]{:S(2)}, u32[]{:S(2)}) collective-permute-start(bf16[16,64,256]{2,1,0:T(8,128)(2,1)S(1)} %add_up.5), channel_id=1, source_target_pairs={{0,96},{32,0},{64,32},{96,64},{1,97},{33,1},{65,33},{97,65},{2,98}... | collective-permute-start | bytes 1572872 | tf_op jit(solution)/shard_map/ppermute | solution.py:514
  129.9 4.2 %feed_forward.5 = (bf16[16,64,256]{2,1,0:T(8,128)(2,1)S(1)}, bf16[16,64,256]{2,1,0:T(8,128)(2,1)S(1)}, f32[8,128]{1,0:T(8,128)}) custom-call(bf16[32,4096]{1,0:T(8,128)(2,1)S(1)} %collective-permute-done.22.refs_0_, bf16[32,4096]{1,0:T(8,128)(2,1)S(1)} %collective-permute-done.23.refs_1_, bf16[32,4096]{1,0:T(8,128)(2,1)S(1)} %collective-permute-done.28.refs_2_, ...), custom_call_target="tpu_custom_call" | custom-call | flops 2818572288 | bytes 2097152 | tf_op jit(solution)/shard_map/feed_forward/pallas_call | solution.py:458
  134.2 7.3 %collective-permute-done.26.refs_2_ = bf16[16,64,256]{2,1,0:T(8,128)(2,1)S(1)} collective-permute-done((bf16[16,64,256]{2,1,0:T(8,128)(2,1)S(1)}, bf16[16,64,256]{2,1,0:T(8,128)(2,1)S(1)}, u32[]{:S(2)}, u32[]{:S(2)}) %collective-permute-start.26) | collective-permute-done | bytes 524320 | tf_op jit(solution)/shard_map/ppermute | solution.py:514
  141.5 3.3 %collective-permute-done.27.refs_3_ = bf16[16,64,256]{2,1,0:T(8,128)(2,1)S(1)} collective-permute-done((bf16[16,64,256]{2,1,0:T(8,128)(2,1)S(1)}, bf16[16,64,256]{2,1,0:T(8,128)(2,1)S(1)}, u32[]{:S(2)}, u32[]{:S(2)}) %collective-permute-start.27) | collective-permute-done | bytes 524320 | tf_op jit(solution)/shard_map/ppermute | solution.py:514
  145.3 14.1 %collective-permute-done.31.refs_1_ = bf16[16,64,256]{2,1,0:T(8,128)(2,1)S(1)} collective-permute-done((bf16[16,64,256]{2,1,0:T(8,128)(2,1)S(1)}, bf16[16,64,256]{2,1,0:T(8,128)(2,1)S(1)}, u32[]{:S(2)}, u32[]{:S(2)}) %collective-permute-start.31) | collective-permute-done | bytes 524320 | tf_op jit(solution)/shard_map/ppermute | solution.py:514
  160.2 3.6 %all-to-all-start.1 = ((bf16[16,64,256]{2,1,0:T(8,128)(2,1)}), bf16[16,64,256]{2,1,0:T(8,128)(2,1)S(1)}, u32[]{:S(2)}, u32[]{:S(2)}) async-start(bf16[16,64,256]{2,1,0:T(8,128)(2,1)} %add_up.9), calls=%async_computation.1 | async-start | bytes 1048576 | tf_op jit(solution)/shard_map/all_to_all | solution.py:583
  164.0 9.9 %all-to-all-done.1.recv_ref = bf16[16,64,256]{2,1,0:T(8,128)(2,1)S(1)} async-done(((bf16[16,64,256]{2,1,0:T(8,128)(2,1)}), bf16[16,64,256]{2,1,0:T(8,128)(2,1)S(1)}, u32[]{:S(2)}, u32[]{:S(2)}) %all-to-all-start.1) | async-done | bytes 524320 | tf_op jit(solution)/shard_map/all_to_all | solution.py:583
  (90 shorter events, 40.1 us)
Async XLA Ops:
  6.5 38.2 %all-gather.3.cloned.1.call-start = ((), (), s32[]{:S(2)}) async-start(), calls=%async_computation.2 | async-start | bytes 4718592 | tf_op jit(solution)/shard_map/all_gather | solution.py:516
  19.5 12.0 %collective-permute-start.1 = (f32[2,17,512]{2,1,0:T(8,128)S(1)}, f32[2,17,512]{2,1,0:T(8,128)S(1)}, u32[]{:S(2)}, u32[]{:S(2)}) collective-permute-start(f32[2,17,512]{2,1,0:T(8,128)S(1)} %pair_up.1), channel_id=1, source_target_pairs={{0,96},{1,97},{2,98},{3,99},{4,100},{5,101},{6,102},{7,103},{8,104... | collective-permute-start | bytes 208904 | tf_op jit(solution)/shard_map/ppermute | solution.py:526
  24.5 7.0 %collective-permute-start.2 = (f32[2,17,512]{2,1,0:T(8,128)S(1)}, f32[2,17,512]{2,1,0:T(8,128)S(1)}, u32[]{:S(2)}, u32[]{:S(2)}) collective-permute-start(f32[2,17,512]{2,1,0:T(8,128)S(1)} %pair_up.1), channel_id=1, source_target_pairs={{0,64},{32,96},{1,65},{33,97},{2,66},{34,98},{3,67},{35,99},{4,68}... | collective-permute-start | bytes 208904 | tf_op jit(solution)/shard_map/ppermute | solution.py:526
  25.8 9.2 %collective-permute-start.3 = (f32[2,17,512]{2,1,0:T(8,128)S(1)}, f32[2,17,512]{2,1,0:T(8,128)S(1)}, u32[]{:S(2)}, u32[]{:S(2)}) collective-permute-start(f32[2,17,512]{2,1,0:T(8,128)S(1)} %pair_up.1), channel_id=1, source_target_pairs={{0,32},{32,64},{64,96},{1,33},{33,65},{65,97},{2,34},{34,66},{66,9... | collective-permute-start | bytes 208904 | tf_op jit(solution)/shard_map/ppermute | solution.py:526
  49.0 9.8 %collective-permute-start.4 = (bf16[4,128,256]{2,1,0:T(8,128)(2,1)S(1)}, bf16[4,128,256]{2,1,0:T(8,128)(2,1)S(1)}, u32[]{:S(2)}, u32[]{:S(2)}) collective-permute-start(bf16[4,128,256]{2,1,0:T(8,128)(2,1)S(1)} %get-tuple-element.68), channel_id=1, source_target_pairs={{0,1},{1,2},{2,3},{3,0},{4,5},{5,6},{6,7},{7,4},{8,9},{9,10},{10,1... | collective-permute-start | bytes 786440 | tf_op jit(solution)/shard_map/ppermute | solution.py:537
  50.6 15.0 %collective-permute-start.5 = (bf16[4,128,256]{2,1,0:T(8,128)(2,1)S(1)}, bf16[4,128,256]{2,1,0:T(8,128)(2,1)S(1)}, u32[]{:S(2)}, u32[]{:S(2)}) collective-permute-start(bf16[4,128,256]{2,1,0:T(8,128)(2,1)S(1)} %get-tuple-element.69), channel_id=1, source_target_pairs={{0,2},{1,3},{2,0},{3,1},{4,6},{5,7},{6,4},{7,5},{8,10},{9,11},{10,... | collective-permute-start | bytes 786440 | tf_op jit(solution)/shard_map/ppermute | solution.py:537
  53.5 12.0 %collective-permute-start.6 = (bf16[4,128,256]{2,1,0:T(8,128)(2,1)S(1)}, bf16[4,128,256]{2,1,0:T(8,128)(2,1)S(1)}, u32[]{:S(2)}, u32[]{:S(2)}) collective-permute-start(bf16[4,128,256]{2,1,0:T(8,128)(2,1)S(1)} %get-tuple-element.70), channel_id=1, source_target_pairs={{0,8},{4,12},{8,0},{12,4},{1,9},{5,13},{9,1},{13,5},{2,10},{6,14},... | collective-permute-start | bytes 786440 | tf_op jit(solution)/shard_map/ppermute | solution.py:537
  56.4 12.1 %collective-permute-start.7 = (bf16[4,128,256]{2,1,0:T(8,128)(2,1)S(1)}, bf16[4,128,256]{2,1,0:T(8,128)(2,1)S(1)}, u32[]{:S(2)}, u32[]{:S(2)}) collective-permute-start(bf16[4,128,256]{2,1,0:T(8,128)(2,1)S(1)} %get-tuple-element.71), channel_id=1, source_target_pairs={{0,4},{4,8},{8,12},{12,0},{1,5},{5,9},{9,13},{13,1},{2,6},{6,10},{... | collective-permute-start | bytes 786440 | tf_op jit(solution)/shard_map/ppermute | solution.py:537
  57.0 11.5 %collective-permute-start.8 = (bf16[4,128,256]{2,1,0:T(8,128)(2,1)S(1)}, bf16[4,128,256]{2,1,0:T(8,128)(2,1)S(1)}, u32[]{:S(2)}, u32[]{:S(2)}) collective-permute-start(bf16[4,128,256]{2,1,0:T(8,128)(2,1)S(1)} %get-tuple-element.72), channel_id=1, source_target_pairs={{0,3},{1,0},{2,1},{3,2},{4,7},{5,4},{6,5},{7,6},{8,11},{9,8},{10,9... | collective-permute-start | bytes 786440 | tf_op jit(solution)/shard_map/ppermute | solution.py:537
  58.7 9.8 %collective-permute-start.9 = (bf16[4,128,256]{2,1,0:T(8,128)(2,1)S(1)}, bf16[4,128,256]{2,1,0:T(8,128)(2,1)S(1)}, u32[]{:S(2)}, u32[]{:S(2)}) collective-permute-start(bf16[4,128,256]{2,1,0:T(8,128)(2,1)S(1)} %get-tuple-element.73), channel_id=1, source_target_pairs={{0,12},{4,0},{8,4},{12,8},{1,13},{5,1},{9,5},{13,9},{2,14},{6,2},{... | collective-permute-start | bytes 786440 | tf_op jit(solution)/shard_map/ppermute | solution.py:537
  69.3 7.0 %collective-permute-start.10 = (bf16[128,256]{1,0:T(8,128)(2,1)S(1)}, bf16[128,256]{1,0:T(8,128)(2,1)S(1)}, u32[]{:S(2)}, u32[]{:S(2)}) collective-permute-start(bf16[128,256]{1,0:T(8,128)(2,1)S(1)} %get-tuple-element.76), channel_id=1, source_target_pairs={{0,4},{4,8},{8,12},{12,0},{1,5},{5,9},{9,13},{13,1},{2,6},{6,10},{... | collective-permute-start | bytes 196616 | tf_op jit(solution)/shard_map/ppermute | solution.py:537
  70.9 7.3 %collective-permute-start.11 = (bf16[128,256]{1,0:T(8,128)(2,1)S(1)}, bf16[128,256]{1,0:T(8,128)(2,1)S(1)}, u32[]{:S(2)}, u32[]{:S(2)}) collective-permute-start(bf16[128,256]{1,0:T(8,128)(2,1)S(1)} %get-tuple-element.77), channel_id=1, source_target_pairs={{0,8},{4,12},{8,0},{12,4},{1,9},{5,13},{9,1},{13,5},{2,10},{6,14},... | collective-permute-start | bytes 196616 | tf_op jit(solution)/shard_map/ppermute | solution.py:537
  73.7 5.8 %collective-permute-start.12 = (bf16[128,256]{1,0:T(8,128)(2,1)S(1)}, bf16[128,256]{1,0:T(8,128)(2,1)S(1)}, u32[]{:S(2)}, u32[]{:S(2)}) collective-permute-start(bf16[128,256]{1,0:T(8,128)(2,1)S(1)} %get-tuple-element.78), channel_id=1, source_target_pairs={{0,2},{1,3},{2,0},{3,1},{4,6},{5,7},{6,4},{7,5},{8,10},{9,11},{10,... | collective-permute-start | bytes 196616 | tf_op jit(solution)/shard_map/ppermute | solution.py:537
  74.8 5.5 %collective-permute-start.13 = (bf16[128,256]{1,0:T(8,128)(2,1)S(1)}, bf16[128,256]{1,0:T(8,128)(2,1)S(1)}, u32[]{:S(2)}, u32[]{:S(2)}) collective-permute-start(bf16[128,256]{1,0:T(8,128)(2,1)S(1)} %get-tuple-element.79), channel_id=1, source_target_pairs={{0,1},{1,2},{2,3},{3,0},{4,5},{5,6},{6,7},{7,4},{8,9},{9,10},{10,1... | collective-permute-start | bytes 196616 | tf_op jit(solution)/shard_map/ppermute | solution.py:537
  96.9 11.4 %collective-permute-start.16 = (bf16[64,4096]{1,0:T(8,128)(2,1)S(1)}, bf16[64,4096]{1,0:T(8,128)(2,1)S(1)}, u32[]{:S(2)}, u32[]{:S(2)}) collective-permute-start(bf16[64,4096]{1,0:T(8,128)(2,1)S(1)} %normalize.1.after_ref.refs_0_), channel_id=1, source_target_pairs={{0,16},{16,0},{1,17},{17,1},{2,18},{18,2},{3,19},{19,3},{4,20},{20... | collective-permute-start | bytes 1572872 | tf_op jit(solution)/shard_map/ppermute | solution.py:511
  97.0 16.4 %collective-permute-start.17 = (bf16[64,4096]{1,0:T(8,128)(2,1)S(1)}, bf16[64,4096]{1,0:T(8,128)(2,1)S(1)}, u32[]{:S(2)}, u32[]{:S(2)}) collective-permute-start(bf16[64,4096]{1,0:T(8,128)(2,1)S(1)} %normalize.1.after_ref.refs_0_), channel_id=1, source_target_pairs={{0,32},{32,64},{64,96},{96,0},{1,33},{33,65},{65,97},{97,1},{2,34}... | collective-permute-start | bytes 1572872 | tf_op jit(solution)/shard_map/ppermute | solution.py:514
  99.5 14.0 %collective-permute-start.18 = (bf16[64,4096]{1,0:T(8,128)(2,1)S(1)}, bf16[64,4096]{1,0:T(8,128)(2,1)S(1)}, u32[]{:S(2)}, u32[]{:S(2)}) collective-permute-start(bf16[64,4096]{1,0:T(8,128)(2,1)S(1)} %normalize.1.after_ref.refs_0_), channel_id=1, source_target_pairs={{0,96},{32,0},{64,32},{96,64},{1,97},{33,1},{65,33},{97,65},{2,98}... | collective-permute-start | bytes 1572872 | tf_op jit(solution)/shard_map/ppermute | solution.py:514
  114.1 10.5 %collective-permute-start.22 = (bf16[32,4096]{1,0:T(8,128)(2,1)S(1)}, bf16[32,4096]{1,0:T(8,128)(2,1)S(1)}, u32[]{:S(2)}, u32[]{:S(2)}) collective-permute-start(bf16[32,4096]{1,0:T(8,128)(2,1)S(1)} %slice.6), channel_id=1, source_target_pairs={{0,32},{32,64},{64,96},{96,0},{1,33},{33,65},{65,97},{97,1},{2,34}... | collective-permute-start | bytes 786440 | tf_op jit(solution)/shard_map/ppermute | solution.py:514
  115.6 9.0 %collective-permute-start.23 = (bf16[32,4096]{1,0:T(8,128)(2,1)S(1)}, bf16[32,4096]{1,0:T(8,128)(2,1)S(1)}, u32[]{:S(2)}, u32[]{:S(2)}) collective-permute-start(bf16[32,4096]{1,0:T(8,128)(2,1)S(1)} %slice.7), channel_id=1, source_target_pairs={{0,96},{32,0},{64,32},{96,64},{1,97},{33,1},{65,33},{97,65},{2,98}... | collective-permute-start | bytes 786440 | tf_op jit(solution)/shard_map/ppermute | solution.py:514
  127.4 14.0 %collective-permute-start.26 = (bf16[16,64,256]{2,1,0:T(8,128)(2,1)S(1)}, bf16[16,64,256]{2,1,0:T(8,128)(2,1)S(1)}, u32[]{:S(2)}, u32[]{:S(2)}) collective-permute-start(bf16[16,64,256]{2,1,0:T(8,128)(2,1)S(1)} %add_up.5), channel_id=1, source_target_pairs={{0,96},{32,0},{64,32},{96,64},{1,97},{33,1},{65,33},{97,65},{2,98}... | collective-permute-start | bytes 1572872 | tf_op jit(solution)/shard_map/ppermute | solution.py:514
  129.9 14.9 %collective-permute-start.27 = (bf16[16,64,256]{2,1,0:T(8,128)(2,1)S(1)}, bf16[16,64,256]{2,1,0:T(8,128)(2,1)S(1)}, u32[]{:S(2)}, u32[]{:S(2)}) collective-permute-start(bf16[16,64,256]{2,1,0:T(8,128)(2,1)S(1)} %add_up.6), channel_id=1, source_target_pairs={{0,32},{32,64},{64,96},{96,0},{1,33},{33,65},{65,97},{97,1},{2,34}... | collective-permute-start | bytes 1572872 | tf_op jit(solution)/shard_map/ppermute | solution.py:514
  134.2 10.6 %collective-permute-start.30 = (bf16[16,64,256]{2,1,0:T(8,128)(2,1)S(1)}, bf16[16,64,256]{2,1,0:T(8,128)(2,1)S(1)}, u32[]{:S(2)}, u32[]{:S(2)}) collective-permute-start(bf16[16,64,256]{2,1,0:T(8,128)(2,1)S(1)} %get-tuple-element.113), channel_id=1, source_target_pairs={{0,16},{16,0},{1,17},{17,1},{2,18},{18,2},{3,19},{19,3},{4,20},{20... | collective-permute-start | bytes 1572872 | tf_op jit(solution)/shard_map/ppermute | solution.py:511
  145.0 14.4 %collective-permute-start.31 = (bf16[16,64,256]{2,1,0:T(8,128)(2,1)S(1)}, bf16[16,64,256]{2,1,0:T(8,128)(2,1)S(1)}, u32[]{:S(2)}, u32[]{:S(2)}) collective-permute-start(bf16[16,64,256]{2,1,0:T(8,128)(2,1)S(1)} %add_up.8), channel_id=1, source_target_pairs={{0,64},{32,96},{64,0},{96,32},{1,65},{33,97},{65,1},{97,33},{2,66}... | collective-permute-start | bytes 1572872 | tf_op jit(solution)/shard_map/ppermute | solution.py:514
  160.2 13.6 %all-to-all-start.1 = ((bf16[16,64,256]{2,1,0:T(8,128)(2,1)}), bf16[16,64,256]{2,1,0:T(8,128)(2,1)S(1)}, u32[]{:S(2)}, u32[]{:S(2)}) async-start(bf16[16,64,256]{2,1,0:T(8,128)(2,1)} %add_up.9), calls=%async_computation.1 | async-start | bytes 1048576 | tf_op jit(solution)/shard_map/all_to_all | solution.py:583
  (16 other events, 175.7 us)
Sparse Core Ops, SparseCore 0:
  9.1 35.6 all-gather.2
